TPU v7x, 768 devices: a whole 4x8x12 slice. The times are simulated.
768 devices in a mesh: row: 16 (over y, core), theta: 12 (over z_hi, x), group: 4 (over z_lo).
Axes of the slice: x: 4, y: 8, z: 12 (z_hi: 3, z_lo: 4; z = z_hi * 4 + z_lo), core: 2. Of those that a mesh axis runs over, the one named last changes fastest.
Arguments:
- dust: bfloat16 [32, 256, 96, 128], P('group', 'row', 'theta'), may hold values from 0.0099487305 to 1
- table: bfloat16 [32, 48], replicated, may hold values from 0.019897461 to 2
- planck: float32 [48], P('group'), may hold values from 0.05 to 0.5
- energy_old: float32 [48, 256, 96, 128], P('group', 'row', 'theta'), may hold values from 0.05 to 1
- temp_old: float32 [256, 96, 128], P('row', 'theta'), may hold values from 0.5 to 1.5
Outputs:
- energy: float32 [48, 256, 96, 128], P('group', 'row', 'theta')
- temperature: float32 [256, 96, 128], P('row', 'theta')
All inputs are finite; a program needn't handle non-finite values.
Results may differ from a plain program's by a relative error of at most 0.00045.
Values may be sent and summed in bfloat16 or wider, within the bound.
No kernel may reach another device: no remote copies, remote signals or barrier semaphores. Data moves between devices by JAX's collectives and lax.ppermute only.
A program may use at most 64 MiB of HBM per device.

v0:
```python
import jax
import jax.numpy as jnp
from jax import lax
from jax.experimental import pallas as pl
from jax.experimental.pallas import tpu as pltpu
from jax.sharding import PartitionSpec as P


HEAT = 2.0
REACH = 20.0
SCALE = 2.0 / REACH


BF = jnp.bfloat16
F32 = jnp.float32
VMEM = pltpu.VMEM
SMEM = pltpu.SMEM

BINS = 8
OWN = 12
GROUPS = 24
ROWS = 8
LAT = 8
LANES = 128
TILES = GROUPS * ROWS
CELLS = TILES * LAT


def call(kernel, outs, args, smem=0, scratch=(), flops=1_000_000, space=VMEM):
    specs = [pl.BlockSpec(memory_space=SMEM)] * smem
    specs += [pl.BlockSpec(memory_space=space)] * (len(args) - smem)
    return pl.pallas_call(
        kernel,
        out_shape=outs,
        in_specs=specs,
        out_specs=[pl.BlockSpec(memory_space=VMEM)] * len(outs),
        scratch_shapes=list(scratch),
        cost_estimate=pl.CostEstimate(flops=flops, bytes_accessed=1_000_000, transcendentals=0),
        compiler_params=pltpu.CompilerParams(vmem_limit_bytes=16 << 20),
    )(*args)


def held(shape, dtype=F32):
    return VMEM(shape, dtype)


def keep(x):
    return pltpu.with_memory_space_constraint(x, VMEM)


def tile(i):
    return pl.ds(pl.multiple_of(i * LAT, LAT), LAT)


UNROLL = 4
SIZE = BINS * ROWS * LAT
PART = OWN * ROWS * LAT
N = ROWS * LAT
COEF = 0.75 / SCALE


def pack_kernel(pos, planck, dust, eold, eown, pair, near, far, stage, shares, sems):
    half = pos[0]
    mine = pl.ds(pl.multiple_of(N * half, N), N)
    other = pl.ds(pl.multiple_of(N * (1 - half), N), N)
    copies = [
        pltpu.make_async_copy(dust.at[:, other, :], far, sems.at[0]),
        pltpu.make_async_copy(eold.at[:, other, :], stage, sems.at[1]),
        pltpu.make_async_copy(dust.at[:, mine, :], near, sems.at[2]),
        pltpu.make_async_copy(eold.at[:, mine, :], eown, sems.at[3]),
        pltpu.make_async_copy(planck, shares, sems.at[4]),
    ]
    for copy in copies:
        copy.start()
    copies[0].wait()
    for b in range(BINS):
        pair[pl.ds(b * N, N), :] = far[b]
    copies[1].wait()
    for g in range(OWN):
        pair[pl.ds(SIZE + g * N, N), :] = stage[g].astype(BF)
    copies[4].wait()
    row = lax.broadcasted_iota(jnp.int32, (2 * LAT, LANES), 0)
    share = jnp.zeros((2 * LAT, LANES), F32)
    for g in range(OWN):
        share = jnp.where(row == g, shares[g], share)
    for i in range(3):
        piece = share.astype(BF)
        pair[pl.ds(SIZE + PART + 2 * i * LAT, 2 * LAT), :] = piece
        share = share - piece.astype(F32)
    copies[2].wait()
    copies[3].wait()


def write_slabs(pos, src, at, t1, t2, r1, r2):
    part, tp = pos[0], pos[1]
    low = src[pl.ds(0, TILES, stride=LAT), :].astype(BF)
    high = src[pl.ds(LAT - 1, TILES, stride=LAT), :].astype(BF)
    rows = pl.ds(at, TILES)

    @pl.when(tp == 0)
    def _():
        t1[rows, :] = high
        t2[rows, :] = low

    @pl.when(tp == 1)
    def _():
        t1[rows, :] = low
        t2[rows, :] = high

    for g in range(0, GROUPS, 2):
        def edge(r):
            a = src[tile(g * ROWS + r), :]
            b = src[tile((g + 1) * ROWS + r), :]
            return jnp.concatenate([a, b], axis=0).astype(BF)

        r1[pl.ds(at + g * LAT, 2 * LAT), :] = edge((ROWS - 1) * (1 - part))
        r2[pl.ds(at + g * LAT, 2 * LAT), :] = edge((ROWS - 1) * part)


def gather_bins(tab, wide, place, blocks, g, acc):
    first = (place // 2) * GROUPS
    for j, k in enumerate(blocks):
        source = jnp.bitwise_xor(place, k)
        for b in range(BINS):
            t = SCALE * tab[(source * BINS + b) * 2 * GROUPS + first + g]
            for r in range(ROWS):
                term = t * wide[tile((j * BINS + b) * ROWS + r), :]
                acc[r] = term if acc[r] is None else acc[r] + term
    return acc


def early_kernel(pos, tab, mine, near, far, kap, wide):
    place = pos[2]
    for j, block in enumerate((mine, near, far)):
        for b in range(BINS):
            wide[pl.ds(j * SIZE + b * N, N), :] = block[b].astype(F32)

    def one(g, carry):
        acc = gather_bins(tab, wide, place, (0, 2, 3), g, [None] * ROWS)
        for r in range(ROWS):
            kap[tile(g * ROWS + r), :] = acc[r]
        return carry

    lax.fori_loop(0, GROUPS, one, 0, unroll=2)


def late_kernel(pos, tab, planck, part, eown, pair, kap, e, share, t1, t2, r1, r2, wide):
    place = pos[2]
    slot = place % 2
    wide[...] = pair[pl.ds(0, SIZE), :].astype(F32)

    def one(g, carry):
        acc = [part[tile(g * ROWS + r), :] for r in range(ROWS)]
        acc = gather_bins(tab, wide, place, (1,), g, acc)
        for r in range(ROWS):
            kap[tile(g * ROWS + r), :] = acc[r]
        return carry

    lax.fori_loop(0, GROUPS, one, 0, unroll=2)
    theirs = pl.multiple_of((1 - slot) * PART, PART)
    mine = pl.multiple_of(slot * PART, PART)
    for g in range(OWN):
        e[pl.ds(mine + g * N, N), :] = eown[g]
    e[pl.ds(theirs, PART), :] = pair[pl.ds(SIZE, PART), :].astype(F32)
    at = SIZE + PART
    pieces = [pair[pl.ds(at + 2 * LAT * i, 2 * LAT), :].astype(F32) for i in range(3)]
    row = lax.broadcasted_iota(jnp.int32, (2 * LAT, LANES), 0)
    ours = jnp.zeros((2 * LAT, LANES), F32)
    for g in range(OWN):
        ours = jnp.where(row == g, planck[g], ours)
    share[slot] = ours
    share[1 - slot] = pieces[0] + pieces[1] + pieces[2]
    write_slabs(pos, e, 0, t1, t2, r1, r2)
    write_slabs(pos, kap, TILES, t1, t2, r1, r2)


def face(ea, eb, c):
    d = eb - ea
    w = 1.0 / (c + jnp.abs(d) / (ea + eb))
    return w, w * d


def spread(row):
    return jnp.broadcast_to(row, (LAT, LANES))


def share_of(share, g):
    part = g // OWN
    return spread(share[part, pl.ds(g - part * OWN, 1), :])


def inner_body(e, coefs, flux, weight, prepare):
    top = lax.broadcasted_iota(jnp.int32, (LAT, LANES), 0) == LAT - 1

    def one(g, carry):
        base = g * ROWS
        tiles = [e[tile(base + r), :] for r in range(ROWS)]
        coef = prepare(g, base, tiles) if prepare else [[c[tile(base + r), :] for c in coefs] for r in range(ROWS)]
        ws, fs = [], []
        for r in range(ROWS):
            here = tiles[r]
            c_up, c_east, c_above = coef[r]
            w_up, f_up = face(here, pltpu.roll(here, LAT - 1, 0), c_up)
            w_up, f_up = jnp.where(top, 0.0, w_up), jnp.where(top, 0.0, f_up)
            w_east, f_east = face(here, pltpu.roll(here, LANES - 1, 1), c_east)
            w = (w_up + pltpu.roll(w_up, 1, 0)) + (w_east + pltpu.roll(w_east, 1, 1))
            f = (f_up - pltpu.roll(f_up, 1, 0)) + (f_east - pltpu.roll(f_east, 1, 1))
            if r > 0:
                w, f = w + w_below, f - f_below
            if r + 1 < ROWS:
                w_below, f_below = face(here, tiles[r + 1], c_above)
                w, f = w + w_below, f + f_below
            ws.append(w)
            fs.append(f)
        for r in range(ROWS):
            weight[tile(base + r), :] = ws[r]
            flux[tile(base + r), :] = fs[r]
        return carry

    lax.fori_loop(0, GROUPS, one, 0, unroll=UNROLL)


def inner_first(pos, e, kap, share, flux, weight, up_c, east_c, above_c, e01, ssum):
    ssum[...] = jnp.zeros_like(ssum)

    def prepare(g, base, tiles):
        ks = [kap[tile(base + r), :] for r in range(ROWS)]
        sums = [ssum[tile(r), :] for r in range(ROWS)]
        share_row = share_of(share, g)
        out = []
        for r in range(ROWS):
            k = ks[r]
            c_up, c_east = COEF * (k + pltpu.roll(k, LAT - 1, 0)), COEF * (k + pltpu.roll(k, LANES - 1, 1))
            out.append((c_up, c_east, COEF * (k + ks[r + 1]) if r + 1 < ROWS else None))
        for r in range(ROWS):
            i = base + r
            up_c[tile(i), :], east_c[tile(i), :] = out[r][:2]
            if r + 1 < ROWS:
                above_c[tile(i), :] = out[r][2]
            e01[tile(i), :] = SCALE * tiles[r]
            ssum[tile(r), :] = sums[r] + ks[r] * share_row
        return out

    inner_body(e, None, flux, weight, prepare)


def inner_next(pos, e, up_c, east_c, above_c, flux, weight):
    inner_body(e, (up_c, east_c, above_c), flux, weight, None)


def unpack_halos(pos, slabs, at, halo):
    part, tp = pos[0], pos[1]
    rows = pl.ds(at, TILES)
    halo[1 - tp] = slabs[0][rows, :].astype(F32)
    halo[tp] = slabs[1][rows, :].astype(F32)
    halo[3 - part] = slabs[2][rows, :].astype(F32)
    halo[2 + part] = slabs[3][rows, :].astype(F32)


def outer_body(e, e01, kap, share, temp4, halo, edge, flux, weight, enew, ksum, numer, denom):
    def one(g, carry):
        base = g * ROWS
        row_share = share_of(share, g)
        refs = (e, kap, weight, flux, e01)
        rows = [[x[tile(base + r), :] for x in refs] + [temp4[tile(r), :]] for r in range(ROWS)]
        ends = {at: (halo[j, tile(g), :], edge[j, tile(g), :]) for j, at in ((2, 0), (3, ROWS - 1))}
        out = []
        for r in range(ROWS):
            here, k, w, f, old, t4 = rows[r]
            if r in ends:
                w_out, f_out = face(here, *ends[r])
                w, f = w + w_out, f + f_out
            out.append((old + k * (row_share * t4) + (here * w + f), SCALE + k + w))
        for r in range(ROWS):
            numer[tile(base + r), :], denom[tile(base + r), :] = out[r]
        return carry

    lax.fori_loop(0, GROUPS, one, 0, unroll=UNROLL)
    for j, at in ((0, 0), (1, LAT - 1)):
        strip = pl.ds(at, TILES, stride=LAT)
        out = halo[j]
        w, _ = face(e[strip, :], out, edge[j])
        numer[strip, :] = numer[strip, :] + w * out
        denom[strip, :] = denom[strip, :] + w

    def two(g, sums):
        at = [tile(g * ROWS + r) for r in range(ROWS)]
        fresh = [numer[i, :] / denom[i, :] for i in at]
        sums = tuple(sums[r] + kap[at[r], :] * fresh[r] for r in range(ROWS))
        for r in range(ROWS):
            enew[at[r], :] = fresh[r]
        return sums

    sums = lax.fori_loop(0, GROUPS, two, (jnp.zeros((LAT, LANES), F32),) * ROWS, unroll=UNROLL)
    for r in range(ROWS):
        ksum[tile(r), :] = sums[r]


def own_rows(pos, ref):
    return ref[pl.ds(pl.multiple_of(pos[0] * N, N), N), :]


def terms(told, t, stot):
    cube = t * t * t
    return HEAT * told + 3.0 * stot * (cube * t), HEAT + 4.0 * stot * cube


def outer_first(pos, e, e01, kap, share, told, ssum, flux, weight, h0, h1, h2, h3, *refs):
    enew, sums, edge, t1, t2, r1, r2 = refs[:7]
    temp4, halo, numer, denom = refs[7:]
    slabs = (h0, h1, h2, h3)
    unpack_halos(pos, slabs, TILES, halo)
    for j, at in ((0, 0), (1, LAT - 1)):
        edge[j] = COEF * (kap[pl.ds(at, TILES, stride=LAT), :] + halo[j])
    for g in range(GROUPS):
        for j, at in ((2, 0), (3, ROWS - 1)):
            edge[j, tile(g), :] = COEF * (kap[tile(g * ROWS + at), :] + halo[j, tile(g), :])
    unpack_halos(pos, slabs, 0, halo)
    t = own_rows(pos, told)
    temp4[...] = t * t * t * t
    outer_body(e, e01, kap, share, temp4, halo, edge, flux, weight, enew, sums.at[pl.ds(0, N)], numer, denom)
    sums[pl.ds(N, N), :] = ssum[...]
    write_slabs(pos, enew, 0, t1, t2, r1, r2)


def outer_middle(pos, e, e01, kap, share, told, sums, got, edge, flux, weight, h0, h1, h2, h3, *refs):
    enew, ksum, tnow, stot, t1, t2, r1, r2 = refs[:8]
    temp4, halo, numer, denom = refs[8:]
    unpack_halos(pos, (h0, h1, h2, h3), 0, halo)
    both = (sums[...] + got[...]) / SCALE
    s = both[N:]
    stot[...] = s
    t = own_rows(pos, told)
    up, down = terms(t, t, s)
    t = (up + both[:N]) / down
    tnow[...] = t
    temp4[...] = t * t * t * t
    outer_body(e, e01, kap, share, temp4, halo, edge, flux, weight, enew, ksum, numer, denom)
    write_slabs(pos, enew, 0, t1, t2, r1, r2)


def outer_last(pos, e, e01, kap, share, told, tprev, stot, part, got, edge, flux, weight, h0, h1, h2, h3, *refs):
    eown, send, ksum = refs[:3]
    temp4, halo, numer, denom, enew = refs[3:]
    unpack_halos(pos, (h0, h1, h2, h3), 0, halo)
    s = stot[...]
    old = own_rows(pos, told)
    up, down = terms(old, tprev[...], s)
    t = (up + (part[...] + got[...]) / SCALE) / down
    temp4[...] = t * t * t * t
    outer_body(e, e01, kap, share, temp4, halo, edge, flux, weight, enew, ksum, numer, denom)
    slot = pos[2] % 2
    eown[...] = enew[pl.ds(pl.multiple_of(slot * PART, PART), PART), :]
    send[pl.ds(0, PART), :] = enew[pl.ds(pl.multiple_of((1 - slot) * PART, PART), PART), :]
    up, down = terms(old, t, s)
    send[pl.ds(PART, N), :] = ksum[...]
    send[pl.ds(PART + N, N), :] = up
    send[pl.ds(PART + 2 * N, N), :] = down


def join_kernel(pos, eown, send, pair, near, far, energy, temp):
    half = pos[0]
    for g in range(OWN):
        src = pl.ds(g * N, N)
        energy[pl.ds(pl.multiple_of((2 * g + half) * N, N), N), :] = eown[src, :]
        energy[pl.ds(pl.multiple_of((2 * g + 1 - half) * N, N), N), :] = pair[src, :]
    k, up, down = pl.ds(PART, N), pl.ds(PART + N, N), pl.ds(PART + 2 * N, N)
    temp[pl.ds(pl.multiple_of(half * N, N), N), :] = (send[up, :] + (send[k, :] + near[...]) / SCALE) / send[down, :]
    temp[pl.ds(pl.multiple_of((1 - half) * N, N), N), :] = (pair[up, :] + (pair[k, :] + far[...]) / SCALE) / pair[down, :]


def theta_pairs(count, odd):
    return [p for i in range(odd, count - 1, 2) for p in ((i, i + 1), (i + 1, i))]


def row_pairs(rows, odd):
    def device(chain, position):
        row, part = position // 2, position % 2
        return row * 4 + 2 * chain + (part ^ (row & 1))

    pairs = []
    for chain in range(2):
        for i in range(odd, 2 * rows - 1, 2):
            a, b = device(chain, i), device(chain, i + 1)
            pairs += [(a, b), (b, a)]
    return pairs


def xor(x, k):
    return lax.ppermute(x, "group", [(i, i ^ k) for i in range(4)])


def swap_halos(slabs, part=None):
    t1, t2, r1, r2 = slabs
    nt, nr = lax.axis_size("theta"), lax.axis_size("row")
    t2 = lax.ppermute(t2, "theta", theta_pairs(nt, 1))
    part = part if part is None else keep(xor(part, 2))
    t1 = lax.ppermute(t1, "theta", theta_pairs(nt, 0))
    r2 = lax.ppermute(r2, ("row", "group"), row_pairs(nr, 1))
    r1 = lax.ppermute(r1, ("row", "group"), row_pairs(nr, 0))
    return tuple(keep(x) for x in (t1, t2, r1, r2)), part


def shards(dust, table, planck, energy_old, temp_old):
    place = lax.axis_index("group")
    row = lax.axis_index("row")
    pos = jnp.stack([(place ^ row) & 1, lax.axis_index("theta") & 1, place, row]).astype(jnp.int32)
    dust = dust.reshape(BINS, 2 * N, LANES)
    energy_old = energy_old.reshape(OWN, 2 * N, LANES)
    told = temp_old.reshape(-1, LANES)
    tab = table.astype(F32).reshape(-1)
    slabs = [held((TILES, LANES), BF)] * 4
    scratch = [VMEM((N, LANES), F32), VMEM((4, TILES, LANES), F32), VMEM((CELLS, LANES), F32), VMEM((CELLS, LANES), F32)]
    full = held((CELLS, LANES))
    sheet = held((N, LANES))
    block = held((BINS, N, LANES), BF)

    eown, pair, mine, far = call(
        pack_kernel,
        [held((OWN, N, LANES)), held((SIZE + PART + 6 * LAT, LANES), BF), block, block],
        (pos, *(pltpu.with_memory_space_constraint(x, pltpu.HBM) for x in (planck, dust, energy_old))), smem=1, space=pl.ANY,
        scratch=[VMEM((OWN, N, LANES), F32), SMEM(planck.shape, F32), pltpu.SemaphoreType.DMA((5,))],
    )
    far = xor(far, 3)
    near = xor(mine, 2)
    pair = xor(pair, 1)
    early, = call(
        early_kernel, [full], (pos, tab, keep(mine), keep(near), keep(far)), smem=2,
        scratch=[VMEM((3 * SIZE, LANES), F32)], flops=20_000_000,
    )
    kap, e, share, *both = call(
        late_kernel,
        [full, full, held((2, 2 * LAT, LANES))] + [held((2 * TILES, LANES), BF)] * 4,
        (pos, tab, planck, keep(early), keep(eown), keep(pair)), smem=3,
        scratch=[VMEM((SIZE, LANES), F32)], flops=5_000_000,
    )
    kap, share, e = keep(kap), keep(share), keep(e)
    halos, _ = swap_halos(both)
    flux, weight, *coefs, e01, ssum = call(
        inner_first, [full] * 6 + [sheet], (pos, e, kap, share), smem=1, flops=20_000_000,
    )
    coefs = [keep(x) for x in coefs]
    e01 = keep(e01)
    e, sums, edge, *rest = call(
        outer_first, [full, held((2 * N, LANES)), held((4, TILES, LANES))] + slabs,
        (pos, e, e01, kap, share, told, keep(ssum), keep(flux), keep(weight), *halos), smem=1,
        scratch=scratch, flops=5_000_000,
    )
    e, edge, sums = keep(e), keep(edge), keep(sums)
    halos, got = swap_halos(rest, sums)
    flux, weight = call(inner_next, [full] * 2, (pos, e, *coefs), smem=1, flops=20_000_000)
    e, part, temp, stot, *rest = call(
        outer_middle, [full, sheet, sheet, sheet] + slabs,
        (pos, e, e01, kap, share, told, sums, got, edge, keep(flux), keep(weight), *halos), smem=1,
        scratch=scratch, flops=5_000_000,
    )
    e, part = keep(e), keep(part)
    halos, got = swap_halos(rest, part)
    flux, weight = call(inner_next, [full] * 2, (pos, e, *coefs), smem=1, flops=20_000_000)
    eown, send, part = call(
        outer_last, [held((PART, LANES)), held((PART + 3 * N, LANES)), sheet],
        (pos, e, e01, kap, share, told, keep(temp), keep(stot), part, got, edge, keep(flux), keep(weight), *halos), smem=1,
        scratch=scratch + [VMEM((CELLS, LANES), F32)], flops=5_000_000,
    )
    pair = xor(send, 1)
    far = xor(part, 3)
    near = xor(part, 2)
    energy, temp = call(
        join_kernel,
        [jax.ShapeDtypeStruct((2 * PART, LANES), F32), jax.ShapeDtypeStruct((2 * N, LANES), F32)],
        (pos, keep(eown), keep(send), keep(pair), keep(near), keep(far)), smem=1,
    )
    return energy.reshape(OWN, 2 * ROWS, LAT, LANES), temp.reshape(2 * ROWS, LAT, LANES)


def solution(mesh):
    return jax.shard_map(
        shards,
        mesh=mesh,
        in_specs=(
            P("group", "row", "theta", None),
            P(),
            P("group"),
            P("group", "row", "theta", None),
            P("row", "theta", None),
        ),
        out_specs=(P("group", "row", "theta", None), P("row", "theta", None)),
        check_vma=False,
    )
```

profile of v0, /device:TPU:31, one launch (start us, length us, event | category | flops | bytes accessed | tf_op | source)
XLA Modules:
  0.0 116.3 jit_solution(14620884025631220168)
XLA Ops:
  0.7 1.8 %shard_map.68 = (f32[12,64,128]{2,1,0:T(8,128)S(1)}, bf16[1328,128]{1,0:T(8,128)(2,1)S(1)}, bf16[8,64,128]{2,1,0:T(8,128)(2,1)S(1)}, bf16[8,64,128]{2,1,0:T(8,128)(2,1)S(1)}) custom-call(s32[4]{0:T(128)S(1)} %pad_add_fusion.pos, f32[12]{0:T(128)} %planck.3, bf16[8,128,128]{2,1,0:T(8,128)(2,1)} %bitcast.13, f32[12,128,128]{2,1,0:T(8,128)} %bitcast.12), custom_call_target="tpu_custom_call" | custom-call | flops 1000000 | bytes 1000000 | tf_op jit(solution)/shard_map/pallas_call | solution.py:32
  2.5 4.0 %collective-permute-start.2 = (bf16[1328,128]{1,0:T(8,128)(2,1)S(1)}, bf16[1328,128]{1,0:T(8,128)(2,1)S(1)}, u32[]{:S(2)}, u32[]{:S(2)}) collective-permute-start(bf16[1328,128]{1,0:T(8,128)(2,1)S(1)} %get-tuple-element.47), channel_id=1, source_target_pairs={{0,1},{1,0},{2,3},{3,2},{4,5},{5,4},{6,7},{7,6},{8,9},{9,8},{10,11... | collective-permute-start | bytes 1019912 | tf_op jit(solution)/shard_map/ppermute | solution.py:390
  6.6 5.5 %collective-permute-start.1 = (bf16[8,64,128]{2,1,0:T(8,128)(2,1)S(1)}, bf16[8,64,128]{2,1,0:T(8,128)(2,1)S(1)}, u32[]{:S(2)}, u32[]{:S(2)}) collective-permute-start(bf16[8,64,128]{2,1,0:T(8,128)(2,1)S(1)} %get-tuple-element.45), channel_id=1, source_target_pairs={{0,3},{1,2},{2,1},{3,0},{4,7},{5,6},{6,5},{7,4},{8,11},{9,10},{10,... | collective-permute-start | bytes 393224 | tf_op jit(solution)/shard_map/ppermute | solution.py:390
  12.1 2.2 %collective-permute-start = (bf16[8,64,128]{2,1,0:T(8,128)(2,1)S(1)}, bf16[8,64,128]{2,1,0:T(8,128)(2,1)S(1)}, u32[]{:S(2)}, u32[]{:S(2)}) collective-permute-start(bf16[8,64,128]{2,1,0:T(8,128)(2,1)S(1)} %get-tuple-element.44.mine), channel_id=1, source_target_pairs={{0,2},{1,3},{2,0},{3,1},{4,6},{5,7},{6,4},{7,5},{8,10},{9,11},{10,... | collective-permute-start | bytes 393224 | tf_op jit(solution)/shard_map/ppermute | solution.py:390
  14.4 6.3 %collective-permute-done.1.far = bf16[8,64,128]{2,1,0:T(8,128)(2,1)S(1)} collective-permute-done((bf16[8,64,128]{2,1,0:T(8,128)(2,1)S(1)}, bf16[8,64,128]{2,1,0:T(8,128)(2,1)S(1)}, u32[]{:S(2)}, u32[]{:S(2)}) %collective-permute-start.1) | collective-permute-done | bytes 131104 | tf_op jit(solution)/shard_map/ppermute | solution.py:390
  20.7 4.5 %collective-permute-done.near = bf16[8,64,128]{2,1,0:T(8,128)(2,1)S(1)} collective-permute-done((bf16[8,64,128]{2,1,0:T(8,128)(2,1)S(1)}, bf16[8,64,128]{2,1,0:T(8,128)(2,1)S(1)}, u32[]{:S(2)}, u32[]{:S(2)}) %collective-permute-start) | collective-permute-done | bytes 131104 | tf_op jit(solution)/shard_map/ppermute | solution.py:390
  25.2 2.3 %shard_map.69.part = f32[1536,128]{1,0:T(8,128)S(1)} custom-call(s32[4]{0:T(128)S(1)} %pad_add_fusion.pos, f32[1536]{0:T(1024)S(1)} %reshape.32.tab, bf16[8,64,128]{2,1,0:T(8,128)(2,1)S(1)} %get-tuple-element.44.mine, bf16[8,64,128]{2,1,0:T(8,128)(2,1)S(1)} %collective-permute-done.near, bf16[8,64,128]{2,1,0:T(8,128)(2,1)S(1)} %collective-permute-done.1.far), custom_call_target="tpu_custom_call" | custom-call | flops 20000000 | bytes 1000000 | tf_op jit(solution)/shard_map/pallas_call | solution.py:32
  28.1 1.5 %shard_map.70 = (f32[1536,128]{1,0:T(8,128)S(1)}, f32[1536,128]{1,0:T(8,128)S(1)}, f32[2,16,128]{2,1,0:T(8,128)S(1)}, bf16[384,128]{1,0:T(8,128)(2,1)S(1)}, bf16...) custom-call(s32[4]{0:T(128)S(1)} %pad_add_fusion.pos, f32[1536]{0:T(1024)S(1)} %reshape.32.tab, ...), custom_call_target="tpu_custom_call" | custom-call | flops 5000000 | bytes 1000000 | tf_op jit(solution)/shard_map/pallas_call | solution.py:32
  29.7 2.5 %collective-permute-start.3 = (bf16[384,128]{1,0:T(8,128)(2,1)S(1)}, bf16[384,128]{1,0:T(8,128)(2,1)S(1)}, u32[]{:S(2)}, u32[]{:S(2)}) collective-permute-start(bf16[384,128]{1,0:T(8,128)(2,1)S(1)} %get-tuple-element.55), channel_id=1, source_target_pairs={{0,4},{4,0},{8,12},{12,8},{16,20},{20,16},{24,28},{28,24},{32,36},... | collective-permute-start | bytes 294920 | tf_op jit(solution)/shard_map/ppermute | solution.py:398
  32.1 10.9 %collective-permute-start.4 = (bf16[384,128]{1,0:T(8,128)(2,1)S(1)}, bf16[384,128]{1,0:T(8,128)(2,1)S(1)}, u32[]{:S(2)}, u32[]{:S(2)}) collective-permute-start(bf16[384,128]{1,0:T(8,128)(2,1)S(1)} %get-tuple-element.56), channel_id=1, source_target_pairs={{4,8},{8,4},{12,16},{16,12},{20,24},{24,20},{28,32},{32,28},{36,40... | collective-permute-start | bytes 294920 | tf_op jit(solution)/shard_map/ppermute | solution.py:396
  43.0 1.9 %collective-permute-start.5 = (bf16[384,128]{1,0:T(8,128)(2,1)S(1)}, bf16[384,128]{1,0:T(8,128)(2,1)S(1)}, u32[]{:S(2)}, u32[]{:S(2)}) collective-permute-start(bf16[384,128]{1,0:T(8,128)(2,1)S(1)} %get-tuple-element.57), channel_id=1, source_target_pairs={{0,1},{1,0},{49,48},{48,49},{96,97},{97,96},{145,144},{144,145},{1... | collective-permute-start | bytes 294920 | tf_op jit(solution)/shard_map/ppermute | solution.py:400
  45.0 6.1 %collective-permute-start.6 = (bf16[384,128]{1,0:T(8,128)(2,1)S(1)}, bf16[384,128]{1,0:T(8,128)(2,1)S(1)}, u32[]{:S(2)}, u32[]{:S(2)}) collective-permute-start(bf16[384,128]{1,0:T(8,128)(2,1)S(1)} %get-tuple-element.58), channel_id=1, source_target_pairs={{1,49},{49,1},{48,96},{96,48},{97,145},{145,97},{144,192},{192,144... | collective-permute-start | bytes 294920 | tf_op jit(solution)/shard_map/ppermute | solution.py:399
  51.1 2.2 %shard_map.71 = (f32[1536,128]{1,0:T(8,128)S(1)}, f32[1536,128]{1,0:T(8,128)S(1)}, f32[1536,128]{1,0:T(8,128)S(1)}, f32[1536,128]{1,0:T(8,128)S(1)}, f32[1536,12...) custom-call(s32[4]{0:T(128)S(1)} %pad_add_fusion.pos, f32[1536,128]{1,0:T(8,128)S(1)} %get-tuple-element.48.e, ...), custom_call_target="tpu_custom_call" | custom-call | flops 20000000 | bytes 1000000 | tf_op jit(solution)/shard_map/pallas_call | solution.py:32
  53.4 1.5 %shard_map.72 = (f32[1536,128]{1,0:T(8,128)S(1)}, f32[128,128]{1,0:T(8,128)S(1)}, f32[4,192,128]{2,1,0:T(8,128)S(1)}, bf16[192,128]{1,0:T(8,128)(2,1)S(1)}, bf16...) custom-call(s32[4]{0:T(128)S(1)} %pad_add_fusion.pos, ...), custom_call_target="tpu_custom_call" | custom-call | flops 5000000 | bytes 1000000 | tf_op jit(solution)/shard_map/pallas_call | solution.py:32
  54.9 3.6 %collective-permute-start.7 = (f32[128,128]{1,0:T(8,128)S(1)}, f32[128,128]{1,0:T(8,128)S(1)}, u32[]{:S(2)}, u32[]{:S(2)}) collective-permute-start(f32[128,128]{1,0:T(8,128)S(1)} %get-tuple-element.60.sums), channel_id=1, source_target_pairs={{0,2},{1,3},{2,0},{3,1},{4,6},{5,7},{6,4},{7,5},{8,10},{9,11},{10,... | collective-permute-start | bytes 196616 | tf_op jit(solution)/shard_map/ppermute | solution.py:390
  58.5 1.9 %collective-permute-start.8 = (bf16[192,128]{1,0:T(8,128)(2,1)S(1)}, bf16[192,128]{1,0:T(8,128)(2,1)S(1)}, u32[]{:S(2)}, u32[]{:S(2)}) collective-permute-start(bf16[192,128]{1,0:T(8,128)(2,1)S(1)} %get-tuple-element.67), channel_id=1, source_target_pairs={{0,4},{4,0},{8,12},{12,8},{16,20},{20,16},{24,28},{28,24},{32,36},... | collective-permute-start | bytes 147464 | tf_op jit(solution)/shard_map/ppermute | solution.py:398
  60.5 4.0 %collective-permute-start.9 = (bf16[192,128]{1,0:T(8,128)(2,1)S(1)}, bf16[192,128]{1,0:T(8,128)(2,1)S(1)}, u32[]{:S(2)}, u32[]{:S(2)}) collective-permute-start(bf16[192,128]{1,0:T(8,128)(2,1)S(1)} %get-tuple-element.68), channel_id=1, source_target_pairs={{4,8},{8,4},{12,16},{16,12},{20,24},{24,20},{28,32},{32,28},{36,40... | collective-permute-start | bytes 147464 | tf_op jit(solution)/shard_map/ppermute | solution.py:396
  64.5 5.1 %collective-permute-start.10 = (bf16[192,128]{1,0:T(8,128)(2,1)S(1)}, bf16[192,128]{1,0:T(8,128)(2,1)S(1)}, u32[]{:S(2)}, u32[]{:S(2)}) collective-permute-start(bf16[192,128]{1,0:T(8,128)(2,1)S(1)} %get-tuple-element.69), channel_id=1, source_target_pairs={{0,1},{1,0},{49,48},{48,49},{96,97},{97,96},{145,144},{144,145},{1... | collective-permute-start | bytes 147464 | tf_op jit(solution)/shard_map/ppermute | solution.py:400
  69.6 5.6 %collective-permute-start.11 = (bf16[192,128]{1,0:T(8,128)(2,1)S(1)}, bf16[192,128]{1,0:T(8,128)(2,1)S(1)}, u32[]{:S(2)}, u32[]{:S(2)}) collective-permute-start(bf16[192,128]{1,0:T(8,128)(2,1)S(1)} %get-tuple-element.70), channel_id=1, source_target_pairs={{1,49},{49,1},{48,96},{96,48},{97,145},{145,97},{144,192},{192,144... | collective-permute-start | bytes 147464 | tf_op jit(solution)/shard_map/ppermute | solution.py:399
  75.3 2.0 %shard_map.73 = (f32[1536,128]{1,0:T(8,128)S(1)}, f32[1536,128]{1,0:T(8,128)S(1)}) custom-call(s32[4]{0:T(128)S(1)} %pad_add_fusion.pos, f32[1536,128]{1,0:T(8,128)S(1)} %get-tuple-element.59.e, f32[1536,128]{1,0:T(8,128)S(1)} %get-tuple-element.62.up_c, f32[1536,128]{1,0:T(8,128)S(1)} %get-tuple-element.63.east_c, f32[1536,128]{1,0:T(8,128)S(1)} %get-tuple-element.64.above_c), custom_call_target="tpu_custom_call" | custom-call | flops 20000000 | bytes 1000000 | tf_op jit(solution)/shard_map/pallas_call | solution.py:32
  78.8 1.9 %collective-permute-start.13 = (bf16[192,128]{1,0:T(8,128)(2,1)S(1)}, bf16[192,128]{1,0:T(8,128)(2,1)S(1)}, u32[]{:S(2)}, u32[]{:S(2)}) collective-permute-start(bf16[192,128]{1,0:T(8,128)(2,1)S(1)} %get-tuple-element.77), channel_id=1, source_target_pairs={{0,4},{4,0},{8,12},{12,8},{16,20},{20,16},{24,28},{28,24},{32,36},... | collective-permute-start | bytes 147464 | tf_op jit(solution)/shard_map/ppermute | solution.py:398
  80.7 4.7 %collective-permute-start.14 = (bf16[192,128]{1,0:T(8,128)(2,1)S(1)}, bf16[192,128]{1,0:T(8,128)(2,1)S(1)}, u32[]{:S(2)}, u32[]{:S(2)}) collective-permute-start(bf16[192,128]{1,0:T(8,128)(2,1)S(1)} %get-tuple-element.78), channel_id=1, source_target_pairs={{4,8},{8,4},{12,16},{16,12},{20,24},{24,20},{28,32},{32,28},{36,40... | collective-permute-start | bytes 147464 | tf_op jit(solution)/shard_map/ppermute | solution.py:396
  85.4 1.9 %collective-permute-start.15 = (bf16[192,128]{1,0:T(8,128)(2,1)S(1)}, bf16[192,128]{1,0:T(8,128)(2,1)S(1)}, u32[]{:S(2)}, u32[]{:S(2)}) collective-permute-start(bf16[192,128]{1,0:T(8,128)(2,1)S(1)} %get-tuple-element.79), channel_id=1, source_target_pairs={{0,1},{1,0},{49,48},{48,49},{96,97},{97,96},{145,144},{144,145},{1... | collective-permute-start | bytes 147464 | tf_op jit(solution)/shard_map/ppermute | solution.py:400
  87.3 5.1 %collective-permute-start.16 = (bf16[192,128]{1,0:T(8,128)(2,1)S(1)}, bf16[192,128]{1,0:T(8,128)(2,1)S(1)}, u32[]{:S(2)}, u32[]{:S(2)}) collective-permute-start(bf16[192,128]{1,0:T(8,128)(2,1)S(1)} %get-tuple-element.80), channel_id=1, source_target_pairs={{1,49},{49,1},{48,96},{96,48},{97,145},{145,97},{144,192},{192,144... | collective-permute-start | bytes 147464 | tf_op jit(solution)/shard_map/ppermute | solution.py:399
  92.5 2.9 %collective-permute-start.12 = (f32[64,128]{1,0:T(8,128)S(1)}, f32[64,128]{1,0:T(8,128)S(1)}, u32[]{:S(2)}, u32[]{:S(2)}) collective-permute-start(f32[64,128]{1,0:T(8,128)S(1)} %get-tuple-element.74.part), channel_id=1, source_target_pairs={{0,2},{1,3},{2,0},{3,1},{4,6},{5,7},{6,4},{7,5},{8,10},{9,11},{10,... | collective-permute-start | bytes 98312 | tf_op jit(solution)/shard_map/ppermute | solution.py:390
  95.4 2.0 %shard_map.75 = (f32[1536,128]{1,0:T(8,128)S(1)}, f32[1536,128]{1,0:T(8,128)S(1)}) custom-call(s32[4]{0:T(128)S(1)} %pad_add_fusion.pos, f32[1536,128]{1,0:T(8,128)S(1)} %get-tuple-element.71.e, f32[1536,128]{1,0:T(8,128)S(1)} %get-tuple-element.62.up_c, f32[1536,128]{1,0:T(8,128)S(1)} %get-tuple-element.63.east_c, f32[1536,128]{1,0:T(8,128)S(1)} %get-tuple-element.64.above_c), custom_call_target="tpu_custom_call" | custom-call | flops 20000000 | bytes 1000000 | tf_op jit(solution)/shard_map/pallas_call | solution.py:32
  98.0 1.5 %shard_map.76 = (f32[768,128]{1,0:T(8,128)S(1)}, f32[960,128]{1,0:T(8,128)S(1)}, f32[64,128]{1,0:T(8,128)S(1)}) custom-call(s32[4]{0:T(128)S(1)} %pad_add_fusion.pos, f32[1536,128]{1,0:T(8,128)S(1)} %get-tuple-element.71.e, f32[1536,128]{1,0:T(8,128)S(1)} %get-tuple-element.51.e01, f32[1536,128]{1,0:T(8,128)S(1)} %get-tuple-element.49.kap, ...), custom_call_target="tpu_custom_call" | custom-call | flops 5000000 | bytes 1000000 | tf_op jit(solution)/shard_map/pallas_call | solution.py:32
  99.5 1.9 %collective-permute-start.17 = (f32[960,128]{1,0:T(8,128)S(1)}, f32[960,128]{1,0:T(8,128)S(1)}, u32[]{:S(2)}, u32[]{:S(2)}) collective-permute-start(f32[960,128]{1,0:T(8,128)S(1)} %get-tuple-element.82.send), channel_id=1, source_target_pairs={{0,1},{1,0},{2,3},{3,2},{4,5},{5,4},{6,7},{7,6},{8,9},{9,8},{10,11... | collective-permute-start | bytes 1474568 | tf_op jit(solution)/shard_map/ppermute | solution.py:390
  101.5 4.1 %collective-permute-start.19 = (f32[64,128]{1,0:T(8,128)S(1)}, f32[64,128]{1,0:T(8,128)S(1)}, u32[]{:S(2)}, u32[]{:S(2)}) collective-permute-start(f32[64,128]{1,0:T(8,128)S(1)} %get-tuple-element.83), channel_id=1, source_target_pairs={{0,3},{1,2},{2,1},{3,0},{4,7},{5,6},{6,5},{7,4},{8,11},{9,10},{10,... | collective-permute-start | bytes 98312 | tf_op jit(solution)/shard_map/ppermute | solution.py:390
  105.6 2.4 %collective-permute-start.18 = (f32[64,128]{1,0:T(8,128)S(1)}, f32[64,128]{1,0:T(8,128)S(1)}, u32[]{:S(2)}, u32[]{:S(2)}) collective-permute-start(f32[64,128]{1,0:T(8,128)S(1)} %get-tuple-element.83), channel_id=1, source_target_pairs={{0,2},{1,3},{2,0},{3,1},{4,6},{5,7},{6,4},{7,5},{8,10},{9,11},{10,... | collective-permute-start | bytes 98312 | tf_op jit(solution)/shard_map/ppermute | solution.py:390
  107.9 6.9 %collective-permute-done.19.far = f32[64,128]{1,0:T(8,128)S(1)} collective-permute-done((f32[64,128]{1,0:T(8,128)S(1)}, f32[64,128]{1,0:T(8,128)S(1)}, u32[]{:S(2)}, u32[]{:S(2)}) %collective-permute-start.19) | collective-permute-done | bytes 32800 | tf_op jit(solution)/shard_map/ppermute | solution.py:390
  114.8 1.5 %shard_map.77 = (f32[1536,128]{1,0:T(8,128)}, f32[128,128]{1,0:T(8,128)}) custom-call(s32[4]{0:T(128)S(1)} %pad_add_fusion.pos, f32[768,128]{1,0:T(8,128)S(1)} %get-tuple-element.81.eown, f32[960,128]{1,0:T(8,128)S(1)} %get-tuple-element.82.send, f32[960,128]{1,0:T(8,128)S(1)} %collective-permute-done.17.pair, f32[64,128]{1,0:T(8,128)S(1)} %collective-permute-done.18.near, ...), custom_call_target="tpu_custom_call" | custom-call | flops 1000000 | bytes 1000000 | tf_op jit(solution)/shard_map/pallas_call | solution.py:32
  (26 shorter events, 3.0 us)
Async XLA Ops:
  0.7 13.6 %copy-start.2 = (bf16[32,48]{1,0:T(8,128)(2,1)S(1)}, bf16[32,48]{1,0:T(8,128)(2,1)}, u32[]{:S(2)}) copy-start(bf16[32,48]{1,0:T(8,128)(2,1)} %param.6) | copy-start | bytes 9220
  2.5 24.9 %collective-permute-start.2 = (bf16[1328,128]{1,0:T(8,128)(2,1)S(1)}, bf16[1328,128]{1,0:T(8,128)(2,1)S(1)}, u32[]{:S(2)}, u32[]{:S(2)}) collective-permute-start(bf16[1328,128]{1,0:T(8,128)(2,1)S(1)} %get-tuple-element.47), channel_id=1, source_target_pairs={{0,1},{1,0},{2,3},{3,2},{4,5},{5,4},{6,7},{7,6},{8,9},{9,8},{10,11... | collective-permute-start | bytes 1019912 | tf_op jit(solution)/shard_map/ppermute | solution.py:390
  6.6 14.1 %collective-permute-start.1 = (bf16[8,64,128]{2,1,0:T(8,128)(2,1)S(1)}, bf16[8,64,128]{2,1,0:T(8,128)(2,1)S(1)}, u32[]{:S(2)}, u32[]{:S(2)}) collective-permute-start(bf16[8,64,128]{2,1,0:T(8,128)(2,1)S(1)} %get-tuple-element.45), channel_id=1, source_target_pairs={{0,3},{1,2},{2,1},{3,0},{4,7},{5,6},{6,5},{7,4},{8,11},{9,10},{10,... | collective-permute-start | bytes 393224 | tf_op jit(solution)/shard_map/ppermute | solution.py:390
  12.1 13.1 %collective-permute-start = (bf16[8,64,128]{2,1,0:T(8,128)(2,1)S(1)}, bf16[8,64,128]{2,1,0:T(8,128)(2,1)S(1)}, u32[]{:S(2)}, u32[]{:S(2)}) collective-permute-start(bf16[8,64,128]{2,1,0:T(8,128)(2,1)S(1)} %get-tuple-element.44.mine), channel_id=1, source_target_pairs={{0,2},{1,3},{2,0},{3,1},{4,6},{5,7},{6,4},{7,5},{8,10},{9,11},{10,... | collective-permute-start | bytes 393224 | tf_op jit(solution)/shard_map/ppermute | solution.py:390
  27.5 0.7 copy-start.1
  29.7 23.6 %collective-permute-start.3 = (bf16[384,128]{1,0:T(8,128)(2,1)S(1)}, bf16[384,128]{1,0:T(8,128)(2,1)S(1)}, u32[]{:S(2)}, u32[]{:S(2)}) collective-permute-start(bf16[384,128]{1,0:T(8,128)(2,1)S(1)} %get-tuple-element.55), channel_id=1, source_target_pairs={{0,4},{4,0},{8,12},{12,8},{16,20},{20,16},{24,28},{28,24},{32,36},... | collective-permute-start | bytes 294920 | tf_op jit(solution)/shard_map/ppermute | solution.py:398
  32.1 21.1 %collective-permute-start.4 = (bf16[384,128]{1,0:T(8,128)(2,1)S(1)}, bf16[384,128]{1,0:T(8,128)(2,1)S(1)}, u32[]{:S(2)}, u32[]{:S(2)}) collective-permute-start(bf16[384,128]{1,0:T(8,128)(2,1)S(1)} %get-tuple-element.56), channel_id=1, source_target_pairs={{4,8},{8,4},{12,16},{16,12},{20,24},{24,20},{28,32},{32,28},{36,40... | collective-permute-start | bytes 294920 | tf_op jit(solution)/shard_map/ppermute | solution.py:396
  43.0 10.2 %collective-permute-start.5 = (bf16[384,128]{1,0:T(8,128)(2,1)S(1)}, bf16[384,128]{1,0:T(8,128)(2,1)S(1)}, u32[]{:S(2)}, u32[]{:S(2)}) collective-permute-start(bf16[384,128]{1,0:T(8,128)(2,1)S(1)} %get-tuple-element.57), channel_id=1, source_target_pairs={{0,1},{1,0},{49,48},{48,49},{96,97},{97,96},{145,144},{144,145},{1... | collective-permute-start | bytes 294920 | tf_op jit(solution)/shard_map/ppermute | solution.py:400
  45.0 8.4 %collective-permute-start.6 = (bf16[384,128]{1,0:T(8,128)(2,1)S(1)}, bf16[384,128]{1,0:T(8,128)(2,1)S(1)}, u32[]{:S(2)}, u32[]{:S(2)}) collective-permute-start(bf16[384,128]{1,0:T(8,128)(2,1)S(1)} %get-tuple-element.58), channel_id=1, source_target_pairs={{1,49},{49,1},{48,96},{96,48},{97,145},{145,97},{144,192},{192,144... | collective-permute-start | bytes 294920 | tf_op jit(solution)/shard_map/ppermute | solution.py:399
  51.1 2.3 %copy-start = (f32[16,8,128]{2,1,0:T(8,128)S(1)}, f32[16,8,128]{2,1,0:T(8,128)}, u32[]{:S(2)}) copy-start(f32[16,8,128]{2,1,0:T(8,128)} %param.9) | copy-start | bytes 196612
  54.9 22.4 %collective-permute-start.7 = (f32[128,128]{1,0:T(8,128)S(1)}, f32[128,128]{1,0:T(8,128)S(1)}, u32[]{:S(2)}, u32[]{:S(2)}) collective-permute-start(f32[128,128]{1,0:T(8,128)S(1)} %get-tuple-element.60.sums), channel_id=1, source_target_pairs={{0,2},{1,3},{2,0},{3,1},{4,6},{5,7},{6,4},{7,5},{8,10},{9,11},{10,... | collective-permute-start | bytes 196616 | tf_op jit(solution)/shard_map/ppermute | solution.py:390
  58.5 18.7 %collective-permute-start.8 = (bf16[192,128]{1,0:T(8,128)(2,1)S(1)}, bf16[192,128]{1,0:T(8,128)(2,1)S(1)}, u32[]{:S(2)}, u32[]{:S(2)}) collective-permute-start(bf16[192,128]{1,0:T(8,128)(2,1)S(1)} %get-tuple-element.67), channel_id=1, source_target_pairs={{0,4},{4,0},{8,12},{12,8},{16,20},{20,16},{24,28},{28,24},{32,36},... | collective-permute-start | bytes 147464 | tf_op jit(solution)/shard_map/ppermute | solution.py:398
  60.5 16.8 %collective-permute-start.9 = (bf16[192,128]{1,0:T(8,128)(2,1)S(1)}, bf16[192,128]{1,0:T(8,128)(2,1)S(1)}, u32[]{:S(2)}, u32[]{:S(2)}) collective-permute-start(bf16[192,128]{1,0:T(8,128)(2,1)S(1)} %get-tuple-element.68), channel_id=1, source_target_pairs={{4,8},{8,4},{12,16},{16,12},{20,24},{24,20},{28,32},{32,28},{36,40... | collective-permute-start | bytes 147464 | tf_op jit(solution)/shard_map/ppermute | solution.py:396
  64.5 12.8 %collective-permute-start.10 = (bf16[192,128]{1,0:T(8,128)(2,1)S(1)}, bf16[192,128]{1,0:T(8,128)(2,1)S(1)}, u32[]{:S(2)}, u32[]{:S(2)}) collective-permute-start(bf16[192,128]{1,0:T(8,128)(2,1)S(1)} %get-tuple-element.69), channel_id=1, source_target_pairs={{0,1},{1,0},{49,48},{48,49},{96,97},{97,96},{145,144},{144,145},{1... | collective-permute-start | bytes 147464 | tf_op jit(solution)/shard_map/ppermute | solution.py:400
  69.6 7.7 %collective-permute-start.11 = (bf16[192,128]{1,0:T(8,128)(2,1)S(1)}, bf16[192,128]{1,0:T(8,128)(2,1)S(1)}, u32[]{:S(2)}, u32[]{:S(2)}) collective-permute-start(bf16[192,128]{1,0:T(8,128)(2,1)S(1)} %get-tuple-element.70), channel_id=1, source_target_pairs={{1,49},{49,1},{48,96},{96,48},{97,145},{145,97},{144,192},{192,144... | collective-permute-start | bytes 147464 | tf_op jit(solution)/shard_map/ppermute | solution.py:399
  78.8 19.2 %collective-permute-start.13 = (bf16[192,128]{1,0:T(8,128)(2,1)S(1)}, bf16[192,128]{1,0:T(8,128)(2,1)S(1)}, u32[]{:S(2)}, u32[]{:S(2)}) collective-permute-start(bf16[192,128]{1,0:T(8,128)(2,1)S(1)} %get-tuple-element.77), channel_id=1, source_target_pairs={{0,4},{4,0},{8,12},{12,8},{16,20},{20,16},{24,28},{28,24},{32,36},... | collective-permute-start | bytes 147464 | tf_op jit(solution)/shard_map/ppermute | solution.py:398
  80.7 17.3 %collective-permute-start.14 = (bf16[192,128]{1,0:T(8,128)(2,1)S(1)}, bf16[192,128]{1,0:T(8,128)(2,1)S(1)}, u32[]{:S(2)}, u32[]{:S(2)}) collective-permute-start(bf16[192,128]{1,0:T(8,128)(2,1)S(1)} %get-tuple-element.78), channel_id=1, source_target_pairs={{4,8},{8,4},{12,16},{16,12},{20,24},{24,20},{28,32},{32,28},{36,40... | collective-permute-start | bytes 147464 | tf_op jit(solution)/shard_map/ppermute | solution.py:396
  85.4 12.6 %collective-permute-start.15 = (bf16[192,128]{1,0:T(8,128)(2,1)S(1)}, bf16[192,128]{1,0:T(8,128)(2,1)S(1)}, u32[]{:S(2)}, u32[]{:S(2)}) collective-permute-start(bf16[192,128]{1,0:T(8,128)(2,1)S(1)} %get-tuple-element.79), channel_id=1, source_target_pairs={{0,1},{1,0},{49,48},{48,49},{96,97},{97,96},{145,144},{144,145},{1... | collective-permute-start | bytes 147464 | tf_op jit(solution)/shard_map/ppermute | solution.py:400
  87.3 10.7 %collective-permute-start.16 = (bf16[192,128]{1,0:T(8,128)(2,1)S(1)}, bf16[192,128]{1,0:T(8,128)(2,1)S(1)}, u32[]{:S(2)}, u32[]{:S(2)}) collective-permute-start(bf16[192,128]{1,0:T(8,128)(2,1)S(1)} %get-tuple-element.80), channel_id=1, source_target_pairs={{1,49},{49,1},{48,96},{96,48},{97,145},{145,97},{144,192},{192,144... | collective-permute-start | bytes 147464 | tf_op jit(solution)/shard_map/ppermute | solution.py:399
  92.5 5.6 %collective-permute-start.12 = (f32[64,128]{1,0:T(8,128)S(1)}, f32[64,128]{1,0:T(8,128)S(1)}, u32[]{:S(2)}, u32[]{:S(2)}) collective-permute-start(f32[64,128]{1,0:T(8,128)S(1)} %get-tuple-element.74.part), channel_id=1, source_target_pairs={{0,2},{1,3},{2,0},{3,1},{4,6},{5,7},{6,4},{7,5},{8,10},{9,11},{10,... | collective-permute-start | bytes 98312 | tf_op jit(solution)/shard_map/ppermute | solution.py:390
  99.5 15.3 %collective-permute-start.17 = (f32[960,128]{1,0:T(8,128)S(1)}, f32[960,128]{1,0:T(8,128)S(1)}, u32[]{:S(2)}, u32[]{:S(2)}) collective-permute-start(f32[960,128]{1,0:T(8,128)S(1)} %get-tuple-element.82.send), channel_id=1, source_target_pairs={{0,1},{1,0},{2,3},{3,2},{4,5},{5,4},{6,7},{7,6},{8,9},{9,8},{10,11... | collective-permute-start | bytes 1474568 | tf_op jit(solution)/shard_map/ppermute | solution.py:390
  101.5 13.3 %collective-permute-start.19 = (f32[64,128]{1,0:T(8,128)S(1)}, f32[64,128]{1,0:T(8,128)S(1)}, u32[]{:S(2)}, u32[]{:S(2)}) collective-permute-start(f32[64,128]{1,0:T(8,128)S(1)} %get-tuple-element.83), channel_id=1, source_target_pairs={{0,3},{1,2},{2,1},{3,0},{4,7},{5,6},{6,5},{7,4},{8,11},{9,10},{10,... | collective-permute-start | bytes 98312 | tf_op jit(solution)/shard_map/ppermute | solution.py:390
  105.6 9.2 %collective-permute-start.18 = (f32[64,128]{1,0:T(8,128)S(1)}, f32[64,128]{1,0:T(8,128)S(1)}, u32[]{:S(2)}, u32[]{:S(2)}) collective-permute-start(f32[64,128]{1,0:T(8,128)S(1)} %get-tuple-element.83), channel_id=1, source_target_pairs={{0,2},{1,3},{2,0},{3,1},{4,6},{5,7},{6,4},{7,5},{8,10},{9,11},{10,... | collective-permute-start | bytes 98312 | tf_op jit(solution)/shard_map/ppermute | solution.py:390
where the time goes:
time: 117 us; the launch traced here: 116 us
  starting transfers between devices  78.4 us (67%)
  waiting for transfers between devices  18.4 us (16%)
  Pallas kernels  17.7 us (15%)
    ppermute x8, starting transfers between devices, xor(): return lax.ppermute(x, 'group', [(i, i ^ k) for i in range(4)])  26.7 us
    ppermute x3, starting transfers between devices, swap_halos(): t2 = lax.ppermute(t2, 'theta', theta_pairs(nt, 1))  19.6 us
    ppermute x8, waiting for transfers between devices, xor(): return lax.ppermute(x, 'group', [(i, i ^ k) for i in range(4)])  18.3 us
    pallas_call x10, Pallas kernels, call(): pl.pallas_call(kernel, out_shape=outs, in_specs=specs, out_specs=[pl.Bloc...  17.7 us
    ppermute x3, starting transfers between devices, swap_halos(): r2 = lax.ppermute(r2, ('row', 'group'), row_pairs(nr, 1))  16.8 us
    ppermute x3, starting transfers between devices, swap_halos(): r1 = lax.ppermute(r1, ('row', 'group'), row_pairs(nr, 0))  8.96 us
    ppermute x3, starting transfers between devices, swap_halos(): t1 = lax.ppermute(t1, 'theta', theta_pairs(nt, 0))  6.29 us
  transfers between devices with their start and end apart: 20, of which 5 were waited for; matrix products, arithmetic and copies ran while one was open for 0% of the time, Pallas kernels for 7%

commit v1 on v0

--- a/solution.py
+++ b/solution.py
@@ -264,6 +264,8 @@
         refs = (e, kap, weight, flux, e01)
         rows = [[x[tile(base + r), :] for x in refs] + [temp4[tile(r), :]] for r in range(ROWS)]
         ends = {at: (halo[j, tile(g), :], edge[j, tile(g), :]) for j, at in ((2, 0), (3, ROWS - 1))}
+        strips = [pl.ds(base * LAT + at, ROWS, stride=LAT) for at in (0, LAT - 1)]
+        strips = [(strip, e[strip, :]) for strip in strips]
         out = []
         for r in range(ROWS):
             here, k, w, f, old, t4 = rows[r]
@@ -273,15 +275,13 @@
             out.append((old + k * (row_share * t4) + (here * w + f), SCALE + k + w))
         for r in range(ROWS):
             numer[tile(base + r), :], denom[tile(base + r), :] = out[r]
+        for j, (strip, past) in enumerate(strips):
+            w, _ = face(past, halo[j, tile(g), :], edge[j, tile(g), :])
+            numer[strip, :] = numer[strip, :] + w * halo[j, tile(g), :]
+            denom[strip, :] = denom[strip, :] + w
         return carry
 
-    lax.fori_loop(0, GROUPS, one, 0, unroll=UNROLL)
-    for j, at in ((0, 0), (1, LAT - 1)):
-        strip = pl.ds(at, TILES, stride=LAT)
-        out = halo[j]
-        w, _ = face(e[strip, :], out, edge[j])
-        numer[strip, :] = numer[strip, :] + w * out
-        denom[strip, :] = denom[strip, :] + w
+    lax.fori_loop(0, GROUPS, one, 0, unroll=8)
 
     def two(g, sums):
         at = [tile(g * ROWS + r) for r in range(ROWS)]
@@ -291,7 +291,7 @@
             enew[at[r], :] = fresh[r]
         return sums
 
-    sums = lax.fori_loop(0, GROUPS, two, (jnp.zeros((LAT, LANES), F32),) * ROWS, unroll=UNROLL)
+    sums = lax.fori_loop(0, GROUPS, two, (jnp.zeros((LAT, LANES), F32),) * ROWS, unroll=8)
     for r in range(ROWS):
         ksum[tile(r), :] = sums[r]
 
@@ -340,33 +340,43 @@
 
 
 def outer_last(pos, e, e01, kap, share, told, tprev, stot, part, got, edge, flux, weight, h0, h1, h2, h3, *refs):
-    eown, send, ksum = refs[:3]
-    temp4, halo, numer, denom, enew = refs[3:]
+    eown, send, ksum, up, down = refs[:5]
+    temp4, halo, numer, denom, enew = refs[5:]
     unpack_halos(pos, (h0, h1, h2, h3), 0, halo)
     s = stot[...]
     old = own_rows(pos, told)
-    up, down = terms(old, tprev[...], s)
-    t = (up + (part[...] + got[...]) / SCALE) / down
+    above, below = terms(old, tprev[...], s)
+    t = (above + (part[...] + got[...]) / SCALE) / below
     temp4[...] = t * t * t * t
     outer_body(e, e01, kap, share, temp4, halo, edge, flux, weight, enew, ksum, numer, denom)
     slot = pos[2] % 2
-    eown[...] = enew[pl.ds(pl.multiple_of(slot * PART, PART), PART), :]
-    send[pl.ds(0, PART), :] = enew[pl.ds(pl.multiple_of((1 - slot) * PART, PART), PART), :]
-    up, down = terms(old, t, s)
-    send[pl.ds(PART, N), :] = ksum[...]
-    send[pl.ds(PART + N, N), :] = up
-    send[pl.ds(PART + 2 * N, N), :] = down
-
-
-def join_kernel(pos, eown, send, pair, near, far, energy, temp):
+    for g in range(OWN):
+        eown[g] = enew[pl.ds(pl.multiple_of((slot * OWN + g) * N, N), N), :]
+        send[g] = enew[pl.ds(pl.multiple_of(((1 - slot) * OWN + g) * N, N), N), :]
+    up[...], down[...] = terms(old, t, s)
+
+
+def finish_kernel(ksum, got, up, down, temp):
+    temp[...] = (up[...] + (ksum[...] + got[...]) / SCALE) / down[...]
+
+
+def half_rows(half):
+    return pl.ds(pl.multiple_of(N * half, N), N)
+
+
+def own_kernel(pos, eown, energy, sem):
+    copy = pltpu.make_async_copy(eown, energy.at[:, half_rows(pos[0]), :], sem)
+    copy.start()
+    copy.wait()
+
+
+def join_kernel(pos, pair, mine, other, held_energy, energy, temp, sem):
     half = pos[0]
-    for g in range(OWN):
-        src = pl.ds(g * N, N)
-        energy[pl.ds(pl.multiple_of((2 * g + half) * N, N), N), :] = eown[src, :]
-        energy[pl.ds(pl.multiple_of((2 * g + 1 - half) * N, N), N), :] = pair[src, :]
-    k, up, down = pl.ds(PART, N), pl.ds(PART + N, N), pl.ds(PART + 2 * N, N)
-    temp[pl.ds(pl.multiple_of(half * N, N), N), :] = (send[up, :] + (send[k, :] + near[...]) / SCALE) / send[down, :]
-    temp[pl.ds(pl.multiple_of((1 - half) * N, N), N), :] = (pair[up, :] + (pair[k, :] + far[...]) / SCALE) / pair[down, :]
+    copy = pltpu.make_async_copy(pair, energy.at[:, half_rows(1 - half), :], sem)
+    copy.start()
+    temp[half_rows(half), :] = mine[...]
+    temp[half_rows(1 - half), :] = other[...]
+    copy.wait()
 
 
 def theta_pairs(count, odd):
@@ -457,19 +467,35 @@
     e, part = keep(e), keep(part)
     halos, got = swap_halos(rest, part)
     flux, weight = call(inner_next, [full] * 2, (pos, e, *coefs), smem=1, flops=20_000_000)
-    eown, send, part = call(
-        outer_last, [held((PART, LANES)), held((PART + 3 * N, LANES)), sheet],
+    eown, send, part, up, down = call(
+        outer_last, [held((OWN, N, LANES)), held((OWN, N, LANES)), sheet, sheet, sheet],
         (pos, e, e01, kap, share, told, keep(temp), keep(stot), part, got, edge, keep(flux), keep(weight), *halos), smem=1,
         scratch=scratch + [VMEM((CELLS, LANES), F32)], flops=5_000_000,
     )
+    whole = pltpu.HBM((OWN, 2 * N, LANES), F32)
     pair = xor(send, 1)
-    far = xor(part, 3)
-    near = xor(part, 2)
-    energy, temp = call(
+    got = xor(part, 2)
+    mine, = call(finish_kernel, [sheet], [keep(x) for x in (part, got, up, down)])
+    other = xor(mine, 1)
+    energy = pl.pallas_call(
+        own_kernel,
+        out_shape=whole,
+        in_specs=[pl.BlockSpec(memory_space=SMEM), pl.BlockSpec(memory_space=VMEM)],
+        out_specs=pl.BlockSpec(memory_space=pl.ANY),
+        scratch_shapes=[pltpu.SemaphoreType.DMA],
+        compiler_params=pltpu.CompilerParams(vmem_limit_bytes=16 << 20),
+        name="own",
+    )(pos, keep(eown))
+    energy, temp = pl.pallas_call(
         join_kernel,
-        [jax.ShapeDtypeStruct((2 * PART, LANES), F32), jax.ShapeDtypeStruct((2 * N, LANES), F32)],
-        (pos, keep(eown), keep(send), keep(pair), keep(near), keep(far)), smem=1,
-    )
+        out_shape=[whole, jax.ShapeDtypeStruct((2 * N, LANES), F32)],
+        in_specs=[pl.BlockSpec(memory_space=SMEM)] + [pl.BlockSpec(memory_space=VMEM)] * 3 + [pl.BlockSpec(memory_space=pl.ANY)],
+        out_specs=[pl.BlockSpec(memory_space=pl.ANY), pl.BlockSpec(memory_space=VMEM)],
+        scratch_shapes=[pltpu.SemaphoreType.DMA],
+        input_output_aliases={4: 0},
+        compiler_params=pltpu.CompilerParams(vmem_limit_bytes=16 << 20),
+        name="join",
+    )(pos, keep(pair), keep(mine), keep(other), energy)
     return energy.reshape(OWN, 2 * ROWS, LAT, LANES), temp.reshape(2 * ROWS, LAT, LANES)
 
 

time: 117 us -> 119 us (1.017)
  the two profiles are of different devices: /device:TPU:31 before, /device:TPU:38 now
where the time goes in v1:
time: 119 us; the launch traced here: 118 us
  starting transfers between devices  73.6 us (62%)
  waiting for transfers between devices  23.8 us (20%)
  Pallas kernels  19.1 us (16%)
    ppermute x8, starting transfers between devices, xor(): return lax.ppermute(x, 'group', [(i, i ^ k) for i in range(4)])  31.3 us
    ppermute x3, starting transfers between devices, swap_halos(): t2 = lax.ppermute(t2, 'theta', theta_pairs(nt, 1))  21.3 us
    ppermute x8, waiting for transfers between devices, xor(): return lax.ppermute(x, 'group', [(i, i ^ k) for i in range(4)])  18.1 us
    pallas_call x10, Pallas kernels, call(): pl.pallas_call(kernel, out_shape=outs, in_specs=specs, out_specs=[pl.Bloc...  15.9 us
    ppermute x3, starting transfers between devices, swap_halos(): r1 = lax.ppermute(r1, ('row', 'group'), row_pairs(nr, 0))  8.62 us
    ppermute x3, starting transfers between devices, swap_halos(): t1 = lax.ppermute(t1, 'theta', theta_pairs(nt, 0))  6.57 us
    ppermute x3, starting transfers between devices, swap_halos(): r2 = lax.ppermute(r2, ('row', 'group'), row_pairs(nr, 1))  5.76 us
    ppermute x3, waiting for transfers between devices, swap_halos(): r2 = lax.ppermute(r2, ('row', 'group'), row_pairs(nr, 1))  4.98 us
  transfers between devices with their start and end apart: 20, of which 8 were waited for; matrix products, arithmetic and copies ran while one was open for 0% of the time, Pallas kernels for 8%

profile of v1, /device:TPU:38, one launch (start us, length us, event | category | flops | bytes accessed | tf_op | source)
XLA Modules:
  0.0 118.3 jit_solution(8199081291400180088)
XLA Ops:
  0.7 1.8 %shard_map.68 = (f32[12,64,128]{2,1,0:T(8,128)S(1)}, bf16[1328,128]{1,0:T(8,128)(2,1)S(1)}, bf16[8,64,128]{2,1,0:T(8,128)(2,1)S(1)}, bf16[8,64,128]{2,1,0:T(8,128)(2,1)S(1)}) custom-call(s32[4]{0:T(128)S(1)} %pad_add_fusion.pos, f32[12]{0:T(128)} %planck.3, bf16[8,128,128]{2,1,0:T(8,128)(2,1)} %bitcast.14, f32[12,128,128]{2,1,0:T(8,128)} %bitcast.13), custom_call_target="tpu_custom_call" | custom-call | flops 1000000 | bytes 1000000 | tf_op jit(solution)/shard_map/pallas_call | solution.py:32
  2.5 4.3 %collective-permute-start.2 = (bf16[1328,128]{1,0:T(8,128)(2,1)S(1)}, bf16[1328,128]{1,0:T(8,128)(2,1)S(1)}, u32[]{:S(2)}, u32[]{:S(2)}) collective-permute-start(bf16[1328,128]{1,0:T(8,128)(2,1)S(1)} %get-tuple-element.49), channel_id=1, source_target_pairs={{0,1},{1,0},{2,3},{3,2},{4,5},{5,4},{6,7},{7,6},{8,9},{9,8},{10,11... | collective-permute-start | bytes 1019912 | tf_op jit(solution)/shard_map/ppermute | solution.py:400
  6.8 5.5 %collective-permute-start.1 = (bf16[8,64,128]{2,1,0:T(8,128)(2,1)S(1)}, bf16[8,64,128]{2,1,0:T(8,128)(2,1)S(1)}, u32[]{:S(2)}, u32[]{:S(2)}) collective-permute-start(bf16[8,64,128]{2,1,0:T(8,128)(2,1)S(1)} %get-tuple-element.47), channel_id=1, source_target_pairs={{0,3},{1,2},{2,1},{3,0},{4,7},{5,6},{6,5},{7,4},{8,11},{9,10},{10,... | collective-permute-start | bytes 393224 | tf_op jit(solution)/shard_map/ppermute | solution.py:400
  12.4 2.5 %collective-permute-start = (bf16[8,64,128]{2,1,0:T(8,128)(2,1)S(1)}, bf16[8,64,128]{2,1,0:T(8,128)(2,1)S(1)}, u32[]{:S(2)}, u32[]{:S(2)}) collective-permute-start(bf16[8,64,128]{2,1,0:T(8,128)(2,1)S(1)} %get-tuple-element.46.mine), channel_id=1, source_target_pairs={{0,2},{1,3},{2,0},{3,1},{4,6},{5,7},{6,4},{7,5},{8,10},{9,11},{10,... | collective-permute-start | bytes 393224 | tf_op jit(solution)/shard_map/ppermute | solution.py:400
  14.9 7.2 %collective-permute-done.1.far = bf16[8,64,128]{2,1,0:T(8,128)(2,1)S(1)} collective-permute-done((bf16[8,64,128]{2,1,0:T(8,128)(2,1)S(1)}, bf16[8,64,128]{2,1,0:T(8,128)(2,1)S(1)}, u32[]{:S(2)}, u32[]{:S(2)}) %collective-permute-start.1) | collective-permute-done | bytes 131104 | tf_op jit(solution)/shard_map/ppermute | solution.py:400
  22.2 3.6 %collective-permute-done.near = bf16[8,64,128]{2,1,0:T(8,128)(2,1)S(1)} collective-permute-done((bf16[8,64,128]{2,1,0:T(8,128)(2,1)S(1)}, bf16[8,64,128]{2,1,0:T(8,128)(2,1)S(1)}, u32[]{:S(2)}, u32[]{:S(2)}) %collective-permute-start) | collective-permute-done | bytes 131104 | tf_op jit(solution)/shard_map/ppermute | solution.py:400
  25.7 2.3 %shard_map.69.part = f32[1536,128]{1,0:T(8,128)S(1)} custom-call(s32[4]{0:T(128)S(1)} %pad_add_fusion.pos, f32[1536]{0:T(1024)S(1)} %reshape.32.tab, bf16[8,64,128]{2,1,0:T(8,128)(2,1)S(1)} %get-tuple-element.46.mine, bf16[8,64,128]{2,1,0:T(8,128)(2,1)S(1)} %collective-permute-done.near, bf16[8,64,128]{2,1,0:T(8,128)(2,1)S(1)} %collective-permute-done.1.far), custom_call_target="tpu_custom_call" | custom-call | flops 20000000 | bytes 1000000 | tf_op jit(solution)/shard_map/pallas_call | solution.py:32
  28.7 1.5 %shard_map.70 = (f32[1536,128]{1,0:T(8,128)S(1)}, f32[1536,128]{1,0:T(8,128)S(1)}, f32[2,16,128]{2,1,0:T(8,128)S(1)}, bf16[384,128]{1,0:T(8,128)(2,1)S(1)}, bf16...) custom-call(s32[4]{0:T(128)S(1)} %pad_add_fusion.pos, f32[1536]{0:T(1024)S(1)} %reshape.32.tab, ...), custom_call_target="tpu_custom_call" | custom-call | flops 5000000 | bytes 1000000 | tf_op jit(solution)/shard_map/pallas_call | solution.py:32
  30.2 2.7 %collective-permute-start.3 = (bf16[384,128]{1,0:T(8,128)(2,1)S(1)}, bf16[384,128]{1,0:T(8,128)(2,1)S(1)}, u32[]{:S(2)}, u32[]{:S(2)}) collective-permute-start(bf16[384,128]{1,0:T(8,128)(2,1)S(1)} %get-tuple-element.57), channel_id=1, source_target_pairs={{0,4},{4,0},{8,12},{12,8},{16,20},{20,16},{24,28},{28,24},{32,36},... | collective-permute-start | bytes 294920 | tf_op jit(solution)/shard_map/ppermute | solution.py:408
  32.9 11.2 %collective-permute-start.4 = (bf16[384,128]{1,0:T(8,128)(2,1)S(1)}, bf16[384,128]{1,0:T(8,128)(2,1)S(1)}, u32[]{:S(2)}, u32[]{:S(2)}) collective-permute-start(bf16[384,128]{1,0:T(8,128)(2,1)S(1)} %get-tuple-element.58), channel_id=1, source_target_pairs={{4,8},{8,4},{12,16},{16,12},{20,24},{24,20},{28,32},{32,28},{36,40... | collective-permute-start | bytes 294920 | tf_op jit(solution)/shard_map/ppermute | solution.py:406
  44.2 1.9 %collective-permute-start.5 = (bf16[384,128]{1,0:T(8,128)(2,1)S(1)}, bf16[384,128]{1,0:T(8,128)(2,1)S(1)}, u32[]{:S(2)}, u32[]{:S(2)}) collective-permute-start(bf16[384,128]{1,0:T(8,128)(2,1)S(1)} %get-tuple-element.59), channel_id=1, source_target_pairs={{0,1},{1,0},{49,48},{48,49},{96,97},{97,96},{145,144},{144,145},{1... | collective-permute-start | bytes 294920 | tf_op jit(solution)/shard_map/ppermute | solution.py:410
  46.1 1.9 %collective-permute-start.6 = (bf16[384,128]{1,0:T(8,128)(2,1)S(1)}, bf16[384,128]{1,0:T(8,128)(2,1)S(1)}, u32[]{:S(2)}, u32[]{:S(2)}) collective-permute-start(bf16[384,128]{1,0:T(8,128)(2,1)S(1)} %get-tuple-element.60), channel_id=1, source_target_pairs={{1,49},{49,1},{48,96},{96,48},{97,145},{145,97},{144,192},{192,144... | collective-permute-start | bytes 294920 | tf_op jit(solution)/shard_map/ppermute | solution.py:409
  48.0 2.2 %shard_map.71 = (f32[1536,128]{1,0:T(8,128)S(1)}, f32[1536,128]{1,0:T(8,128)S(1)}, f32[1536,128]{1,0:T(8,128)S(1)}, f32[1536,128]{1,0:T(8,128)S(1)}, f32[1536,12...) custom-call(s32[4]{0:T(128)S(1)} %pad_add_fusion.pos, f32[1536,128]{1,0:T(8,128)S(1)} %get-tuple-element.50.e, ...), custom_call_target="tpu_custom_call" | custom-call | flops 20000000 | bytes 1000000 | tf_op jit(solution)/shard_map/pallas_call | solution.py:32
  50.9 2.3 %collective-permute-done.6.h3 = bf16[384,128]{1,0:T(8,128)(2,1)S(1)} collective-permute-done((bf16[384,128]{1,0:T(8,128)(2,1)S(1)}, bf16[384,128]{1,0:T(8,128)(2,1)S(1)}, u32[]{:S(2)}, u32[]{:S(2)}) %collective-permute-start.6) | collective-permute-done | bytes 98336 | tf_op jit(solution)/shard_map/ppermute | solution.py:409
  54.6 3.9 %collective-permute-start.7 = (f32[128,128]{1,0:T(8,128)S(1)}, f32[128,128]{1,0:T(8,128)S(1)}, u32[]{:S(2)}, u32[]{:S(2)}) collective-permute-start(f32[128,128]{1,0:T(8,128)S(1)} %get-tuple-element.62.sums), channel_id=1, source_target_pairs={{0,2},{1,3},{2,0},{3,1},{4,6},{5,7},{6,4},{7,5},{8,10},{9,11},{10,... | collective-permute-start | bytes 196616 | tf_op jit(solution)/shard_map/ppermute | solution.py:400
  58.6 1.9 %collective-permute-start.8 = (bf16[192,128]{1,0:T(8,128)(2,1)S(1)}, bf16[192,128]{1,0:T(8,128)(2,1)S(1)}, u32[]{:S(2)}, u32[]{:S(2)}) collective-permute-start(bf16[192,128]{1,0:T(8,128)(2,1)S(1)} %get-tuple-element.69), channel_id=1, source_target_pairs={{0,4},{4,0},{8,12},{12,8},{16,20},{20,16},{24,28},{28,24},{32,36},... | collective-permute-start | bytes 147464 | tf_op jit(solution)/shard_map/ppermute | solution.py:408
  60.5 4.9 %collective-permute-start.9 = (bf16[192,128]{1,0:T(8,128)(2,1)S(1)}, bf16[192,128]{1,0:T(8,128)(2,1)S(1)}, u32[]{:S(2)}, u32[]{:S(2)}) collective-permute-start(bf16[192,128]{1,0:T(8,128)(2,1)S(1)} %get-tuple-element.70), channel_id=1, source_target_pairs={{4,8},{8,4},{12,16},{16,12},{20,24},{24,20},{28,32},{32,28},{36,40... | collective-permute-start | bytes 147464 | tf_op jit(solution)/shard_map/ppermute | solution.py:406
  65.4 4.8 %collective-permute-start.10 = (bf16[192,128]{1,0:T(8,128)(2,1)S(1)}, bf16[192,128]{1,0:T(8,128)(2,1)S(1)}, u32[]{:S(2)}, u32[]{:S(2)}) collective-permute-start(bf16[192,128]{1,0:T(8,128)(2,1)S(1)} %get-tuple-element.71), channel_id=1, source_target_pairs={{0,1},{1,0},{49,48},{48,49},{96,97},{97,96},{145,144},{144,145},{1... | collective-permute-start | bytes 147464 | tf_op jit(solution)/shard_map/ppermute | solution.py:410
  70.2 1.9 %collective-permute-start.11 = (bf16[192,128]{1,0:T(8,128)(2,1)S(1)}, bf16[192,128]{1,0:T(8,128)(2,1)S(1)}, u32[]{:S(2)}, u32[]{:S(2)}) collective-permute-start(bf16[192,128]{1,0:T(8,128)(2,1)S(1)} %get-tuple-element.72), channel_id=1, source_target_pairs={{1,49},{49,1},{48,96},{96,48},{97,145},{145,97},{144,192},{192,144... | collective-permute-start | bytes 147464 | tf_op jit(solution)/shard_map/ppermute | solution.py:409
  72.1 2.0 %shard_map.73 = (f32[1536,128]{1,0:T(8,128)S(1)}, f32[1536,128]{1,0:T(8,128)S(1)}) custom-call(s32[4]{0:T(128)S(1)} %pad_add_fusion.pos, f32[1536,128]{1,0:T(8,128)S(1)} %get-tuple-element.61.e, f32[1536,128]{1,0:T(8,128)S(1)} %get-tuple-element.64.up_c, f32[1536,128]{1,0:T(8,128)S(1)} %get-tuple-element.65.east_c, f32[1536,128]{1,0:T(8,128)S(1)} %get-tuple-element.66.above_c), custom_call_target="tpu_custom_call" | custom-call | flops 20000000 | bytes 1000000 | tf_op jit(solution)/shard_map/pallas_call | solution.py:32
  74.1 2.7 %collective-permute-done.11.h3 = bf16[192,128]{1,0:T(8,128)(2,1)S(1)} collective-permute-done((bf16[192,128]{1,0:T(8,128)(2,1)S(1)}, bf16[192,128]{1,0:T(8,128)(2,1)S(1)}, u32[]{:S(2)}, u32[]{:S(2)}) %collective-permute-start.11) | collective-permute-done | bytes 49184 | tf_op jit(solution)/shard_map/ppermute | solution.py:409
  78.1 1.9 %collective-permute-start.13 = (bf16[192,128]{1,0:T(8,128)(2,1)S(1)}, bf16[192,128]{1,0:T(8,128)(2,1)S(1)}, u32[]{:S(2)}, u32[]{:S(2)}) collective-permute-start(bf16[192,128]{1,0:T(8,128)(2,1)S(1)} %get-tuple-element.79), channel_id=1, source_target_pairs={{0,4},{4,0},{8,12},{12,8},{16,20},{20,16},{24,28},{28,24},{32,36},... | collective-permute-start | bytes 147464 | tf_op jit(solution)/shard_map/ppermute | solution.py:408
  80.0 5.2 %collective-permute-start.14 = (bf16[192,128]{1,0:T(8,128)(2,1)S(1)}, bf16[192,128]{1,0:T(8,128)(2,1)S(1)}, u32[]{:S(2)}, u32[]{:S(2)}) collective-permute-start(bf16[192,128]{1,0:T(8,128)(2,1)S(1)} %get-tuple-element.80), channel_id=1, source_target_pairs={{4,8},{8,4},{12,16},{16,12},{20,24},{24,20},{28,32},{32,28},{36,40... | collective-permute-start | bytes 147464 | tf_op jit(solution)/shard_map/ppermute | solution.py:406
  85.3 1.9 %collective-permute-start.15 = (bf16[192,128]{1,0:T(8,128)(2,1)S(1)}, bf16[192,128]{1,0:T(8,128)(2,1)S(1)}, u32[]{:S(2)}, u32[]{:S(2)}) collective-permute-start(bf16[192,128]{1,0:T(8,128)(2,1)S(1)} %get-tuple-element.81), channel_id=1, source_target_pairs={{0,1},{1,0},{49,48},{48,49},{96,97},{97,96},{145,144},{144,145},{1... | collective-permute-start | bytes 147464 | tf_op jit(solution)/shard_map/ppermute | solution.py:410
  87.2 1.9 %collective-permute-start.16 = (bf16[192,128]{1,0:T(8,128)(2,1)S(1)}, bf16[192,128]{1,0:T(8,128)(2,1)S(1)}, u32[]{:S(2)}, u32[]{:S(2)}) collective-permute-start(bf16[192,128]{1,0:T(8,128)(2,1)S(1)} %get-tuple-element.82), channel_id=1, source_target_pairs={{1,49},{49,1},{48,96},{96,48},{97,145},{145,97},{144,192},{192,144... | collective-permute-start | bytes 147464 | tf_op jit(solution)/shard_map/ppermute | solution.py:409
  89.1 3.2 %collective-permute-start.12 = (f32[64,128]{1,0:T(8,128)S(1)}, f32[64,128]{1,0:T(8,128)S(1)}, u32[]{:S(2)}, u32[]{:S(2)}) collective-permute-start(f32[64,128]{1,0:T(8,128)S(1)} %get-tuple-element.76.part), channel_id=1, source_target_pairs={{0,2},{1,3},{2,0},{3,1},{4,6},{5,7},{6,4},{7,5},{8,10},{9,11},{10,... | collective-permute-start | bytes 98312 | tf_op jit(solution)/shard_map/ppermute | solution.py:400
  92.3 2.0 %shard_map.75 = (f32[1536,128]{1,0:T(8,128)S(1)}, f32[1536,128]{1,0:T(8,128)S(1)}) custom-call(s32[4]{0:T(128)S(1)} %pad_add_fusion.pos, f32[1536,128]{1,0:T(8,128)S(1)} %get-tuple-element.73.e, f32[1536,128]{1,0:T(8,128)S(1)} %get-tuple-element.64.up_c, f32[1536,128]{1,0:T(8,128)S(1)} %get-tuple-element.65.east_c, f32[1536,128]{1,0:T(8,128)S(1)} %get-tuple-element.66.above_c), custom_call_target="tpu_custom_call" | custom-call | flops 20000000 | bytes 1000000 | tf_op jit(solution)/shard_map/pallas_call | solution.py:32
  97.3 3.9 %collective-permute-start.17 = (f32[12,64,128]{2,1,0:T(8,128)S(1)}, f32[12,64,128]{2,1,0:T(8,128)S(1)}, u32[]{:S(2)}, u32[]{:S(2)}) collective-permute-start(f32[12,64,128]{2,1,0:T(8,128)S(1)} %get-tuple-element.83), channel_id=1, source_target_pairs={{0,1},{1,0},{2,3},{3,2},{4,5},{5,4},{6,7},{7,6},{8,9},{9,8},{10,11... | collective-permute-start | bytes 1179656 | tf_op jit(solution)/shard_map/ppermute | solution.py:400
  101.2 3.4 %collective-permute-start.18 = (f32[64,128]{1,0:T(8,128)S(1)}, f32[64,128]{1,0:T(8,128)S(1)}, u32[]{:S(2)}, u32[]{:S(2)}) collective-permute-start(f32[64,128]{1,0:T(8,128)S(1)} %get-tuple-element.84.ksum), channel_id=1, source_target_pairs={{0,2},{1,3},{2,0},{3,1},{4,6},{5,7},{6,4},{7,5},{8,10},{9,11},{10,... | collective-permute-start | bytes 98312 | tf_op jit(solution)/shard_map/ppermute | solution.py:400
  104.6 5.2 %collective-permute-done.18.got = f32[64,128]{1,0:T(8,128)S(1)} collective-permute-done((f32[64,128]{1,0:T(8,128)S(1)}, f32[64,128]{1,0:T(8,128)S(1)}, u32[]{:S(2)}, u32[]{:S(2)}) %collective-permute-start.18) | collective-permute-done | bytes 32800 | tf_op jit(solution)/shard_map/ppermute | solution.py:400
  109.8 4.7 %collective-permute-start.19 = (f32[64,128]{1,0:T(8,128)S(1)}, f32[64,128]{1,0:T(8,128)S(1)}, u32[]{:S(2)}, u32[]{:S(2)}) collective-permute-start(f32[64,128]{1,0:T(8,128)S(1)} %shard_map.77.mine), channel_id=1, source_target_pairs={{0,1},{1,0},{2,3},{3,2},{4,5},{5,4},{6,7},{7,6},{8,9},{9,8},{10,11... | collective-permute-start | bytes 98312 | tf_op jit(solution)/shard_map/ppermute | solution.py:400
  116.3 1.9 %join.1 = (f32[12,128,128]{2,1,0:T(8,128)}, f32[128,128]{1,0:T(8,128)}) custom-call(s32[4]{0:T(128)S(1)} %pad_add_fusion.pos, f32[12,64,128]{2,1,0:T(8,128)S(1)} %collective-permute-done.17.pair, f32[64,128]{1,0:T(8,128)S(1)} %shard_map.77.mine, f32[64,128]{1,0:T(8,128)S(1)} %collective-permute-done.19.other, ...), custom_call_target="tpu_custom_call", output_to_operand_aliasing={{0}: (4, {})} | custom-call | tf_op jit(solution)/shard_map/join/pallas_call | solution.py:489
  (28 shorter events, 9.1 us)
Async XLA Ops:
  0.7 14.1 %copy-start.2 = (bf16[32,48]{1,0:T(8,128)(2,1)S(1)}, bf16[32,48]{1,0:T(8,128)(2,1)}, u32[]{:S(2)}) copy-start(bf16[32,48]{1,0:T(8,128)(2,1)} %param.6) | copy-start | bytes 9220
  2.5 25.5 %collective-permute-start.2 = (bf16[1328,128]{1,0:T(8,128)(2,1)S(1)}, bf16[1328,128]{1,0:T(8,128)(2,1)S(1)}, u32[]{:S(2)}, u32[]{:S(2)}) collective-permute-start(bf16[1328,128]{1,0:T(8,128)(2,1)S(1)} %get-tuple-element.49), channel_id=1, source_target_pairs={{0,1},{1,0},{2,3},{3,2},{4,5},{5,4},{6,7},{7,6},{8,9},{9,8},{10,11... | collective-permute-start | bytes 1019912 | tf_op jit(solution)/shard_map/ppermute | solution.py:400
  6.8 15.3 %collective-permute-start.1 = (bf16[8,64,128]{2,1,0:T(8,128)(2,1)S(1)}, bf16[8,64,128]{2,1,0:T(8,128)(2,1)S(1)}, u32[]{:S(2)}, u32[]{:S(2)}) collective-permute-start(bf16[8,64,128]{2,1,0:T(8,128)(2,1)S(1)} %get-tuple-element.47), channel_id=1, source_target_pairs={{0,3},{1,2},{2,1},{3,0},{4,7},{5,6},{6,5},{7,4},{8,11},{9,10},{10,... | collective-permute-start | bytes 393224 | tf_op jit(solution)/shard_map/ppermute | solution.py:400
  12.4 13.4 %collective-permute-start = (bf16[8,64,128]{2,1,0:T(8,128)(2,1)S(1)}, bf16[8,64,128]{2,1,0:T(8,128)(2,1)S(1)}, u32[]{:S(2)}, u32[]{:S(2)}) collective-permute-start(bf16[8,64,128]{2,1,0:T(8,128)(2,1)S(1)} %get-tuple-element.46.mine), channel_id=1, source_target_pairs={{0,2},{1,3},{2,0},{3,1},{4,6},{5,7},{6,4},{7,5},{8,10},{9,11},{10,... | collective-permute-start | bytes 393224 | tf_op jit(solution)/shard_map/ppermute | solution.py:400
  28.0 0.7 copy-start.1
  30.2 20.0 %collective-permute-start.3 = (bf16[384,128]{1,0:T(8,128)(2,1)S(1)}, bf16[384,128]{1,0:T(8,128)(2,1)S(1)}, u32[]{:S(2)}, u32[]{:S(2)}) collective-permute-start(bf16[384,128]{1,0:T(8,128)(2,1)S(1)} %get-tuple-element.57), channel_id=1, source_target_pairs={{0,4},{4,0},{8,12},{12,8},{16,20},{20,16},{24,28},{28,24},{32,36},... | collective-permute-start | bytes 294920 | tf_op jit(solution)/shard_map/ppermute | solution.py:408
  32.9 18.0 %collective-permute-start.4 = (bf16[384,128]{1,0:T(8,128)(2,1)S(1)}, bf16[384,128]{1,0:T(8,128)(2,1)S(1)}, u32[]{:S(2)}, u32[]{:S(2)}) collective-permute-start(bf16[384,128]{1,0:T(8,128)(2,1)S(1)} %get-tuple-element.58), channel_id=1, source_target_pairs={{4,8},{8,4},{12,16},{16,12},{20,24},{24,20},{28,32},{32,28},{36,40... | collective-permute-start | bytes 294920 | tf_op jit(solution)/shard_map/ppermute | solution.py:406
  44.2 6.8 %collective-permute-start.5 = (bf16[384,128]{1,0:T(8,128)(2,1)S(1)}, bf16[384,128]{1,0:T(8,128)(2,1)S(1)}, u32[]{:S(2)}, u32[]{:S(2)}) collective-permute-start(bf16[384,128]{1,0:T(8,128)(2,1)S(1)} %get-tuple-element.59), channel_id=1, source_target_pairs={{0,1},{1,0},{49,48},{48,49},{96,97},{97,96},{145,144},{144,145},{1... | collective-permute-start | bytes 294920 | tf_op jit(solution)/shard_map/ppermute | solution.py:410
  46.1 7.1 %collective-permute-start.6 = (bf16[384,128]{1,0:T(8,128)(2,1)S(1)}, bf16[384,128]{1,0:T(8,128)(2,1)S(1)}, u32[]{:S(2)}, u32[]{:S(2)}) collective-permute-start(bf16[384,128]{1,0:T(8,128)(2,1)S(1)} %get-tuple-element.60), channel_id=1, source_target_pairs={{1,49},{49,1},{48,96},{96,48},{97,145},{145,97},{144,192},{192,144... | collective-permute-start | bytes 294920 | tf_op jit(solution)/shard_map/ppermute | solution.py:409
  48.0 5.2 %copy-start = (f32[16,8,128]{2,1,0:T(8,128)S(1)}, f32[16,8,128]{2,1,0:T(8,128)}, u32[]{:S(2)}) copy-start(f32[16,8,128]{2,1,0:T(8,128)} %param.9) | copy-start | bytes 196612
  54.6 22.1 %collective-permute-start.7 = (f32[128,128]{1,0:T(8,128)S(1)}, f32[128,128]{1,0:T(8,128)S(1)}, u32[]{:S(2)}, u32[]{:S(2)}) collective-permute-start(f32[128,128]{1,0:T(8,128)S(1)} %get-tuple-element.62.sums), channel_id=1, source_target_pairs={{0,2},{1,3},{2,0},{3,1},{4,6},{5,7},{6,4},{7,5},{8,10},{9,11},{10,... | collective-permute-start | bytes 196616 | tf_op jit(solution)/shard_map/ppermute | solution.py:400
  58.6 15.5 %collective-permute-start.8 = (bf16[192,128]{1,0:T(8,128)(2,1)S(1)}, bf16[192,128]{1,0:T(8,128)(2,1)S(1)}, u32[]{:S(2)}, u32[]{:S(2)}) collective-permute-start(bf16[192,128]{1,0:T(8,128)(2,1)S(1)} %get-tuple-element.69), channel_id=1, source_target_pairs={{0,4},{4,0},{8,12},{12,8},{16,20},{20,16},{24,28},{28,24},{32,36},... | collective-permute-start | bytes 147464 | tf_op jit(solution)/shard_map/ppermute | solution.py:408
  60.5 13.6 %collective-permute-start.9 = (bf16[192,128]{1,0:T(8,128)(2,1)S(1)}, bf16[192,128]{1,0:T(8,128)(2,1)S(1)}, u32[]{:S(2)}, u32[]{:S(2)}) collective-permute-start(bf16[192,128]{1,0:T(8,128)(2,1)S(1)} %get-tuple-element.70), channel_id=1, source_target_pairs={{4,8},{8,4},{12,16},{16,12},{20,24},{24,20},{28,32},{32,28},{36,40... | collective-permute-start | bytes 147464 | tf_op jit(solution)/shard_map/ppermute | solution.py:406
  65.4 8.7 %collective-permute-start.10 = (bf16[192,128]{1,0:T(8,128)(2,1)S(1)}, bf16[192,128]{1,0:T(8,128)(2,1)S(1)}, u32[]{:S(2)}, u32[]{:S(2)}) collective-permute-start(bf16[192,128]{1,0:T(8,128)(2,1)S(1)} %get-tuple-element.71), channel_id=1, source_target_pairs={{0,1},{1,0},{49,48},{48,49},{96,97},{97,96},{145,144},{144,145},{1... | collective-permute-start | bytes 147464 | tf_op jit(solution)/shard_map/ppermute | solution.py:410
  70.2 6.6 %collective-permute-start.11 = (bf16[192,128]{1,0:T(8,128)(2,1)S(1)}, bf16[192,128]{1,0:T(8,128)(2,1)S(1)}, u32[]{:S(2)}, u32[]{:S(2)}) collective-permute-start(bf16[192,128]{1,0:T(8,128)(2,1)S(1)} %get-tuple-element.72), channel_id=1, source_target_pairs={{1,49},{49,1},{48,96},{96,48},{97,145},{145,97},{144,192},{192,144... | collective-permute-start | bytes 147464 | tf_op jit(solution)/shard_map/ppermute | solution.py:409
  78.1 17.7 %collective-permute-start.13 = (bf16[192,128]{1,0:T(8,128)(2,1)S(1)}, bf16[192,128]{1,0:T(8,128)(2,1)S(1)}, u32[]{:S(2)}, u32[]{:S(2)}) collective-permute-start(bf16[192,128]{1,0:T(8,128)(2,1)S(1)} %get-tuple-element.79), channel_id=1, source_target_pairs={{0,4},{4,0},{8,12},{12,8},{16,20},{20,16},{24,28},{28,24},{32,36},... | collective-permute-start | bytes 147464 | tf_op jit(solution)/shard_map/ppermute | solution.py:408
  80.0 15.8 %collective-permute-start.14 = (bf16[192,128]{1,0:T(8,128)(2,1)S(1)}, bf16[192,128]{1,0:T(8,128)(2,1)S(1)}, u32[]{:S(2)}, u32[]{:S(2)}) collective-permute-start(bf16[192,128]{1,0:T(8,128)(2,1)S(1)} %get-tuple-element.80), channel_id=1, source_target_pairs={{4,8},{8,4},{12,16},{16,12},{20,24},{24,20},{28,32},{32,28},{36,40... | collective-permute-start | bytes 147464 | tf_op jit(solution)/shard_map/ppermute | solution.py:406
  85.3 10.6 %collective-permute-start.15 = (bf16[192,128]{1,0:T(8,128)(2,1)S(1)}, bf16[192,128]{1,0:T(8,128)(2,1)S(1)}, u32[]{:S(2)}, u32[]{:S(2)}) collective-permute-start(bf16[192,128]{1,0:T(8,128)(2,1)S(1)} %get-tuple-element.81), channel_id=1, source_target_pairs={{0,1},{1,0},{49,48},{48,49},{96,97},{97,96},{145,144},{144,145},{1... | collective-permute-start | bytes 147464 | tf_op jit(solution)/shard_map/ppermute | solution.py:410
  87.2 8.7 %collective-permute-start.16 = (bf16[192,128]{1,0:T(8,128)(2,1)S(1)}, bf16[192,128]{1,0:T(8,128)(2,1)S(1)}, u32[]{:S(2)}, u32[]{:S(2)}) collective-permute-start(bf16[192,128]{1,0:T(8,128)(2,1)S(1)} %get-tuple-element.82), channel_id=1, source_target_pairs={{1,49},{49,1},{48,96},{96,48},{97,145},{145,97},{144,192},{192,144... | collective-permute-start | bytes 147464 | tf_op jit(solution)/shard_map/ppermute | solution.py:409
  89.1 6.7 %collective-permute-start.12 = (f32[64,128]{1,0:T(8,128)S(1)}, f32[64,128]{1,0:T(8,128)S(1)}, u32[]{:S(2)}, u32[]{:S(2)}) collective-permute-start(f32[64,128]{1,0:T(8,128)S(1)} %get-tuple-element.76.part), channel_id=1, source_target_pairs={{0,2},{1,3},{2,0},{3,1},{4,6},{5,7},{6,4},{7,5},{8,10},{9,11},{10,... | collective-permute-start | bytes 98312 | tf_op jit(solution)/shard_map/ppermute | solution.py:400
  97.3 19.1 %collective-permute-start.17 = (f32[12,64,128]{2,1,0:T(8,128)S(1)}, f32[12,64,128]{2,1,0:T(8,128)S(1)}, u32[]{:S(2)}, u32[]{:S(2)}) collective-permute-start(f32[12,64,128]{2,1,0:T(8,128)S(1)} %get-tuple-element.83), channel_id=1, source_target_pairs={{0,1},{1,0},{2,3},{3,2},{4,5},{5,4},{6,7},{7,6},{8,9},{9,8},{10,11... | collective-permute-start | bytes 1179656 | tf_op jit(solution)/shard_map/ppermute | solution.py:400
  101.2 8.6 %collective-permute-start.18 = (f32[64,128]{1,0:T(8,128)S(1)}, f32[64,128]{1,0:T(8,128)S(1)}, u32[]{:S(2)}, u32[]{:S(2)}) collective-permute-start(f32[64,128]{1,0:T(8,128)S(1)} %get-tuple-element.84.ksum), channel_id=1, source_target_pairs={{0,2},{1,3},{2,0},{3,1},{4,6},{5,7},{6,4},{7,5},{8,10},{9,11},{10,... | collective-permute-start | bytes 98312 | tf_op jit(solution)/shard_map/ppermute | solution.py:400
  109.8 6.6 %collective-permute-start.19 = (f32[64,128]{1,0:T(8,128)S(1)}, f32[64,128]{1,0:T(8,128)S(1)}, u32[]{:S(2)}, u32[]{:S(2)}) collective-permute-start(f32[64,128]{1,0:T(8,128)S(1)} %shard_map.77.mine), channel_id=1, source_target_pairs={{0,1},{1,0},{2,3},{3,2},{4,5},{5,4},{6,7},{7,6},{8,9},{9,8},{10,11... | collective-permute-start | bytes 98312 | tf_op jit(solution)/shard_map/ppermute | solution.py:400

commit v2 on v1

--- a/solution.py
+++ b/solution.py
@@ -59,26 +59,23 @@
 COEF = 0.75 / SCALE
 
 
+def half_rows(half):
+    return pl.ds(pl.multiple_of(N * half, N), N)
+
+
 def pack_kernel(pos, planck, dust, eold, eown, pair, near, far, stage, shares, sems):
     half = pos[0]
-    mine = pl.ds(pl.multiple_of(N * half, N), N)
-    other = pl.ds(pl.multiple_of(N * (1 - half), N), N)
-    copies = [
-        pltpu.make_async_copy(dust.at[:, other, :], far, sems.at[0]),
-        pltpu.make_async_copy(eold.at[:, other, :], stage, sems.at[1]),
-        pltpu.make_async_copy(dust.at[:, mine, :], near, sems.at[2]),
-        pltpu.make_async_copy(eold.at[:, mine, :], eown, sems.at[3]),
-        pltpu.make_async_copy(planck, shares, sems.at[4]),
+    mine, other = half_rows(half), half_rows(1 - half)
+    give = [pltpu.make_async_copy(eold.at[g, other, :], stage.at[g], sems.at[g]) for g in range(OWN)]
+    away = [pltpu.make_async_copy(dust.at[b, other, :], far.at[b], sems.at[OWN + b]) for b in range(BINS)]
+    shared = pltpu.make_async_copy(planck, shares, sems.at[OWN + BINS])
+    rest = [
+        pltpu.make_async_copy(dust.at[:, mine, :], near, sems.at[OWN + BINS + 1]),
+        pltpu.make_async_copy(eold.at[:, mine, :], eown, sems.at[OWN + BINS + 2]),
     ]
-    for copy in copies:
+    for copy in [shared] + away + give + rest:
         copy.start()
-    copies[0].wait()
-    for b in range(BINS):
-        pair[pl.ds(b * N, N), :] = far[b]
-    copies[1].wait()
-    for g in range(OWN):
-        pair[pl.ds(SIZE + g * N, N), :] = stage[g].astype(BF)
-    copies[4].wait()
+    shared.wait()
     row = lax.broadcasted_iota(jnp.int32, (2 * LAT, LANES), 0)
     share = jnp.zeros((2 * LAT, LANES), F32)
     for g in range(OWN):
@@ -87,8 +84,14 @@
         piece = share.astype(BF)
         pair[pl.ds(SIZE + PART + 2 * i * LAT, 2 * LAT), :] = piece
         share = share - piece.astype(F32)
-    copies[2].wait()
-    copies[3].wait()
+    for b in range(BINS):
+        away[b].wait()
+        pair[pl.ds(b * N, N), :] = far[b]
+    for g in range(OWN):
+        give[g].wait()
+        pair[pl.ds(SIZE + g * N, N), :] = stage[g].astype(BF)
+    for copy in rest:
+        copy.wait()
 
 
 def write_slabs(pos, src, at, t1, t2, r1, r2):
@@ -129,39 +132,24 @@
     return acc
 
 
-def early_kernel(pos, tab, mine, near, far, kap, wide):
+def early_kernel(pos, tab, planck, mine, pair, near, eown, kap, e, share, wide):
     place = pos[2]
-    for j, block in enumerate((mine, near, far)):
-        for b in range(BINS):
-            wide[pl.ds(j * SIZE + b * N, N), :] = block[b].astype(F32)
+    slot = place % 2
+    for b in range(BINS):
+        wide[pl.ds(b * N, N), :] = mine[b].astype(F32)
+        wide[pl.ds(SIZE + b * N, N), :] = pair[pl.ds(b * N, N), :].astype(F32)
+        wide[pl.ds(2 * SIZE + b * N, N), :] = near[b].astype(F32)
 
     def one(g, carry):
-        acc = gather_bins(tab, wide, place, (0, 2, 3), g, [None] * ROWS)
+        acc = gather_bins(tab, wide, place, (0, 1, 2), g, [None] * ROWS)
         for r in range(ROWS):
             kap[tile(g * ROWS + r), :] = acc[r]
         return carry
 
     lax.fori_loop(0, GROUPS, one, 0, unroll=2)
-
-
-def late_kernel(pos, tab, planck, part, eown, pair, kap, e, share, t1, t2, r1, r2, wide):
-    place = pos[2]
-    slot = place % 2
-    wide[...] = pair[pl.ds(0, SIZE), :].astype(F32)
-
-    def one(g, carry):
-        acc = [part[tile(g * ROWS + r), :] for r in range(ROWS)]
-        acc = gather_bins(tab, wide, place, (1,), g, acc)
-        for r in range(ROWS):
-            kap[tile(g * ROWS + r), :] = acc[r]
-        return carry
-
-    lax.fori_loop(0, GROUPS, one, 0, unroll=2)
-    theirs = pl.multiple_of((1 - slot) * PART, PART)
-    mine = pl.multiple_of(slot * PART, PART)
     for g in range(OWN):
-        e[pl.ds(mine + g * N, N), :] = eown[g]
-    e[pl.ds(theirs, PART), :] = pair[pl.ds(SIZE, PART), :].astype(F32)
+        e[half_rows(slot * OWN + g), :] = eown[g]
+        e[half_rows((1 - slot) * OWN + g), :] = pair[pl.ds(SIZE + g * N, N), :].astype(F32)
     at = SIZE + PART
     pieces = [pair[pl.ds(at + 2 * LAT * i, 2 * LAT), :].astype(F32) for i in range(3)]
     row = lax.broadcasted_iota(jnp.int32, (2 * LAT, LANES), 0)
@@ -170,6 +158,21 @@
         ours = jnp.where(row == g, planck[g], ours)
     share[slot] = ours
     share[1 - slot] = pieces[0] + pieces[1] + pieces[2]
+
+
+def late_kernel(pos, tab, part, far, e, kap, t1, t2, r1, r2, wide):
+    place = pos[2]
+    for b in range(BINS):
+        wide[pl.ds(b * N, N), :] = far[b].astype(F32)
+
+    def one(g, carry):
+        acc = [part[tile(g * ROWS + r), :] for r in range(ROWS)]
+        acc = gather_bins(tab, wide, place, (3,), g, acc)
+        for r in range(ROWS):
+            kap[tile(g * ROWS + r), :] = acc[r]
+        return carry
+
+    lax.fori_loop(0, GROUPS, one, 0, unroll=4)
     write_slabs(pos, e, 0, t1, t2, r1, r2)
     write_slabs(pos, kap, TILES, t1, t2, r1, r2)
 
@@ -360,23 +363,25 @@
     temp[...] = (up[...] + (ksum[...] + got[...]) / SCALE) / down[...]
 
 
-def half_rows(half):
-    return pl.ds(pl.multiple_of(N * half, N), N)
-
-
-def own_kernel(pos, eown, energy, sem):
-    copy = pltpu.make_async_copy(eown, energy.at[:, half_rows(pos[0]), :], sem)
-    copy.start()
-    copy.wait()
-
-
-def join_kernel(pos, pair, mine, other, held_energy, energy, temp, sem):
+def put(src, energy, half, sems):
+    copies = [pltpu.make_async_copy(src.at[g], energy.at[g, half_rows(half), :], sems.at[g]) for g in range(OWN)]
+    for copy in copies:
+        copy.start()
+    return copies
+
+
+def own_kernel(pos, eown, energy, sems):
+    for copy in put(eown, energy, pos[0], sems):
+        copy.wait()
+
+
+def join_kernel(pos, pair, mine, other, held_energy, energy, temp, sems):
     half = pos[0]
-    copy = pltpu.make_async_copy(pair, energy.at[:, half_rows(1 - half), :], sem)
-    copy.start()
+    copies = put(pair, energy, 1 - half, sems)
     temp[half_rows(half), :] = mine[...]
     temp[half_rows(1 - half), :] = other[...]
-    copy.wait()
+    for copy in copies:
+        copy.wait()
 
 
 def theta_pairs(count, odd):
@@ -429,22 +434,24 @@
         pack_kernel,
         [held((OWN, N, LANES)), held((SIZE + PART + 6 * LAT, LANES), BF), block, block],
         (pos, *(pltpu.with_memory_space_constraint(x, pltpu.HBM) for x in (planck, dust, energy_old))), smem=1, space=pl.ANY,
-        scratch=[VMEM((OWN, N, LANES), F32), SMEM(planck.shape, F32), pltpu.SemaphoreType.DMA((5,))],
-    )
+        scratch=[VMEM((OWN, N, LANES), F32), SMEM(planck.shape, F32), pltpu.SemaphoreType.DMA((OWN + BINS + 3,))],
+    )
+    pair = xor(pair, 1)
+    near = xor(mine, 2)
     far = xor(far, 3)
-    near = xor(mine, 2)
-    pair = xor(pair, 1)
-    early, = call(
-        early_kernel, [full], (pos, tab, keep(mine), keep(near), keep(far)), smem=2,
+    early, e, share = call(
+        early_kernel, [full, full, held((2, 2 * LAT, LANES))],
+        (pos, tab, planck, keep(mine), keep(pair), keep(near), keep(eown)), smem=3,
         scratch=[VMEM((3 * SIZE, LANES), F32)], flops=20_000_000,
     )
-    kap, e, share, *both = call(
+    e = keep(e)
+    kap, *both = call(
         late_kernel,
-        [full, full, held((2, 2 * LAT, LANES))] + [held((2 * TILES, LANES), BF)] * 4,
-        (pos, tab, planck, keep(early), keep(eown), keep(pair)), smem=3,
+        [full] + [held((2 * TILES, LANES), BF)] * 4,
+        (pos, tab, keep(early), keep(far), e), smem=2,
         scratch=[VMEM((SIZE, LANES), F32)], flops=5_000_000,
     )
-    kap, share, e = keep(kap), keep(share), keep(e)
+    kap, share = keep(kap), keep(share)
     halos, _ = swap_halos(both)
     flux, weight, *coefs, e01, ssum = call(
         inner_first, [full] * 6 + [sheet], (pos, e, kap, share), smem=1, flops=20_000_000,
@@ -473,8 +480,8 @@
         scratch=scratch + [VMEM((CELLS, LANES), F32)], flops=5_000_000,
     )
     whole = pltpu.HBM((OWN, 2 * N, LANES), F32)
+    got = xor(part, 2)
     pair = xor(send, 1)
-    got = xor(part, 2)
     mine, = call(finish_kernel, [sheet], [keep(x) for x in (part, got, up, down)])
     other = xor(mine, 1)
     energy = pl.pallas_call(
@@ -482,7 +489,7 @@
         out_shape=whole,
         in_specs=[pl.BlockSpec(memory_space=SMEM), pl.BlockSpec(memory_space=VMEM)],
         out_specs=pl.BlockSpec(memory_space=pl.ANY),
-        scratch_shapes=[pltpu.SemaphoreType.DMA],
+        scratch_shapes=[pltpu.SemaphoreType.DMA((OWN,))],
         compiler_params=pltpu.CompilerParams(vmem_limit_bytes=16 << 20),
         name="own",
     )(pos, keep(eown))
@@ -491,7 +498,7 @@
         out_shape=[whole, jax.ShapeDtypeStruct((2 * N, LANES), F32)],
         in_specs=[pl.BlockSpec(memory_space=SMEM)] + [pl.BlockSpec(memory_space=VMEM)] * 3 + [pl.BlockSpec(memory_space=pl.ANY)],
         out_specs=[pl.BlockSpec(memory_space=pl.ANY), pl.BlockSpec(memory_space=VMEM)],
-        scratch_shapes=[pltpu.SemaphoreType.DMA],
+        scratch_shapes=[pltpu.SemaphoreType.DMA((OWN,))],
         input_output_aliases={4: 0},
         compiler_params=pltpu.CompilerParams(vmem_limit_bytes=16 << 20),
         name="join",

time: 119 us -> 116 us (0.975)
  the two profiles are of different devices: /device:TPU:38 before, /device:TPU:30 now
where the time goes in v2:
time: 116 us; the launch traced here: 115 us
  starting transfers between devices  74.4 us (64%)
  waiting for transfers between devices  20.3 us (18%)
  Pallas kernels  19.5 us (17%)
    ppermute x8, starting transfers between devices, xor(): return lax.ppermute(x, 'group', [(i, i ^ k) for i in range(4)])  30.9 us
    ppermute x3, starting transfers between devices, swap_halos(): t2 = lax.ppermute(t2, 'theta', theta_pairs(nt, 1))  21.8 us
    ppermute x8, waiting for transfers between devices, xor(): return lax.ppermute(x, 'group', [(i, i ^ k) for i in range(4)])  17 us
    pallas_call x10, Pallas kernels, call(): pl.pallas_call(kernel, out_shape=outs, in_specs=specs, out_specs=[pl.Bloc...  16.1 us
    ppermute x3, starting transfers between devices, swap_halos(): r1 = lax.ppermute(r1, ('row', 'group'), row_pairs(nr, 0))  9.38 us
    ppermute x3, starting transfers between devices, swap_halos(): t1 = lax.ppermute(t1, 'theta', theta_pairs(nt, 0))  6.57 us
    ppermute x3, starting transfers between devices, swap_halos(): r2 = lax.ppermute(r2, ('row', 'group'), row_pairs(nr, 1))  5.76 us
    ppermute x3, waiting for transfers between devices, swap_halos(): r2 = lax.ppermute(r2, ('row', 'group'), row_pairs(nr, 1))  3.2 us
  transfers between devices with their start and end apart: 20, of which 8 were waited for; matrix products, arithmetic and copies ran while one was open for 0% of the time, Pallas kernels for 9%

profile of v2, /device:TPU:30, one launch (start us, length us, event | category | flops | bytes accessed | tf_op | source)
XLA Modules:
  0.0 115.3 jit_solution(6846420285309126028)
XLA Ops:
  0.7 2.1 %shard_map.68 = (f32[12,64,128]{2,1,0:T(8,128)S(1)}, bf16[1328,128]{1,0:T(8,128)(2,1)S(1)}, bf16[8,64,128]{2,1,0:T(8,128)(2,1)S(1)}, bf16[8,64,128]{2,1,0:T(8,128)(2,1)S(1)}) custom-call(s32[4]{0:T(128)S(1)} %pad_add_fusion.pos, f32[12]{0:T(128)} %planck.3, bf16[8,128,128]{2,1,0:T(8,128)(2,1)} %bitcast.14, f32[12,128,128]{2,1,0:T(8,128)} %bitcast.13), custom_call_target="tpu_custom_call" | custom-call | flops 1000000 | bytes 1000000 | tf_op jit(solution)/shard_map/pallas_call | solution.py:32
  2.8 4.3 %collective-permute-start = (bf16[1328,128]{1,0:T(8,128)(2,1)S(1)}, bf16[1328,128]{1,0:T(8,128)(2,1)S(1)}, u32[]{:S(2)}, u32[]{:S(2)}) collective-permute-start(bf16[1328,128]{1,0:T(8,128)(2,1)S(1)} %get-tuple-element.48), channel_id=1, source_target_pairs={{0,1},{1,0},{2,3},{3,2},{4,5},{5,4},{6,7},{7,6},{8,9},{9,8},{10,11... | collective-permute-start | bytes 1019912 | tf_op jit(solution)/shard_map/ppermute | solution.py:405
  7.1 6.1 %collective-permute-start.1 = (bf16[8,64,128]{2,1,0:T(8,128)(2,1)S(1)}, bf16[8,64,128]{2,1,0:T(8,128)(2,1)S(1)}, u32[]{:S(2)}, u32[]{:S(2)}) collective-permute-start(bf16[8,64,128]{2,1,0:T(8,128)(2,1)S(1)} %get-tuple-element.47.mine), channel_id=1, source_target_pairs={{0,2},{1,3},{2,0},{3,1},{4,6},{5,7},{6,4},{7,5},{8,10},{9,11},{10,... | collective-permute-start | bytes 393224 | tf_op jit(solution)/shard_map/ppermute | solution.py:405
  13.2 1.9 %collective-permute-start.2 = (bf16[8,64,128]{2,1,0:T(8,128)(2,1)S(1)}, bf16[8,64,128]{2,1,0:T(8,128)(2,1)S(1)}, u32[]{:S(2)}, u32[]{:S(2)}) collective-permute-start(bf16[8,64,128]{2,1,0:T(8,128)(2,1)S(1)} %get-tuple-element.52), channel_id=1, source_target_pairs={{0,3},{1,2},{2,1},{3,0},{4,7},{5,6},{6,5},{7,4},{8,11},{9,10},{10,... | collective-permute-start | bytes 393224 | tf_op jit(solution)/shard_map/ppermute | solution.py:405
  15.2 3.1 %collective-permute-done.1.near = bf16[8,64,128]{2,1,0:T(8,128)(2,1)S(1)} collective-permute-done((bf16[8,64,128]{2,1,0:T(8,128)(2,1)S(1)}, bf16[8,64,128]{2,1,0:T(8,128)(2,1)S(1)}, u32[]{:S(2)}, u32[]{:S(2)}) %collective-permute-start.1) | collective-permute-done | bytes 131104 | tf_op jit(solution)/shard_map/ppermute | solution.py:405
  18.3 2.3 %shard_map.69 = (f32[1536,128]{1,0:T(8,128)S(1)}, f32[1536,128]{1,0:T(8,128)S(1)}, f32[2,16,128]{2,1,0:T(8,128)S(1)}) custom-call(s32[4]{0:T(128)S(1)} %pad_add_fusion.pos, f32[1536]{0:T(1024)S(1)} %reshape.32.tab, f32[12]{0:T(128)S(1)} %copy-done.1, bf16[8,64,128]{2,1,0:T(8,128)(2,1)S(1)} %get-tuple-element.47.mine, ...), custom_call_target="tpu_custom_call" | custom-call | flops 20000000 | bytes 1000000 | tf_op jit(solution)/shard_map/pallas_call | solution.py:32
  20.7 3.7 %collective-permute-done.2.far = bf16[8,64,128]{2,1,0:T(8,128)(2,1)S(1)} collective-permute-done((bf16[8,64,128]{2,1,0:T(8,128)(2,1)S(1)}, bf16[8,64,128]{2,1,0:T(8,128)(2,1)S(1)}, u32[]{:S(2)}, u32[]{:S(2)}) %collective-permute-start.2) | collective-permute-done | bytes 131104 | tf_op jit(solution)/shard_map/ppermute | solution.py:405
  25.8 2.7 %collective-permute-start.3 = (bf16[384,128]{1,0:T(8,128)(2,1)S(1)}, bf16[384,128]{1,0:T(8,128)(2,1)S(1)}, u32[]{:S(2)}, u32[]{:S(2)}) collective-permute-start(bf16[384,128]{1,0:T(8,128)(2,1)S(1)} %get-tuple-element.59), channel_id=1, source_target_pairs={{0,4},{4,0},{8,12},{12,8},{16,20},{20,16},{24,28},{28,24},{32,36},... | collective-permute-start | bytes 294920 | tf_op jit(solution)/shard_map/ppermute | solution.py:413
  28.5 11.2 %collective-permute-start.4 = (bf16[384,128]{1,0:T(8,128)(2,1)S(1)}, bf16[384,128]{1,0:T(8,128)(2,1)S(1)}, u32[]{:S(2)}, u32[]{:S(2)}) collective-permute-start(bf16[384,128]{1,0:T(8,128)(2,1)S(1)} %get-tuple-element.60), channel_id=1, source_target_pairs={{4,8},{8,4},{12,16},{16,12},{20,24},{24,20},{28,32},{32,28},{36,40... | collective-permute-start | bytes 294920 | tf_op jit(solution)/shard_map/ppermute | solution.py:411
  39.7 3.2 %collective-permute-start.5 = (bf16[384,128]{1,0:T(8,128)(2,1)S(1)}, bf16[384,128]{1,0:T(8,128)(2,1)S(1)}, u32[]{:S(2)}, u32[]{:S(2)}) collective-permute-start(bf16[384,128]{1,0:T(8,128)(2,1)S(1)} %get-tuple-element.61), channel_id=1, source_target_pairs={{0,1},{1,0},{49,48},{48,49},{96,97},{97,96},{145,144},{144,145},{1... | collective-permute-start | bytes 294920 | tf_op jit(solution)/shard_map/ppermute | solution.py:415
  42.9 1.9 %collective-permute-start.6 = (bf16[384,128]{1,0:T(8,128)(2,1)S(1)}, bf16[384,128]{1,0:T(8,128)(2,1)S(1)}, u32[]{:S(2)}, u32[]{:S(2)}) collective-permute-start(bf16[384,128]{1,0:T(8,128)(2,1)S(1)} %get-tuple-element.62), channel_id=1, source_target_pairs={{1,49},{49,1},{48,96},{96,48},{97,145},{145,97},{144,192},{192,144... | collective-permute-start | bytes 294920 | tf_op jit(solution)/shard_map/ppermute | solution.py:414
  44.9 2.2 %shard_map.71 = (f32[1536,128]{1,0:T(8,128)S(1)}, f32[1536,128]{1,0:T(8,128)S(1)}, f32[1536,128]{1,0:T(8,128)S(1)}, f32[1536,128]{1,0:T(8,128)S(1)}, f32[1536,12...) custom-call(s32[4]{0:T(128)S(1)} %pad_add_fusion.pos, f32[1536,128]{1,0:T(8,128)S(1)} %get-tuple-element.50.e, ...), custom_call_target="tpu_custom_call" | custom-call | flops 20000000 | bytes 1000000 | tf_op jit(solution)/shard_map/pallas_call | solution.py:32
  47.1 1.7 %collective-permute-done.6.h3 = bf16[384,128]{1,0:T(8,128)(2,1)S(1)} collective-permute-done((bf16[384,128]{1,0:T(8,128)(2,1)S(1)}, bf16[384,128]{1,0:T(8,128)(2,1)S(1)}, u32[]{:S(2)}, u32[]{:S(2)}) %collective-permute-start.6) | collective-permute-done | bytes 98336 | tf_op jit(solution)/shard_map/ppermute | solution.py:414
  50.3 5.2 %collective-permute-start.7 = (f32[128,128]{1,0:T(8,128)S(1)}, f32[128,128]{1,0:T(8,128)S(1)}, u32[]{:S(2)}, u32[]{:S(2)}) collective-permute-start(f32[128,128]{1,0:T(8,128)S(1)} %get-tuple-element.64.sums), channel_id=1, source_target_pairs={{0,2},{1,3},{2,0},{3,1},{4,6},{5,7},{6,4},{7,5},{8,10},{9,11},{10,... | collective-permute-start | bytes 196616 | tf_op jit(solution)/shard_map/ppermute | solution.py:405
  55.5 1.9 %collective-permute-start.8 = (bf16[192,128]{1,0:T(8,128)(2,1)S(1)}, bf16[192,128]{1,0:T(8,128)(2,1)S(1)}, u32[]{:S(2)}, u32[]{:S(2)}) collective-permute-start(bf16[192,128]{1,0:T(8,128)(2,1)S(1)} %get-tuple-element.71), channel_id=1, source_target_pairs={{0,4},{4,0},{8,12},{12,8},{16,20},{20,16},{24,28},{28,24},{32,36},... | collective-permute-start | bytes 147464 | tf_op jit(solution)/shard_map/ppermute | solution.py:413
  57.4 5.4 %collective-permute-start.9 = (bf16[192,128]{1,0:T(8,128)(2,1)S(1)}, bf16[192,128]{1,0:T(8,128)(2,1)S(1)}, u32[]{:S(2)}, u32[]{:S(2)}) collective-permute-start(bf16[192,128]{1,0:T(8,128)(2,1)S(1)} %get-tuple-element.72), channel_id=1, source_target_pairs={{4,8},{8,4},{12,16},{16,12},{20,24},{24,20},{28,32},{32,28},{36,40... | collective-permute-start | bytes 147464 | tf_op jit(solution)/shard_map/ppermute | solution.py:411
  62.8 4.3 %collective-permute-start.10 = (bf16[192,128]{1,0:T(8,128)(2,1)S(1)}, bf16[192,128]{1,0:T(8,128)(2,1)S(1)}, u32[]{:S(2)}, u32[]{:S(2)}) collective-permute-start(bf16[192,128]{1,0:T(8,128)(2,1)S(1)} %get-tuple-element.73), channel_id=1, source_target_pairs={{0,1},{1,0},{49,48},{48,49},{96,97},{97,96},{145,144},{144,145},{1... | collective-permute-start | bytes 147464 | tf_op jit(solution)/shard_map/ppermute | solution.py:415
  67.1 1.9 %collective-permute-start.11 = (bf16[192,128]{1,0:T(8,128)(2,1)S(1)}, bf16[192,128]{1,0:T(8,128)(2,1)S(1)}, u32[]{:S(2)}, u32[]{:S(2)}) collective-permute-start(bf16[192,128]{1,0:T(8,128)(2,1)S(1)} %get-tuple-element.74), channel_id=1, source_target_pairs={{1,49},{49,1},{48,96},{96,48},{97,145},{145,97},{144,192},{192,144... | collective-permute-start | bytes 147464 | tf_op jit(solution)/shard_map/ppermute | solution.py:414
  69.0 2.0 %shard_map.73 = (f32[1536,128]{1,0:T(8,128)S(1)}, f32[1536,128]{1,0:T(8,128)S(1)}) custom-call(s32[4]{0:T(128)S(1)} %pad_add_fusion.pos, f32[1536,128]{1,0:T(8,128)S(1)} %get-tuple-element.63.e, f32[1536,128]{1,0:T(8,128)S(1)} %get-tuple-element.66.up_c, f32[1536,128]{1,0:T(8,128)S(1)} %get-tuple-element.67.east_c, f32[1536,128]{1,0:T(8,128)S(1)} %get-tuple-element.68.above_c), custom_call_target="tpu_custom_call" | custom-call | flops 20000000 | bytes 1000000 | tf_op jit(solution)/shard_map/pallas_call | solution.py:32
  73.8 1.9 %collective-permute-start.13 = (bf16[192,128]{1,0:T(8,128)(2,1)S(1)}, bf16[192,128]{1,0:T(8,128)(2,1)S(1)}, u32[]{:S(2)}, u32[]{:S(2)}) collective-permute-start(bf16[192,128]{1,0:T(8,128)(2,1)S(1)} %get-tuple-element.81), channel_id=1, source_target_pairs={{0,4},{4,0},{8,12},{12,8},{16,20},{20,16},{24,28},{28,24},{32,36},... | collective-permute-start | bytes 147464 | tf_op jit(solution)/shard_map/ppermute | solution.py:413
  75.7 5.3 %collective-permute-start.14 = (bf16[192,128]{1,0:T(8,128)(2,1)S(1)}, bf16[192,128]{1,0:T(8,128)(2,1)S(1)}, u32[]{:S(2)}, u32[]{:S(2)}) collective-permute-start(bf16[192,128]{1,0:T(8,128)(2,1)S(1)} %get-tuple-element.82), channel_id=1, source_target_pairs={{4,8},{8,4},{12,16},{16,12},{20,24},{24,20},{28,32},{32,28},{36,40... | collective-permute-start | bytes 147464 | tf_op jit(solution)/shard_map/ppermute | solution.py:411
  81.0 1.9 %collective-permute-start.15 = (bf16[192,128]{1,0:T(8,128)(2,1)S(1)}, bf16[192,128]{1,0:T(8,128)(2,1)S(1)}, u32[]{:S(2)}, u32[]{:S(2)}) collective-permute-start(bf16[192,128]{1,0:T(8,128)(2,1)S(1)} %get-tuple-element.83), channel_id=1, source_target_pairs={{0,1},{1,0},{49,48},{48,49},{96,97},{97,96},{145,144},{144,145},{1... | collective-permute-start | bytes 147464 | tf_op jit(solution)/shard_map/ppermute | solution.py:415
  82.9 1.9 %collective-permute-start.16 = (bf16[192,128]{1,0:T(8,128)(2,1)S(1)}, bf16[192,128]{1,0:T(8,128)(2,1)S(1)}, u32[]{:S(2)}, u32[]{:S(2)}) collective-permute-start(bf16[192,128]{1,0:T(8,128)(2,1)S(1)} %get-tuple-element.84), channel_id=1, source_target_pairs={{1,49},{49,1},{48,96},{96,48},{97,145},{145,97},{144,192},{192,144... | collective-permute-start | bytes 147464 | tf_op jit(solution)/shard_map/ppermute | solution.py:414
  84.9 3.2 %collective-permute-start.12 = (f32[64,128]{1,0:T(8,128)S(1)}, f32[64,128]{1,0:T(8,128)S(1)}, u32[]{:S(2)}, u32[]{:S(2)}) collective-permute-start(f32[64,128]{1,0:T(8,128)S(1)} %get-tuple-element.78.part), channel_id=1, source_target_pairs={{0,2},{1,3},{2,0},{3,1},{4,6},{5,7},{6,4},{7,5},{8,10},{9,11},{10,... | collective-permute-start | bytes 98312 | tf_op jit(solution)/shard_map/ppermute | solution.py:405
  88.0 2.0 %shard_map.75 = (f32[1536,128]{1,0:T(8,128)S(1)}, f32[1536,128]{1,0:T(8,128)S(1)}) custom-call(s32[4]{0:T(128)S(1)} %pad_add_fusion.pos, f32[1536,128]{1,0:T(8,128)S(1)} %get-tuple-element.75.e, f32[1536,128]{1,0:T(8,128)S(1)} %get-tuple-element.66.up_c, f32[1536,128]{1,0:T(8,128)S(1)} %get-tuple-element.67.east_c, f32[1536,128]{1,0:T(8,128)S(1)} %get-tuple-element.68.above_c), custom_call_target="tpu_custom_call" | custom-call | flops 20000000 | bytes 1000000 | tf_op jit(solution)/shard_map/pallas_call | solution.py:32
  90.0 1.5 %collective-permute-done.12.got = f32[64,128]{1,0:T(8,128)S(1)} collective-permute-done((f32[64,128]{1,0:T(8,128)S(1)}, f32[64,128]{1,0:T(8,128)S(1)}, u32[]{:S(2)}, u32[]{:S(2)}) %collective-permute-start.12) | collective-permute-done | bytes 32800 | tf_op jit(solution)/shard_map/ppermute | solution.py:405
  93.0 4.9 %collective-permute-start.17 = (f32[12,64,128]{2,1,0:T(8,128)S(1)}, f32[12,64,128]{2,1,0:T(8,128)S(1)}, u32[]{:S(2)}, u32[]{:S(2)}) collective-permute-start(f32[12,64,128]{2,1,0:T(8,128)S(1)} %get-tuple-element.85), channel_id=1, source_target_pairs={{0,1},{1,0},{2,3},{3,2},{4,5},{5,4},{6,7},{7,6},{8,9},{9,8},{10,11... | collective-permute-start | bytes 1179656 | tf_op jit(solution)/shard_map/ppermute | solution.py:405
  97.9 2.8 %collective-permute-start.18 = (f32[64,128]{1,0:T(8,128)S(1)}, f32[64,128]{1,0:T(8,128)S(1)}, u32[]{:S(2)}, u32[]{:S(2)}) collective-permute-start(f32[64,128]{1,0:T(8,128)S(1)} %get-tuple-element.86.ksum), channel_id=1, source_target_pairs={{0,2},{1,3},{2,0},{3,1},{4,6},{5,7},{6,4},{7,5},{8,10},{9,11},{10,... | collective-permute-start | bytes 98312 | tf_op jit(solution)/shard_map/ppermute | solution.py:405
  100.7 6.8 %collective-permute-done.18.got = f32[64,128]{1,0:T(8,128)S(1)} collective-permute-done((f32[64,128]{1,0:T(8,128)S(1)}, f32[64,128]{1,0:T(8,128)S(1)}, u32[]{:S(2)}, u32[]{:S(2)}) %collective-permute-start.18) | collective-permute-done | bytes 32800 | tf_op jit(solution)/shard_map/ppermute | solution.py:405
  107.5 2.5 %collective-permute-start.19 = (f32[64,128]{1,0:T(8,128)S(1)}, f32[64,128]{1,0:T(8,128)S(1)}, u32[]{:S(2)}, u32[]{:S(2)}) collective-permute-start(f32[64,128]{1,0:T(8,128)S(1)} %shard_map.77.mine), channel_id=1, source_target_pairs={{0,1},{1,0},{2,3},{3,2},{4,5},{5,4},{6,7},{7,6},{8,9},{9,8},{10,11... | collective-permute-start | bytes 98312 | tf_op jit(solution)/shard_map/ppermute | solution.py:405
  111.4 1.9 %collective-permute-done.19.other = f32[64,128]{1,0:T(8,128)S(1)} collective-permute-done((f32[64,128]{1,0:T(8,128)S(1)}, f32[64,128]{1,0:T(8,128)S(1)}, u32[]{:S(2)}, u32[]{:S(2)}) %collective-permute-start.19) | collective-permute-done | bytes 32800 | tf_op jit(solution)/shard_map/ppermute | solution.py:405
  113.3 2.0 %join.1 = (f32[12,128,128]{2,1,0:T(8,128)}, f32[128,128]{1,0:T(8,128)}) custom-call(s32[4]{0:T(128)S(1)} %pad_add_fusion.pos, f32[12,64,128]{2,1,0:T(8,128)S(1)} %collective-permute-done.17.pair, f32[64,128]{1,0:T(8,128)S(1)} %shard_map.77.mine, f32[64,128]{1,0:T(8,128)S(1)} %collective-permute-done.19.other, ...), custom_call_target="tpu_custom_call", output_to_operand_aliasing={{0}: (4, {})} | custom-call | tf_op jit(solution)/shard_map/join/pallas_call | solution.py:496
  (28 shorter events, 8.6 us)
Async XLA Ops:
  0.7 14.4 %copy-start.2 = (bf16[32,48]{1,0:T(8,128)(2,1)S(1)}, bf16[32,48]{1,0:T(8,128)(2,1)}, u32[]{:S(2)}) copy-start(bf16[32,48]{1,0:T(8,128)(2,1)} %param.6) | copy-start | bytes 9220
  2.8 15.5 %collective-permute-start = (bf16[1328,128]{1,0:T(8,128)(2,1)S(1)}, bf16[1328,128]{1,0:T(8,128)(2,1)S(1)}, u32[]{:S(2)}, u32[]{:S(2)}) collective-permute-start(bf16[1328,128]{1,0:T(8,128)(2,1)S(1)} %get-tuple-element.48), channel_id=1, source_target_pairs={{0,1},{1,0},{2,3},{3,2},{4,5},{5,4},{6,7},{7,6},{8,9},{9,8},{10,11... | collective-permute-start | bytes 1019912 | tf_op jit(solution)/shard_map/ppermute | solution.py:405
  7.1 11.2 %collective-permute-start.1 = (bf16[8,64,128]{2,1,0:T(8,128)(2,1)S(1)}, bf16[8,64,128]{2,1,0:T(8,128)(2,1)S(1)}, u32[]{:S(2)}, u32[]{:S(2)}) collective-permute-start(bf16[8,64,128]{2,1,0:T(8,128)(2,1)S(1)} %get-tuple-element.47.mine), channel_id=1, source_target_pairs={{0,2},{1,3},{2,0},{3,1},{4,6},{5,7},{6,4},{7,5},{8,10},{9,11},{10,... | collective-permute-start | bytes 393224 | tf_op jit(solution)/shard_map/ppermute | solution.py:405
  13.2 11.2 %collective-permute-start.2 = (bf16[8,64,128]{2,1,0:T(8,128)(2,1)S(1)}, bf16[8,64,128]{2,1,0:T(8,128)(2,1)S(1)}, u32[]{:S(2)}, u32[]{:S(2)}) collective-permute-start(bf16[8,64,128]{2,1,0:T(8,128)(2,1)S(1)} %get-tuple-element.52), channel_id=1, source_target_pairs={{0,3},{1,2},{2,1},{3,0},{4,7},{5,6},{6,5},{7,4},{8,11},{9,10},{10,... | collective-permute-start | bytes 393224 | tf_op jit(solution)/shard_map/ppermute | solution.py:405
  15.2 3.1 %copy-start.1 = (f32[12]{0:T(128)S(1)}, f32[12]{0:T(128)}, u32[]{:S(2)}) copy-start(f32[12]{0:T(128)} %planck.3) | copy-start | bytes 148
  25.8 21.3 %collective-permute-start.3 = (bf16[384,128]{1,0:T(8,128)(2,1)S(1)}, bf16[384,128]{1,0:T(8,128)(2,1)S(1)}, u32[]{:S(2)}, u32[]{:S(2)}) collective-permute-start(bf16[384,128]{1,0:T(8,128)(2,1)S(1)} %get-tuple-element.59), channel_id=1, source_target_pairs={{0,4},{4,0},{8,12},{12,8},{16,20},{20,16},{24,28},{28,24},{32,36},... | collective-permute-start | bytes 294920 | tf_op jit(solution)/shard_map/ppermute | solution.py:413
  28.5 18.6 %collective-permute-start.4 = (bf16[384,128]{1,0:T(8,128)(2,1)S(1)}, bf16[384,128]{1,0:T(8,128)(2,1)S(1)}, u32[]{:S(2)}, u32[]{:S(2)}) collective-permute-start(bf16[384,128]{1,0:T(8,128)(2,1)S(1)} %get-tuple-element.60), channel_id=1, source_target_pairs={{4,8},{8,4},{12,16},{16,12},{20,24},{24,20},{28,32},{32,28},{36,40... | collective-permute-start | bytes 294920 | tf_op jit(solution)/shard_map/ppermute | solution.py:411
  39.7 7.4 %collective-permute-start.5 = (bf16[384,128]{1,0:T(8,128)(2,1)S(1)}, bf16[384,128]{1,0:T(8,128)(2,1)S(1)}, u32[]{:S(2)}, u32[]{:S(2)}) collective-permute-start(bf16[384,128]{1,0:T(8,128)(2,1)S(1)} %get-tuple-element.61), channel_id=1, source_target_pairs={{0,1},{1,0},{49,48},{48,49},{96,97},{97,96},{145,144},{144,145},{1... | collective-permute-start | bytes 294920 | tf_op jit(solution)/shard_map/ppermute | solution.py:415
  42.9 5.9 %collective-permute-start.6 = (bf16[384,128]{1,0:T(8,128)(2,1)S(1)}, bf16[384,128]{1,0:T(8,128)(2,1)S(1)}, u32[]{:S(2)}, u32[]{:S(2)}) collective-permute-start(bf16[384,128]{1,0:T(8,128)(2,1)S(1)} %get-tuple-element.62), channel_id=1, source_target_pairs={{1,49},{49,1},{48,96},{96,48},{97,145},{145,97},{144,192},{192,144... | collective-permute-start | bytes 294920 | tf_op jit(solution)/shard_map/ppermute | solution.py:414
  44.9 4.0 %copy-start = (f32[16,8,128]{2,1,0:T(8,128)S(1)}, f32[16,8,128]{2,1,0:T(8,128)}, u32[]{:S(2)}) copy-start(f32[16,8,128]{2,1,0:T(8,128)} %param.9) | copy-start | bytes 196612
  50.3 22.2 %collective-permute-start.7 = (f32[128,128]{1,0:T(8,128)S(1)}, f32[128,128]{1,0:T(8,128)S(1)}, u32[]{:S(2)}, u32[]{:S(2)}) collective-permute-start(f32[128,128]{1,0:T(8,128)S(1)} %get-tuple-element.64.sums), channel_id=1, source_target_pairs={{0,2},{1,3},{2,0},{3,1},{4,6},{5,7},{6,4},{7,5},{8,10},{9,11},{10,... | collective-permute-start | bytes 196616 | tf_op jit(solution)/shard_map/ppermute | solution.py:405
  55.5 15.5 %collective-permute-start.8 = (bf16[192,128]{1,0:T(8,128)(2,1)S(1)}, bf16[192,128]{1,0:T(8,128)(2,1)S(1)}, u32[]{:S(2)}, u32[]{:S(2)}) collective-permute-start(bf16[192,128]{1,0:T(8,128)(2,1)S(1)} %get-tuple-element.71), channel_id=1, source_target_pairs={{0,4},{4,0},{8,12},{12,8},{16,20},{20,16},{24,28},{28,24},{32,36},... | collective-permute-start | bytes 147464 | tf_op jit(solution)/shard_map/ppermute | solution.py:413
  57.4 13.6 %collective-permute-start.9 = (bf16[192,128]{1,0:T(8,128)(2,1)S(1)}, bf16[192,128]{1,0:T(8,128)(2,1)S(1)}, u32[]{:S(2)}, u32[]{:S(2)}) collective-permute-start(bf16[192,128]{1,0:T(8,128)(2,1)S(1)} %get-tuple-element.72), channel_id=1, source_target_pairs={{4,8},{8,4},{12,16},{16,12},{20,24},{24,20},{28,32},{32,28},{36,40... | collective-permute-start | bytes 147464 | tf_op jit(solution)/shard_map/ppermute | solution.py:411
  62.8 8.2 %collective-permute-start.10 = (bf16[192,128]{1,0:T(8,128)(2,1)S(1)}, bf16[192,128]{1,0:T(8,128)(2,1)S(1)}, u32[]{:S(2)}, u32[]{:S(2)}) collective-permute-start(bf16[192,128]{1,0:T(8,128)(2,1)S(1)} %get-tuple-element.73), channel_id=1, source_target_pairs={{0,1},{1,0},{49,48},{48,49},{96,97},{97,96},{145,144},{144,145},{1... | collective-permute-start | bytes 147464 | tf_op jit(solution)/shard_map/ppermute | solution.py:415
  67.1 5.4 %collective-permute-start.11 = (bf16[192,128]{1,0:T(8,128)(2,1)S(1)}, bf16[192,128]{1,0:T(8,128)(2,1)S(1)}, u32[]{:S(2)}, u32[]{:S(2)}) collective-permute-start(bf16[192,128]{1,0:T(8,128)(2,1)S(1)} %get-tuple-element.74), channel_id=1, source_target_pairs={{1,49},{49,1},{48,96},{96,48},{97,145},{145,97},{144,192},{192,144... | collective-permute-start | bytes 147464 | tf_op jit(solution)/shard_map/ppermute | solution.py:414
  73.8 17.8 %collective-permute-start.13 = (bf16[192,128]{1,0:T(8,128)(2,1)S(1)}, bf16[192,128]{1,0:T(8,128)(2,1)S(1)}, u32[]{:S(2)}, u32[]{:S(2)}) collective-permute-start(bf16[192,128]{1,0:T(8,128)(2,1)S(1)} %get-tuple-element.81), channel_id=1, source_target_pairs={{0,4},{4,0},{8,12},{12,8},{16,20},{20,16},{24,28},{28,24},{32,36},... | collective-permute-start | bytes 147464 | tf_op jit(solution)/shard_map/ppermute | solution.py:413
  75.7 15.8 %collective-permute-start.14 = (bf16[192,128]{1,0:T(8,128)(2,1)S(1)}, bf16[192,128]{1,0:T(8,128)(2,1)S(1)}, u32[]{:S(2)}, u32[]{:S(2)}) collective-permute-start(bf16[192,128]{1,0:T(8,128)(2,1)S(1)} %get-tuple-element.82), channel_id=1, source_target_pairs={{4,8},{8,4},{12,16},{16,12},{20,24},{24,20},{28,32},{32,28},{36,40... | collective-permute-start | bytes 147464 | tf_op jit(solution)/shard_map/ppermute | solution.py:411
  81.0 10.6 %collective-permute-start.15 = (bf16[192,128]{1,0:T(8,128)(2,1)S(1)}, bf16[192,128]{1,0:T(8,128)(2,1)S(1)}, u32[]{:S(2)}, u32[]{:S(2)}) collective-permute-start(bf16[192,128]{1,0:T(8,128)(2,1)S(1)} %get-tuple-element.83), channel_id=1, source_target_pairs={{0,1},{1,0},{49,48},{48,49},{96,97},{97,96},{145,144},{144,145},{1... | collective-permute-start | bytes 147464 | tf_op jit(solution)/shard_map/ppermute | solution.py:415
  82.9 8.7 %collective-permute-start.16 = (bf16[192,128]{1,0:T(8,128)(2,1)S(1)}, bf16[192,128]{1,0:T(8,128)(2,1)S(1)}, u32[]{:S(2)}, u32[]{:S(2)}) collective-permute-start(bf16[192,128]{1,0:T(8,128)(2,1)S(1)} %get-tuple-element.84), channel_id=1, source_target_pairs={{1,49},{49,1},{48,96},{96,48},{97,145},{145,97},{144,192},{192,144... | collective-permute-start | bytes 147464 | tf_op jit(solution)/shard_map/ppermute | solution.py:414
  84.9 6.7 %collective-permute-start.12 = (f32[64,128]{1,0:T(8,128)S(1)}, f32[64,128]{1,0:T(8,128)S(1)}, u32[]{:S(2)}, u32[]{:S(2)}) collective-permute-start(f32[64,128]{1,0:T(8,128)S(1)} %get-tuple-element.78.part), channel_id=1, source_target_pairs={{0,2},{1,3},{2,0},{3,1},{4,6},{5,7},{6,4},{7,5},{8,10},{9,11},{10,... | collective-permute-start | bytes 98312 | tf_op jit(solution)/shard_map/ppermute | solution.py:405
  93.0 20.3 %collective-permute-start.17 = (f32[12,64,128]{2,1,0:T(8,128)S(1)}, f32[12,64,128]{2,1,0:T(8,128)S(1)}, u32[]{:S(2)}, u32[]{:S(2)}) collective-permute-start(f32[12,64,128]{2,1,0:T(8,128)S(1)} %get-tuple-element.85), channel_id=1, source_target_pairs={{0,1},{1,0},{2,3},{3,2},{4,5},{5,4},{6,7},{7,6},{8,9},{9,8},{10,11... | collective-permute-start | bytes 1179656 | tf_op jit(solution)/shard_map/ppermute | solution.py:405
  97.9 9.6 %collective-permute-start.18 = (f32[64,128]{1,0:T(8,128)S(1)}, f32[64,128]{1,0:T(8,128)S(1)}, u32[]{:S(2)}, u32[]{:S(2)}) collective-permute-start(f32[64,128]{1,0:T(8,128)S(1)} %get-tuple-element.86.ksum), channel_id=1, source_target_pairs={{0,2},{1,3},{2,0},{3,1},{4,6},{5,7},{6,4},{7,5},{8,10},{9,11},{10,... | collective-permute-start | bytes 98312 | tf_op jit(solution)/shard_map/ppermute | solution.py:405
  107.5 5.8 %collective-permute-start.19 = (f32[64,128]{1,0:T(8,128)S(1)}, f32[64,128]{1,0:T(8,128)S(1)}, u32[]{:S(2)}, u32[]{:S(2)}) collective-permute-start(f32[64,128]{1,0:T(8,128)S(1)} %shard_map.77.mine), channel_id=1, source_target_pairs={{0,1},{1,0},{2,3},{3,2},{4,5},{5,4},{6,7},{7,6},{8,9},{9,8},{10,11... | collective-permute-start | bytes 98312 | tf_op jit(solution)/shard_map/ppermute | solution.py:405

commit v3 on v0

--- a/solution.py
+++ b/solution.py
@@ -57,6 +57,10 @@
 PART = OWN * ROWS * LAT
 N = ROWS * LAT
 COEF = 0.75 / SCALE
+
+
+def half_rows(half):
+    return pl.ds(pl.multiple_of(N * half, N), N)
 
 
 def pack_kernel(pos, planck, dust, eold, eown, pair, near, far, stage, shares, sems):
@@ -129,39 +133,24 @@
     return acc
 
 
-def early_kernel(pos, tab, mine, near, far, kap, wide):
+def early_kernel(pos, tab, planck, mine, pair, far, eown, kap, e, share, wide):
     place = pos[2]
-    for j, block in enumerate((mine, near, far)):
-        for b in range(BINS):
-            wide[pl.ds(j * SIZE + b * N, N), :] = block[b].astype(F32)
+    slot = place % 2
+    for b in range(BINS):
+        wide[pl.ds(b * N, N), :] = mine[b].astype(F32)
+        wide[pl.ds(SIZE + b * N, N), :] = pair[pl.ds(b * N, N), :].astype(F32)
+        wide[pl.ds(2 * SIZE + b * N, N), :] = far[b].astype(F32)
 
     def one(g, carry):
-        acc = gather_bins(tab, wide, place, (0, 2, 3), g, [None] * ROWS)
+        acc = gather_bins(tab, wide, place, (0, 1, 3), g, [None] * ROWS)
         for r in range(ROWS):
             kap[tile(g * ROWS + r), :] = acc[r]
         return carry
 
     lax.fori_loop(0, GROUPS, one, 0, unroll=2)
-
-
-def late_kernel(pos, tab, planck, part, eown, pair, kap, e, share, t1, t2, r1, r2, wide):
-    place = pos[2]
-    slot = place % 2
-    wide[...] = pair[pl.ds(0, SIZE), :].astype(F32)
-
-    def one(g, carry):
-        acc = [part[tile(g * ROWS + r), :] for r in range(ROWS)]
-        acc = gather_bins(tab, wide, place, (1,), g, acc)
-        for r in range(ROWS):
-            kap[tile(g * ROWS + r), :] = acc[r]
-        return carry
-
-    lax.fori_loop(0, GROUPS, one, 0, unroll=2)
-    theirs = pl.multiple_of((1 - slot) * PART, PART)
-    mine = pl.multiple_of(slot * PART, PART)
     for g in range(OWN):
-        e[pl.ds(mine + g * N, N), :] = eown[g]
-    e[pl.ds(theirs, PART), :] = pair[pl.ds(SIZE, PART), :].astype(F32)
+        e[half_rows(slot * OWN + g), :] = eown[g]
+        e[half_rows((1 - slot) * OWN + g), :] = pair[pl.ds(SIZE + g * N, N), :].astype(F32)
     at = SIZE + PART
     pieces = [pair[pl.ds(at + 2 * LAT * i, 2 * LAT), :].astype(F32) for i in range(3)]
     row = lax.broadcasted_iota(jnp.int32, (2 * LAT, LANES), 0)
@@ -170,6 +159,21 @@
         ours = jnp.where(row == g, planck[g], ours)
     share[slot] = ours
     share[1 - slot] = pieces[0] + pieces[1] + pieces[2]
+
+
+def late_kernel(pos, tab, part, near, e, kap, t1, t2, r1, r2, wide):
+    place = pos[2]
+    for b in range(BINS):
+        wide[pl.ds(b * N, N), :] = near[b].astype(F32)
+
+    def one(g, carry):
+        acc = [part[tile(g * ROWS + r), :] for r in range(ROWS)]
+        acc = gather_bins(tab, wide, place, (2,), g, acc)
+        for r in range(ROWS):
+            kap[tile(g * ROWS + r), :] = acc[r]
+        return carry
+
+    lax.fori_loop(0, GROUPS, one, 0, unroll=4)
     write_slabs(pos, e, 0, t1, t2, r1, r2)
     write_slabs(pos, kap, TILES, t1, t2, r1, r2)
 
@@ -190,8 +194,6 @@
 
 
 def inner_body(e, coefs, flux, weight, prepare):
-    top = lax.broadcasted_iota(jnp.int32, (LAT, LANES), 0) == LAT - 1
-
     def one(g, carry):
         base = g * ROWS
         tiles = [e[tile(base + r), :] for r in range(ROWS)]
@@ -201,7 +203,6 @@
             here = tiles[r]
             c_up, c_east, c_above = coef[r]
             w_up, f_up = face(here, pltpu.roll(here, LAT - 1, 0), c_up)
-            w_up, f_up = jnp.where(top, 0.0, w_up), jnp.where(top, 0.0, f_up)
             w_east, f_east = face(here, pltpu.roll(here, LANES - 1, 1), c_east)
             w = (w_up + pltpu.roll(w_up, 1, 0)) + (w_east + pltpu.roll(w_east, 1, 1))
             f = (f_up - pltpu.roll(f_up, 1, 0)) + (f_east - pltpu.roll(f_east, 1, 1))
@@ -222,6 +223,7 @@
 
 def inner_first(pos, e, kap, share, flux, weight, up_c, east_c, above_c, e01, ssum):
     ssum[...] = jnp.zeros_like(ssum)
+    top = lax.broadcasted_iota(jnp.int32, (LAT, LANES), 0) == LAT - 1
 
     def prepare(g, base, tiles):
         ks = [kap[tile(base + r), :] for r in range(ROWS)]
@@ -230,7 +232,8 @@
         out = []
         for r in range(ROWS):
             k = ks[r]
-            c_up, c_east = COEF * (k + pltpu.roll(k, LAT - 1, 0)), COEF * (k + pltpu.roll(k, LANES - 1, 1))
+            c_up = jnp.where(top, jnp.inf, COEF * (k + pltpu.roll(k, LAT - 1, 0)))
+            c_east = COEF * (k + pltpu.roll(k, LANES - 1, 1))
             out.append((c_up, c_east, COEF * (k + ks[r + 1]) if r + 1 < ROWS else None))
         for r in range(ROWS):
             i = base + r
@@ -264,6 +267,8 @@
         refs = (e, kap, weight, flux, e01)
         rows = [[x[tile(base + r), :] for x in refs] + [temp4[tile(r), :]] for r in range(ROWS)]
         ends = {at: (halo[j, tile(g), :], edge[j, tile(g), :]) for j, at in ((2, 0), (3, ROWS - 1))}
+        strips = [pl.ds(base * LAT + at, ROWS, stride=LAT) for at in (0, LAT - 1)]
+        strips = [(strip, e[strip, :]) for strip in strips]
         out = []
         for r in range(ROWS):
             here, k, w, f, old, t4 = rows[r]
@@ -273,15 +278,13 @@
             out.append((old + k * (row_share * t4) + (here * w + f), SCALE + k + w))
         for r in range(ROWS):
             numer[tile(base + r), :], denom[tile(base + r), :] = out[r]
+        for j, (strip, past) in enumerate(strips):
+            w, _ = face(past, halo[j, tile(g), :], edge[j, tile(g), :])
+            numer[strip, :] = numer[strip, :] + w * halo[j, tile(g), :]
+            denom[strip, :] = denom[strip, :] + w
         return carry
 
-    lax.fori_loop(0, GROUPS, one, 0, unroll=UNROLL)
-    for j, at in ((0, 0), (1, LAT - 1)):
-        strip = pl.ds(at, TILES, stride=LAT)
-        out = halo[j]
-        w, _ = face(e[strip, :], out, edge[j])
-        numer[strip, :] = numer[strip, :] + w * out
-        denom[strip, :] = denom[strip, :] + w
+    lax.fori_loop(0, GROUPS, one, 0, unroll=8)
 
     def two(g, sums):
         at = [tile(g * ROWS + r) for r in range(ROWS)]
@@ -291,7 +294,7 @@
             enew[at[r], :] = fresh[r]
         return sums
 
-    sums = lax.fori_loop(0, GROUPS, two, (jnp.zeros((LAT, LANES), F32),) * ROWS, unroll=UNROLL)
+    sums = lax.fori_loop(0, GROUPS, two, (jnp.zeros((LAT, LANES), F32),) * ROWS, unroll=8)
     for r in range(ROWS):
         ksum[tile(r), :] = sums[r]
 
@@ -345,8 +348,8 @@
     unpack_halos(pos, (h0, h1, h2, h3), 0, halo)
     s = stot[...]
     old = own_rows(pos, told)
-    up, down = terms(old, tprev[...], s)
-    t = (up + (part[...] + got[...]) / SCALE) / down
+    above, below = terms(old, tprev[...], s)
+    t = (above + (part[...] + got[...]) / SCALE) / below
     temp4[...] = t * t * t * t
     outer_body(e, e01, kap, share, temp4, halo, edge, flux, weight, enew, ksum, numer, denom)
     slot = pos[2] % 2
@@ -421,20 +424,22 @@
         (pos, *(pltpu.with_memory_space_constraint(x, pltpu.HBM) for x in (planck, dust, energy_old))), smem=1, space=pl.ANY,
         scratch=[VMEM((OWN, N, LANES), F32), SMEM(planck.shape, F32), pltpu.SemaphoreType.DMA((5,))],
     )
+    pair = xor(pair, 1)
+    near = xor(mine, 2)
     far = xor(far, 3)
-    near = xor(mine, 2)
-    pair = xor(pair, 1)
-    early, = call(
-        early_kernel, [full], (pos, tab, keep(mine), keep(near), keep(far)), smem=2,
+    early, e, share = call(
+        early_kernel, [full, full, held((2, 2 * LAT, LANES))],
+        (pos, tab, planck, keep(mine), keep(pair), keep(far), keep(eown)), smem=3,
         scratch=[VMEM((3 * SIZE, LANES), F32)], flops=20_000_000,
     )
-    kap, e, share, *both = call(
+    e = keep(e)
+    kap, *both = call(
         late_kernel,
-        [full, full, held((2, 2 * LAT, LANES))] + [held((2 * TILES, LANES), BF)] * 4,
-        (pos, tab, planck, keep(early), keep(eown), keep(pair)), smem=3,
+        [full] + [held((2 * TILES, LANES), BF)] * 4,
+        (pos, tab, keep(early), keep(near), e), smem=2,
         scratch=[VMEM((SIZE, LANES), F32)], flops=5_000_000,
     )
-    kap, share, e = keep(kap), keep(share), keep(e)
+    kap, share = keep(kap), keep(share)
     halos, _ = swap_halos(both)
     flux, weight, *coefs, e01, ssum = call(
         inner_first, [full] * 6 + [sheet], (pos, e, kap, share), smem=1, flops=20_000_000,

time: 117 us -> 114 us (0.974)
  waiting for transfers between devices: 18.4 us -> 16.2 us
    ppermute x8, waiting for transfers between devices: 18.3 us -> 16 us  [xor(): return lax.ppermute(x, 'group', [(i, i ^ k) for i in range(4)])]
where the time goes in v3:
time: 114 us; the launch traced here: 113 us
  starting transfers between devices  78.4 us (69%)
  Pallas kernels  17.2 us (15%)
  waiting for transfers between devices  16.2 us (14%)
    ppermute x8, starting transfers between devices, xor(): return lax.ppermute(x, 'group', [(i, i ^ k) for i in range(4)])  26.9 us
    ppermute x3, starting transfers between devices, swap_halos(): t2 = lax.ppermute(t2, 'theta', theta_pairs(nt, 1))  19.4 us
    ppermute x3, starting transfers between devices, swap_halos(): r2 = lax.ppermute(r2, ('row', 'group'), row_pairs(nr, 1))  17.6 us
    pallas_call x10, Pallas kernels, call(): pl.pallas_call(kernel, out_shape=outs, in_specs=specs, out_specs=[pl.Bloc...  17.2 us
    ppermute x8, waiting for transfers between devices, xor(): return lax.ppermute(x, 'group', [(i, i ^ k) for i in range(4)])  16 us
    ppermute x3, starting transfers between devices, swap_halos(): r1 = lax.ppermute(r1, ('row', 'group'), row_pairs(nr, 0))  8.2 us
    ppermute x3, starting transfers between devices, swap_halos(): t1 = lax.ppermute(t1, 'theta', theta_pairs(nt, 0))  6.29 us
  transfers between devices with their start and end apart: 20, of which 5 were waited for; matrix products, arithmetic and copies ran while one was open for 0% of the time, Pallas kernels for 7%

profile of v3, /device:TPU:31, one launch (start us, length us, event | category | flops | bytes accessed | tf_op | source)
XLA Modules:
  0.0 112.8 jit_solution(1351271836926029601)
XLA Ops:
  0.7 1.8 %shard_map.68 = (f32[12,64,128]{2,1,0:T(8,128)S(1)}, bf16[1328,128]{1,0:T(8,128)(2,1)S(1)}, bf16[8,64,128]{2,1,0:T(8,128)(2,1)S(1)}, bf16[8,64,128]{2,1,0:T(8,128)(2,1)S(1)}) custom-call(s32[4]{0:T(128)S(1)} %pad_add_fusion.pos, f32[12]{0:T(128)} %planck.3, bf16[8,128,128]{2,1,0:T(8,128)(2,1)} %bitcast.13, f32[12,128,128]{2,1,0:T(8,128)} %bitcast.12), custom_call_target="tpu_custom_call" | custom-call | flops 1000000 | bytes 1000000 | tf_op jit(solution)/shard_map/pallas_call | solution.py:32
  2.5 4.0 %collective-permute-start = (bf16[1328,128]{1,0:T(8,128)(2,1)S(1)}, bf16[1328,128]{1,0:T(8,128)(2,1)S(1)}, u32[]{:S(2)}, u32[]{:S(2)}) collective-permute-start(bf16[1328,128]{1,0:T(8,128)(2,1)S(1)} %get-tuple-element.46), channel_id=1, source_target_pairs={{0,1},{1,0},{2,3},{3,2},{4,5},{5,4},{6,7},{7,6},{8,9},{9,8},{10,11... | collective-permute-start | bytes 1019912 | tf_op jit(solution)/shard_map/ppermute | solution.py:393
  6.6 5.5 %collective-permute-start.1 = (bf16[8,64,128]{2,1,0:T(8,128)(2,1)S(1)}, bf16[8,64,128]{2,1,0:T(8,128)(2,1)S(1)}, u32[]{:S(2)}, u32[]{:S(2)}) collective-permute-start(bf16[8,64,128]{2,1,0:T(8,128)(2,1)S(1)} %get-tuple-element.47), channel_id=1, source_target_pairs={{0,3},{1,2},{2,1},{3,0},{4,7},{5,6},{6,5},{7,4},{8,11},{9,10},{10,... | collective-permute-start | bytes 393224 | tf_op jit(solution)/shard_map/ppermute | solution.py:393
  12.1 2.2 %collective-permute-start.2 = (bf16[8,64,128]{2,1,0:T(8,128)(2,1)S(1)}, bf16[8,64,128]{2,1,0:T(8,128)(2,1)S(1)}, u32[]{:S(2)}, u32[]{:S(2)}) collective-permute-start(bf16[8,64,128]{2,1,0:T(8,128)(2,1)S(1)} %get-tuple-element.45.mine), channel_id=1, source_target_pairs={{0,2},{1,3},{2,0},{3,1},{4,6},{5,7},{6,4},{7,5},{8,10},{9,11},{10,... | collective-permute-start | bytes 393224 | tf_op jit(solution)/shard_map/ppermute | solution.py:393
  14.4 6.3 %collective-permute-done.1.far = bf16[8,64,128]{2,1,0:T(8,128)(2,1)S(1)} collective-permute-done((bf16[8,64,128]{2,1,0:T(8,128)(2,1)S(1)}, bf16[8,64,128]{2,1,0:T(8,128)(2,1)S(1)}, u32[]{:S(2)}, u32[]{:S(2)}) %collective-permute-start.1) | collective-permute-done | bytes 131104 | tf_op jit(solution)/shard_map/ppermute | solution.py:393
  20.7 2.3 %shard_map.69 = (f32[1536,128]{1,0:T(8,128)S(1)}, f32[1536,128]{1,0:T(8,128)S(1)}, f32[2,16,128]{2,1,0:T(8,128)S(1)}) custom-call(s32[4]{0:T(128)S(1)} %pad_add_fusion.pos, f32[1536]{0:T(1024)S(1)} %reshape.32.tab, f32[12]{0:T(128)S(1)} %copy-done.1, bf16[8,64,128]{2,1,0:T(8,128)(2,1)S(1)} %get-tuple-element.45.mine, ...), custom_call_target="tpu_custom_call" | custom-call | flops 20000000 | bytes 1000000 | tf_op jit(solution)/shard_map/pallas_call | solution.py:32
  23.0 2.2 %collective-permute-done.2.near = bf16[8,64,128]{2,1,0:T(8,128)(2,1)S(1)} collective-permute-done((bf16[8,64,128]{2,1,0:T(8,128)(2,1)S(1)}, bf16[8,64,128]{2,1,0:T(8,128)(2,1)S(1)}, u32[]{:S(2)}, u32[]{:S(2)}) %collective-permute-start.2) | collective-permute-done | bytes 131104 | tf_op jit(solution)/shard_map/ppermute | solution.py:393
  25.2 1.4 %shard_map.70 = (f32[1536,128]{1,0:T(8,128)S(1)}, bf16[384,128]{1,0:T(8,128)(2,1)S(1)}, bf16[384,128]{1,0:T(8,128)(2,1)S(1)}, bf16[384,128]{1,0:T(8,128)(2,1)S(1)}, bf16[384,128]{1,0:T(8,128)(2,1)S(1)}) custom-call(s32[4]{0:T(128)S(1)} %pad_add_fusion.pos, f32[1536]{0:T(1024)S(1)} %reshape.32.tab, f32[1536,128]{1,0:T(8,128)S(1)} %get-tuple-element.50.part, ...), custom_call_target="tpu_custom_call" | custom-call | flops 5000000 | bytes 1000000 | tf_op jit(solution)/shard_map/pallas_call | solution.py:32
  26.6 2.5 %collective-permute-start.3 = (bf16[384,128]{1,0:T(8,128)(2,1)S(1)}, bf16[384,128]{1,0:T(8,128)(2,1)S(1)}, u32[]{:S(2)}, u32[]{:S(2)}) collective-permute-start(bf16[384,128]{1,0:T(8,128)(2,1)S(1)} %get-tuple-element.57), channel_id=1, source_target_pairs={{0,4},{4,0},{8,12},{12,8},{16,20},{20,16},{24,28},{28,24},{32,36},... | collective-permute-start | bytes 294920 | tf_op jit(solution)/shard_map/ppermute | solution.py:401
  29.0 10.9 %collective-permute-start.4 = (bf16[384,128]{1,0:T(8,128)(2,1)S(1)}, bf16[384,128]{1,0:T(8,128)(2,1)S(1)}, u32[]{:S(2)}, u32[]{:S(2)}) collective-permute-start(bf16[384,128]{1,0:T(8,128)(2,1)S(1)} %get-tuple-element.58), channel_id=1, source_target_pairs={{4,8},{8,4},{12,16},{16,12},{20,24},{24,20},{28,32},{32,28},{36,40... | collective-permute-start | bytes 294920 | tf_op jit(solution)/shard_map/ppermute | solution.py:399
  40.0 1.9 %collective-permute-start.5 = (bf16[384,128]{1,0:T(8,128)(2,1)S(1)}, bf16[384,128]{1,0:T(8,128)(2,1)S(1)}, u32[]{:S(2)}, u32[]{:S(2)}) collective-permute-start(bf16[384,128]{1,0:T(8,128)(2,1)S(1)} %get-tuple-element.59), channel_id=1, source_target_pairs={{0,1},{1,0},{49,48},{48,49},{96,97},{97,96},{145,144},{144,145},{1... | collective-permute-start | bytes 294920 | tf_op jit(solution)/shard_map/ppermute | solution.py:403
  41.9 6.1 %collective-permute-start.6 = (bf16[384,128]{1,0:T(8,128)(2,1)S(1)}, bf16[384,128]{1,0:T(8,128)(2,1)S(1)}, u32[]{:S(2)}, u32[]{:S(2)}) collective-permute-start(bf16[384,128]{1,0:T(8,128)(2,1)S(1)} %get-tuple-element.60), channel_id=1, source_target_pairs={{1,49},{49,1},{48,96},{96,48},{97,145},{145,97},{144,192},{192,144... | collective-permute-start | bytes 294920 | tf_op jit(solution)/shard_map/ppermute | solution.py:402
  48.0 2.1 %shard_map.71 = (f32[1536,128]{1,0:T(8,128)S(1)}, f32[1536,128]{1,0:T(8,128)S(1)}, f32[1536,128]{1,0:T(8,128)S(1)}, f32[1536,128]{1,0:T(8,128)S(1)}, f32[1536,12...) custom-call(s32[4]{0:T(128)S(1)} %pad_add_fusion.pos, f32[1536,128]{1,0:T(8,128)S(1)} %get-tuple-element.49.e, ...), custom_call_target="tpu_custom_call" | custom-call | flops 20000000 | bytes 1000000 | tf_op jit(solution)/shard_map/pallas_call | solution.py:32
  50.3 1.4 %shard_map.72 = (f32[1536,128]{1,0:T(8,128)S(1)}, f32[128,128]{1,0:T(8,128)S(1)}, f32[4,192,128]{2,1,0:T(8,128)S(1)}, bf16[192,128]{1,0:T(8,128)(2,1)S(1)}, bf16...) custom-call(s32[4]{0:T(128)S(1)} %pad_add_fusion.pos, ...), custom_call_target="tpu_custom_call" | custom-call | flops 5000000 | bytes 1000000 | tf_op jit(solution)/shard_map/pallas_call | solution.py:32
  51.7 3.6 %collective-permute-start.7 = (f32[128,128]{1,0:T(8,128)S(1)}, f32[128,128]{1,0:T(8,128)S(1)}, u32[]{:S(2)}, u32[]{:S(2)}) collective-permute-start(f32[128,128]{1,0:T(8,128)S(1)} %get-tuple-element.62.sums), channel_id=1, source_target_pairs={{0,2},{1,3},{2,0},{3,1},{4,6},{5,7},{6,4},{7,5},{8,10},{9,11},{10,... | collective-permute-start | bytes 196616 | tf_op jit(solution)/shard_map/ppermute | solution.py:393
  55.3 1.9 %collective-permute-start.8 = (bf16[192,128]{1,0:T(8,128)(2,1)S(1)}, bf16[192,128]{1,0:T(8,128)(2,1)S(1)}, u32[]{:S(2)}, u32[]{:S(2)}) collective-permute-start(bf16[192,128]{1,0:T(8,128)(2,1)S(1)} %get-tuple-element.69), channel_id=1, source_target_pairs={{0,4},{4,0},{8,12},{12,8},{16,20},{20,16},{24,28},{28,24},{32,36},... | collective-permute-start | bytes 147464 | tf_op jit(solution)/shard_map/ppermute | solution.py:401
  57.2 4.0 %collective-permute-start.9 = (bf16[192,128]{1,0:T(8,128)(2,1)S(1)}, bf16[192,128]{1,0:T(8,128)(2,1)S(1)}, u32[]{:S(2)}, u32[]{:S(2)}) collective-permute-start(bf16[192,128]{1,0:T(8,128)(2,1)S(1)} %get-tuple-element.70), channel_id=1, source_target_pairs={{4,8},{8,4},{12,16},{16,12},{20,24},{24,20},{28,32},{32,28},{36,40... | collective-permute-start | bytes 147464 | tf_op jit(solution)/shard_map/ppermute | solution.py:399
  61.3 4.4 %collective-permute-start.10 = (bf16[192,128]{1,0:T(8,128)(2,1)S(1)}, bf16[192,128]{1,0:T(8,128)(2,1)S(1)}, u32[]{:S(2)}, u32[]{:S(2)}) collective-permute-start(bf16[192,128]{1,0:T(8,128)(2,1)S(1)} %get-tuple-element.71), channel_id=1, source_target_pairs={{0,1},{1,0},{49,48},{48,49},{96,97},{97,96},{145,144},{144,145},{1... | collective-permute-start | bytes 147464 | tf_op jit(solution)/shard_map/ppermute | solution.py:403
  65.6 6.4 %collective-permute-start.11 = (bf16[192,128]{1,0:T(8,128)(2,1)S(1)}, bf16[192,128]{1,0:T(8,128)(2,1)S(1)}, u32[]{:S(2)}, u32[]{:S(2)}) collective-permute-start(bf16[192,128]{1,0:T(8,128)(2,1)S(1)} %get-tuple-element.72), channel_id=1, source_target_pairs={{1,49},{49,1},{48,96},{96,48},{97,145},{145,97},{144,192},{192,144... | collective-permute-start | bytes 147464 | tf_op jit(solution)/shard_map/ppermute | solution.py:402
  72.0 2.0 %shard_map.73 = (f32[1536,128]{1,0:T(8,128)S(1)}, f32[1536,128]{1,0:T(8,128)S(1)}) custom-call(s32[4]{0:T(128)S(1)} %pad_add_fusion.pos, f32[1536,128]{1,0:T(8,128)S(1)} %get-tuple-element.61.e, f32[1536,128]{1,0:T(8,128)S(1)} %get-tuple-element.64.up_c, f32[1536,128]{1,0:T(8,128)S(1)} %get-tuple-element.65.east_c, f32[1536,128]{1,0:T(8,128)S(1)} %get-tuple-element.66.above_c), custom_call_target="tpu_custom_call" | custom-call | flops 20000000 | bytes 1000000 | tf_op jit(solution)/shard_map/pallas_call | solution.py:32
  75.4 1.9 %collective-permute-start.13 = (bf16[192,128]{1,0:T(8,128)(2,1)S(1)}, bf16[192,128]{1,0:T(8,128)(2,1)S(1)}, u32[]{:S(2)}, u32[]{:S(2)}) collective-permute-start(bf16[192,128]{1,0:T(8,128)(2,1)S(1)} %get-tuple-element.79), channel_id=1, source_target_pairs={{0,4},{4,0},{8,12},{12,8},{16,20},{20,16},{24,28},{28,24},{32,36},... | collective-permute-start | bytes 147464 | tf_op jit(solution)/shard_map/ppermute | solution.py:401
  77.4 4.4 %collective-permute-start.14 = (bf16[192,128]{1,0:T(8,128)(2,1)S(1)}, bf16[192,128]{1,0:T(8,128)(2,1)S(1)}, u32[]{:S(2)}, u32[]{:S(2)}) collective-permute-start(bf16[192,128]{1,0:T(8,128)(2,1)S(1)} %get-tuple-element.80), channel_id=1, source_target_pairs={{4,8},{8,4},{12,16},{16,12},{20,24},{24,20},{28,32},{32,28},{36,40... | collective-permute-start | bytes 147464 | tf_op jit(solution)/shard_map/ppermute | solution.py:399
  81.8 1.9 %collective-permute-start.15 = (bf16[192,128]{1,0:T(8,128)(2,1)S(1)}, bf16[192,128]{1,0:T(8,128)(2,1)S(1)}, u32[]{:S(2)}, u32[]{:S(2)}) collective-permute-start(bf16[192,128]{1,0:T(8,128)(2,1)S(1)} %get-tuple-element.81), channel_id=1, source_target_pairs={{0,1},{1,0},{49,48},{48,49},{96,97},{97,96},{145,144},{144,145},{1... | collective-permute-start | bytes 147464 | tf_op jit(solution)/shard_map/ppermute | solution.py:403
  83.8 5.1 %collective-permute-start.16 = (bf16[192,128]{1,0:T(8,128)(2,1)S(1)}, bf16[192,128]{1,0:T(8,128)(2,1)S(1)}, u32[]{:S(2)}, u32[]{:S(2)}) collective-permute-start(bf16[192,128]{1,0:T(8,128)(2,1)S(1)} %get-tuple-element.82), channel_id=1, source_target_pairs={{1,49},{49,1},{48,96},{96,48},{97,145},{145,97},{144,192},{192,144... | collective-permute-start | bytes 147464 | tf_op jit(solution)/shard_map/ppermute | solution.py:402
  88.9 3.1 %collective-permute-start.12 = (f32[64,128]{1,0:T(8,128)S(1)}, f32[64,128]{1,0:T(8,128)S(1)}, u32[]{:S(2)}, u32[]{:S(2)}) collective-permute-start(f32[64,128]{1,0:T(8,128)S(1)} %get-tuple-element.76.part), channel_id=1, source_target_pairs={{0,2},{1,3},{2,0},{3,1},{4,6},{5,7},{6,4},{7,5},{8,10},{9,11},{10,... | collective-permute-start | bytes 98312 | tf_op jit(solution)/shard_map/ppermute | solution.py:393
  92.0 2.0 %shard_map.75 = (f32[1536,128]{1,0:T(8,128)S(1)}, f32[1536,128]{1,0:T(8,128)S(1)}) custom-call(s32[4]{0:T(128)S(1)} %pad_add_fusion.pos, f32[1536,128]{1,0:T(8,128)S(1)} %get-tuple-element.73.e, f32[1536,128]{1,0:T(8,128)S(1)} %get-tuple-element.64.up_c, f32[1536,128]{1,0:T(8,128)S(1)} %get-tuple-element.65.east_c, f32[1536,128]{1,0:T(8,128)S(1)} %get-tuple-element.66.above_c), custom_call_target="tpu_custom_call" | custom-call | flops 20000000 | bytes 1000000 | tf_op jit(solution)/shard_map/pallas_call | solution.py:32
  94.5 1.4 %shard_map.76 = (f32[768,128]{1,0:T(8,128)S(1)}, f32[960,128]{1,0:T(8,128)S(1)}, f32[64,128]{1,0:T(8,128)S(1)}) custom-call(s32[4]{0:T(128)S(1)} %pad_add_fusion.pos, f32[1536,128]{1,0:T(8,128)S(1)} %get-tuple-element.73.e, f32[1536,128]{1,0:T(8,128)S(1)} %get-tuple-element.53.e01, f32[1536,128]{1,0:T(8,128)S(1)} %get-tuple-element.51.kap, ...), custom_call_target="tpu_custom_call" | custom-call | flops 5000000 | bytes 1000000 | tf_op jit(solution)/shard_map/pallas_call | solution.py:32
  95.9 1.9 %collective-permute-start.17 = (f32[960,128]{1,0:T(8,128)S(1)}, f32[960,128]{1,0:T(8,128)S(1)}, u32[]{:S(2)}, u32[]{:S(2)}) collective-permute-start(f32[960,128]{1,0:T(8,128)S(1)} %get-tuple-element.84.send), channel_id=1, source_target_pairs={{0,1},{1,0},{2,3},{3,2},{4,5},{5,4},{6,7},{7,6},{8,9},{9,8},{10,11... | collective-permute-start | bytes 1474568 | tf_op jit(solution)/shard_map/ppermute | solution.py:393
  97.8 4.3 %collective-permute-start.19 = (f32[64,128]{1,0:T(8,128)S(1)}, f32[64,128]{1,0:T(8,128)S(1)}, u32[]{:S(2)}, u32[]{:S(2)}) collective-permute-start(f32[64,128]{1,0:T(8,128)S(1)} %get-tuple-element.85), channel_id=1, source_target_pairs={{0,3},{1,2},{2,1},{3,0},{4,7},{5,6},{6,5},{7,4},{8,11},{9,10},{10,... | collective-permute-start | bytes 98312 | tf_op jit(solution)/shard_map/ppermute | solution.py:393
  102.1 2.1 %collective-permute-start.18 = (f32[64,128]{1,0:T(8,128)S(1)}, f32[64,128]{1,0:T(8,128)S(1)}, u32[]{:S(2)}, u32[]{:S(2)}) collective-permute-start(f32[64,128]{1,0:T(8,128)S(1)} %get-tuple-element.85), channel_id=1, source_target_pairs={{0,2},{1,3},{2,0},{3,1},{4,6},{5,7},{6,4},{7,5},{8,10},{9,11},{10,... | collective-permute-start | bytes 98312 | tf_op jit(solution)/shard_map/ppermute | solution.py:393
  104.2 7.1 %collective-permute-done.19.far = f32[64,128]{1,0:T(8,128)S(1)} collective-permute-done((f32[64,128]{1,0:T(8,128)S(1)}, f32[64,128]{1,0:T(8,128)S(1)}, u32[]{:S(2)}, u32[]{:S(2)}) %collective-permute-start.19) | collective-permute-done | bytes 32800 | tf_op jit(solution)/shard_map/ppermute | solution.py:393
  111.3 1.5 %shard_map.77 = (f32[1536,128]{1,0:T(8,128)}, f32[128,128]{1,0:T(8,128)}) custom-call(s32[4]{0:T(128)S(1)} %pad_add_fusion.pos, f32[768,128]{1,0:T(8,128)S(1)} %get-tuple-element.83.eown, f32[960,128]{1,0:T(8,128)S(1)} %get-tuple-element.84.send, f32[960,128]{1,0:T(8,128)S(1)} %collective-permute-done.17.pair, f32[64,128]{1,0:T(8,128)S(1)} %collective-permute-done.18.near, ...), custom_call_target="tpu_custom_call" | custom-call | flops 1000000 | bytes 1000000 | tf_op jit(solution)/shard_map/pallas_call | solution.py:32
  (26 shorter events, 2.1 us)
Async XLA Ops:
  0.7 13.6 %copy-start.2 = (bf16[32,48]{1,0:T(8,128)(2,1)S(1)}, bf16[32,48]{1,0:T(8,128)(2,1)}, u32[]{:S(2)}) copy-start(bf16[32,48]{1,0:T(8,128)(2,1)} %param.6) | copy-start | bytes 9220
  2.5 18.1 %collective-permute-start = (bf16[1328,128]{1,0:T(8,128)(2,1)S(1)}, bf16[1328,128]{1,0:T(8,128)(2,1)S(1)}, u32[]{:S(2)}, u32[]{:S(2)}) collective-permute-start(bf16[1328,128]{1,0:T(8,128)(2,1)S(1)} %get-tuple-element.46), channel_id=1, source_target_pairs={{0,1},{1,0},{2,3},{3,2},{4,5},{5,4},{6,7},{7,6},{8,9},{9,8},{10,11... | collective-permute-start | bytes 1019912 | tf_op jit(solution)/shard_map/ppermute | solution.py:393
  6.6 14.1 %collective-permute-start.1 = (bf16[8,64,128]{2,1,0:T(8,128)(2,1)S(1)}, bf16[8,64,128]{2,1,0:T(8,128)(2,1)S(1)}, u32[]{:S(2)}, u32[]{:S(2)}) collective-permute-start(bf16[8,64,128]{2,1,0:T(8,128)(2,1)S(1)} %get-tuple-element.47), channel_id=1, source_target_pairs={{0,3},{1,2},{2,1},{3,0},{4,7},{5,6},{6,5},{7,4},{8,11},{9,10},{10,... | collective-permute-start | bytes 393224 | tf_op jit(solution)/shard_map/ppermute | solution.py:393
  12.1 13.1 %collective-permute-start.2 = (bf16[8,64,128]{2,1,0:T(8,128)(2,1)S(1)}, bf16[8,64,128]{2,1,0:T(8,128)(2,1)S(1)}, u32[]{:S(2)}, u32[]{:S(2)}) collective-permute-start(bf16[8,64,128]{2,1,0:T(8,128)(2,1)S(1)} %get-tuple-element.45.mine), channel_id=1, source_target_pairs={{0,2},{1,3},{2,0},{3,1},{4,6},{5,7},{6,4},{7,5},{8,10},{9,11},{10,... | collective-permute-start | bytes 393224 | tf_op jit(solution)/shard_map/ppermute | solution.py:393
  14.4 6.3 %copy-start.1 = (f32[12]{0:T(128)S(1)}, f32[12]{0:T(128)}, u32[]{:S(2)}) copy-start(f32[12]{0:T(128)} %planck.3) | copy-start | bytes 148
  26.6 23.5 %collective-permute-start.3 = (bf16[384,128]{1,0:T(8,128)(2,1)S(1)}, bf16[384,128]{1,0:T(8,128)(2,1)S(1)}, u32[]{:S(2)}, u32[]{:S(2)}) collective-permute-start(bf16[384,128]{1,0:T(8,128)(2,1)S(1)} %get-tuple-element.57), channel_id=1, source_target_pairs={{0,4},{4,0},{8,12},{12,8},{16,20},{20,16},{24,28},{28,24},{32,36},... | collective-permute-start | bytes 294920 | tf_op jit(solution)/shard_map/ppermute | solution.py:401
  29.0 21.0 %collective-permute-start.4 = (bf16[384,128]{1,0:T(8,128)(2,1)S(1)}, bf16[384,128]{1,0:T(8,128)(2,1)S(1)}, u32[]{:S(2)}, u32[]{:S(2)}) collective-permute-start(bf16[384,128]{1,0:T(8,128)(2,1)S(1)} %get-tuple-element.58), channel_id=1, source_target_pairs={{4,8},{8,4},{12,16},{16,12},{20,24},{24,20},{28,32},{32,28},{36,40... | collective-permute-start | bytes 294920 | tf_op jit(solution)/shard_map/ppermute | solution.py:399
  40.0 10.1 %collective-permute-start.5 = (bf16[384,128]{1,0:T(8,128)(2,1)S(1)}, bf16[384,128]{1,0:T(8,128)(2,1)S(1)}, u32[]{:S(2)}, u32[]{:S(2)}) collective-permute-start(bf16[384,128]{1,0:T(8,128)(2,1)S(1)} %get-tuple-element.59), channel_id=1, source_target_pairs={{0,1},{1,0},{49,48},{48,49},{96,97},{97,96},{145,144},{144,145},{1... | collective-permute-start | bytes 294920 | tf_op jit(solution)/shard_map/ppermute | solution.py:403
  41.9 8.4 %collective-permute-start.6 = (bf16[384,128]{1,0:T(8,128)(2,1)S(1)}, bf16[384,128]{1,0:T(8,128)(2,1)S(1)}, u32[]{:S(2)}, u32[]{:S(2)}) collective-permute-start(bf16[384,128]{1,0:T(8,128)(2,1)S(1)} %get-tuple-element.60), channel_id=1, source_target_pairs={{1,49},{49,1},{48,96},{96,48},{97,145},{145,97},{144,192},{192,144... | collective-permute-start | bytes 294920 | tf_op jit(solution)/shard_map/ppermute | solution.py:402
  48.0 2.3 %copy-start = (f32[16,8,128]{2,1,0:T(8,128)S(1)}, f32[16,8,128]{2,1,0:T(8,128)}, u32[]{:S(2)}) copy-start(f32[16,8,128]{2,1,0:T(8,128)} %param.9) | copy-start | bytes 196612
  51.7 22.4 %collective-permute-start.7 = (f32[128,128]{1,0:T(8,128)S(1)}, f32[128,128]{1,0:T(8,128)S(1)}, u32[]{:S(2)}, u32[]{:S(2)}) collective-permute-start(f32[128,128]{1,0:T(8,128)S(1)} %get-tuple-element.62.sums), channel_id=1, source_target_pairs={{0,2},{1,3},{2,0},{3,1},{4,6},{5,7},{6,4},{7,5},{8,10},{9,11},{10,... | collective-permute-start | bytes 196616 | tf_op jit(solution)/shard_map/ppermute | solution.py:393
  55.3 18.7 %collective-permute-start.8 = (bf16[192,128]{1,0:T(8,128)(2,1)S(1)}, bf16[192,128]{1,0:T(8,128)(2,1)S(1)}, u32[]{:S(2)}, u32[]{:S(2)}) collective-permute-start(bf16[192,128]{1,0:T(8,128)(2,1)S(1)} %get-tuple-element.69), channel_id=1, source_target_pairs={{0,4},{4,0},{8,12},{12,8},{16,20},{20,16},{24,28},{28,24},{32,36},... | collective-permute-start | bytes 147464 | tf_op jit(solution)/shard_map/ppermute | solution.py:401
  57.2 16.8 %collective-permute-start.9 = (bf16[192,128]{1,0:T(8,128)(2,1)S(1)}, bf16[192,128]{1,0:T(8,128)(2,1)S(1)}, u32[]{:S(2)}, u32[]{:S(2)}) collective-permute-start(bf16[192,128]{1,0:T(8,128)(2,1)S(1)} %get-tuple-element.70), channel_id=1, source_target_pairs={{4,8},{8,4},{12,16},{16,12},{20,24},{24,20},{28,32},{32,28},{36,40... | collective-permute-start | bytes 147464 | tf_op jit(solution)/shard_map/ppermute | solution.py:399
  61.3 12.8 %collective-permute-start.10 = (bf16[192,128]{1,0:T(8,128)(2,1)S(1)}, bf16[192,128]{1,0:T(8,128)(2,1)S(1)}, u32[]{:S(2)}, u32[]{:S(2)}) collective-permute-start(bf16[192,128]{1,0:T(8,128)(2,1)S(1)} %get-tuple-element.71), channel_id=1, source_target_pairs={{0,1},{1,0},{49,48},{48,49},{96,97},{97,96},{145,144},{144,145},{1... | collective-permute-start | bytes 147464 | tf_op jit(solution)/shard_map/ppermute | solution.py:403
  65.6 8.4 %collective-permute-start.11 = (bf16[192,128]{1,0:T(8,128)(2,1)S(1)}, bf16[192,128]{1,0:T(8,128)(2,1)S(1)}, u32[]{:S(2)}, u32[]{:S(2)}) collective-permute-start(bf16[192,128]{1,0:T(8,128)(2,1)S(1)} %get-tuple-element.72), channel_id=1, source_target_pairs={{1,49},{49,1},{48,96},{96,48},{97,145},{145,97},{144,192},{192,144... | collective-permute-start | bytes 147464 | tf_op jit(solution)/shard_map/ppermute | solution.py:402
  75.4 19.0 %collective-permute-start.13 = (bf16[192,128]{1,0:T(8,128)(2,1)S(1)}, bf16[192,128]{1,0:T(8,128)(2,1)S(1)}, u32[]{:S(2)}, u32[]{:S(2)}) collective-permute-start(bf16[192,128]{1,0:T(8,128)(2,1)S(1)} %get-tuple-element.79), channel_id=1, source_target_pairs={{0,4},{4,0},{8,12},{12,8},{16,20},{20,16},{24,28},{28,24},{32,36},... | collective-permute-start | bytes 147464 | tf_op jit(solution)/shard_map/ppermute | solution.py:401
  77.4 17.1 %collective-permute-start.14 = (bf16[192,128]{1,0:T(8,128)(2,1)S(1)}, bf16[192,128]{1,0:T(8,128)(2,1)S(1)}, u32[]{:S(2)}, u32[]{:S(2)}) collective-permute-start(bf16[192,128]{1,0:T(8,128)(2,1)S(1)} %get-tuple-element.80), channel_id=1, source_target_pairs={{4,8},{8,4},{12,16},{16,12},{20,24},{24,20},{28,32},{32,28},{36,40... | collective-permute-start | bytes 147464 | tf_op jit(solution)/shard_map/ppermute | solution.py:399
  81.8 12.6 %collective-permute-start.15 = (bf16[192,128]{1,0:T(8,128)(2,1)S(1)}, bf16[192,128]{1,0:T(8,128)(2,1)S(1)}, u32[]{:S(2)}, u32[]{:S(2)}) collective-permute-start(bf16[192,128]{1,0:T(8,128)(2,1)S(1)} %get-tuple-element.81), channel_id=1, source_target_pairs={{0,1},{1,0},{49,48},{48,49},{96,97},{97,96},{145,144},{144,145},{1... | collective-permute-start | bytes 147464 | tf_op jit(solution)/shard_map/ppermute | solution.py:403
  83.8 10.7 %collective-permute-start.16 = (bf16[192,128]{1,0:T(8,128)(2,1)S(1)}, bf16[192,128]{1,0:T(8,128)(2,1)S(1)}, u32[]{:S(2)}, u32[]{:S(2)}) collective-permute-start(bf16[192,128]{1,0:T(8,128)(2,1)S(1)} %get-tuple-element.82), channel_id=1, source_target_pairs={{1,49},{49,1},{48,96},{96,48},{97,145},{145,97},{144,192},{192,144... | collective-permute-start | bytes 147464 | tf_op jit(solution)/shard_map/ppermute | solution.py:402
  88.9 5.6 %collective-permute-start.12 = (f32[64,128]{1,0:T(8,128)S(1)}, f32[64,128]{1,0:T(8,128)S(1)}, u32[]{:S(2)}, u32[]{:S(2)}) collective-permute-start(f32[64,128]{1,0:T(8,128)S(1)} %get-tuple-element.76.part), channel_id=1, source_target_pairs={{0,2},{1,3},{2,0},{3,1},{4,6},{5,7},{6,4},{7,5},{8,10},{9,11},{10,... | collective-permute-start | bytes 98312 | tf_op jit(solution)/shard_map/ppermute | solution.py:393
  95.9 15.5 %collective-permute-start.17 = (f32[960,128]{1,0:T(8,128)S(1)}, f32[960,128]{1,0:T(8,128)S(1)}, u32[]{:S(2)}, u32[]{:S(2)}) collective-permute-start(f32[960,128]{1,0:T(8,128)S(1)} %get-tuple-element.84.send), channel_id=1, source_target_pairs={{0,1},{1,0},{2,3},{3,2},{4,5},{5,4},{6,7},{7,6},{8,9},{9,8},{10,11... | collective-permute-start | bytes 1474568 | tf_op jit(solution)/shard_map/ppermute | solution.py:393
  97.8 13.6 %collective-permute-start.19 = (f32[64,128]{1,0:T(8,128)S(1)}, f32[64,128]{1,0:T(8,128)S(1)}, u32[]{:S(2)}, u32[]{:S(2)}) collective-permute-start(f32[64,128]{1,0:T(8,128)S(1)} %get-tuple-element.85), channel_id=1, source_target_pairs={{0,3},{1,2},{2,1},{3,0},{4,7},{5,6},{6,5},{7,4},{8,11},{9,10},{10,... | collective-permute-start | bytes 98312 | tf_op jit(solution)/shard_map/ppermute | solution.py:393
  102.1 9.2 %collective-permute-start.18 = (f32[64,128]{1,0:T(8,128)S(1)}, f32[64,128]{1,0:T(8,128)S(1)}, u32[]{:S(2)}, u32[]{:S(2)}) collective-permute-start(f32[64,128]{1,0:T(8,128)S(1)} %get-tuple-element.85), channel_id=1, source_target_pairs={{0,2},{1,3},{2,0},{3,1},{4,6},{5,7},{6,4},{7,5},{8,10},{9,11},{10,... | collective-permute-start | bytes 98312 | tf_op jit(solution)/shard_map/ppermute | solution.py:393

commit v4 on v3

--- a/solution.py
+++ b/solution.py
@@ -26,7 +26,7 @@
 CELLS = TILES * LAT
 
 
-def call(kernel, outs, args, smem=0, scratch=(), flops=1_000_000, space=VMEM):
+def call(kernel, outs, args, smem=0, scratch=(), flops=1_000_000, space=VMEM, aliases=()):
     specs = [pl.BlockSpec(memory_space=SMEM)] * smem
     specs += [pl.BlockSpec(memory_space=space)] * (len(args) - smem)
     return pl.pallas_call(
@@ -35,6 +35,7 @@
         in_specs=specs,
         out_specs=[pl.BlockSpec(memory_space=VMEM)] * len(outs),
         scratch_shapes=list(scratch),
+        input_output_aliases=dict(aliases),
         cost_estimate=pl.CostEstimate(flops=flops, bytes_accessed=1_000_000, transcendentals=0),
         compiler_params=pltpu.CompilerParams(vmem_limit_bytes=16 << 20),
     )(*args)
@@ -133,16 +134,16 @@
     return acc
 
 
-def early_kernel(pos, tab, planck, mine, pair, far, eown, kap, e, share, wide):
+def early_kernel(pos, tab, planck, mine, pair, near, eown, kap, e, share, wide):
     place = pos[2]
     slot = place % 2
     for b in range(BINS):
         wide[pl.ds(b * N, N), :] = mine[b].astype(F32)
         wide[pl.ds(SIZE + b * N, N), :] = pair[pl.ds(b * N, N), :].astype(F32)
-        wide[pl.ds(2 * SIZE + b * N, N), :] = far[b].astype(F32)
+        wide[pl.ds(2 * SIZE + b * N, N), :] = near[b].astype(F32)
 
     def one(g, carry):
-        acc = gather_bins(tab, wide, place, (0, 1, 3), g, [None] * ROWS)
+        acc = gather_bins(tab, wide, place, (0, 1, 2), g, [None] * ROWS)
         for r in range(ROWS):
             kap[tile(g * ROWS + r), :] = acc[r]
         return carry
@@ -161,14 +162,14 @@
     share[1 - slot] = pieces[0] + pieces[1] + pieces[2]
 
 
-def late_kernel(pos, tab, part, near, e, kap, t1, t2, r1, r2, wide):
+def late_kernel(pos, tab, part, far, e, kap, t1, t2, r1, r2, wide):
     place = pos[2]
     for b in range(BINS):
-        wide[pl.ds(b * N, N), :] = near[b].astype(F32)
+        wide[pl.ds(b * N, N), :] = far[b].astype(F32)
 
     def one(g, carry):
         acc = [part[tile(g * ROWS + r), :] for r in range(ROWS)]
-        acc = gather_bins(tab, wide, place, (2,), g, acc)
+        acc = gather_bins(tab, wide, place, (3,), g, acc)
         for r in range(ROWS):
             kap[tile(g * ROWS + r), :] = acc[r]
         return carry
@@ -193,12 +194,13 @@
     return spread(share[part, pl.ds(g - part * OWN, 1), :])
 
 
-def inner_body(e, coefs, flux, weight, prepare):
+def inner_body(e, kap, numer, denom, prepare):
     def one(g, carry):
         base = g * ROWS
         tiles = [e[tile(base + r), :] for r in range(ROWS)]
-        coef = prepare(g, base, tiles) if prepare else [[c[tile(base + r), :] for c in coefs] for r in range(ROWS)]
-        ws, fs = [], []
+        ks = [kap[tile(base + r), :] for r in range(ROWS)]
+        coef, olds = prepare(g, base, tiles, ks)
+        out = []
         for r in range(ROWS):
             here = tiles[r]
             c_up, c_east, c_above = coef[r]
@@ -211,24 +213,22 @@
             if r + 1 < ROWS:
                 w_below, f_below = face(here, tiles[r + 1], c_above)
                 w, f = w + w_below, f + f_below
-            ws.append(w)
-            fs.append(f)
-        for r in range(ROWS):
-            weight[tile(base + r), :] = ws[r]
-            flux[tile(base + r), :] = fs[r]
+            out.append((olds[r] + (here * w + f), SCALE + ks[r] + w))
+        for r in range(ROWS):
+            numer[tile(base + r), :], denom[tile(base + r), :] = out[r]
         return carry
 
     lax.fori_loop(0, GROUPS, one, 0, unroll=UNROLL)
 
 
-def inner_first(pos, e, kap, share, flux, weight, up_c, east_c, above_c, e01, ssum):
+def inner_first(pos, e, kap, share, numer, denom, up_c, east_c, above_c, e01, ssum):
     ssum[...] = jnp.zeros_like(ssum)
     top = lax.broadcasted_iota(jnp.int32, (LAT, LANES), 0) == LAT - 1
 
-    def prepare(g, base, tiles):
-        ks = [kap[tile(base + r), :] for r in range(ROWS)]
+    def prepare(g, base, tiles, ks):
         sums = [ssum[tile(r), :] for r in range(ROWS)]
         share_row = share_of(share, g)
+        olds = [SCALE * x for x in tiles]
         out = []
         for r in range(ROWS):
             k = ks[r]
@@ -240,15 +240,19 @@
             up_c[tile(i), :], east_c[tile(i), :] = out[r][:2]
             if r + 1 < ROWS:
                 above_c[tile(i), :] = out[r][2]
-            e01[tile(i), :] = SCALE * tiles[r]
+            e01[tile(i), :] = olds[r]
             ssum[tile(r), :] = sums[r] + ks[r] * share_row
-        return out
-
-    inner_body(e, None, flux, weight, prepare)
-
-
-def inner_next(pos, e, up_c, east_c, above_c, flux, weight):
-    inner_body(e, (up_c, east_c, above_c), flux, weight, None)
+        return out, olds
+
+    inner_body(e, kap, numer, denom, prepare)
+
+
+def inner_next(pos, e, kap, e01, up_c, east_c, above_c, numer, denom):
+    def prepare(g, base, tiles, ks):
+        at = [tile(base + r) for r in range(ROWS)]
+        return [(up_c[i, :], east_c[i, :], above_c[i, :]) for i in at], [e01[i, :] for i in at]
+
+    inner_body(e, kap, numer, denom, prepare)
 
 
 def unpack_halos(pos, slabs, at, halo):
@@ -260,41 +264,33 @@
     halo[2 + part] = slabs[3][rows, :].astype(F32)
 
 
-def outer_body(e, e01, kap, share, temp4, halo, edge, flux, weight, enew, ksum, numer, denom):
-    def one(g, carry):
-        base = g * ROWS
+def outer_body(e, kap, share, temp4, halo, edge, numer, denom, enew, ksum):
+    def close(g, carry):
+        lows = tile(g)
+        base = g * ROWS * LAT
+        places = [pl.ds(base, ROWS, stride=LAT), pl.ds(base + LAT - 1, ROWS, stride=LAT)]
+        places += [tile(g * ROWS), tile(g * ROWS + ROWS - 1)]
+        pasts = [e[i, :] for i in places]
+        outs = [halo[j, lows, :] for j in range(4)]
+        ws = [face(pasts[j], outs[j], edge[j, lows, :])[0] for j in range(4)]
+        for j, i in enumerate(places):
+            numer[i, :] = numer[i, :] + ws[j] * outs[j]
+            denom[i, :] = denom[i, :] + ws[j]
+        return carry
+
+    lax.fori_loop(0, GROUPS, close, 0, unroll=8)
+
+    def finish(g, sums):
         row_share = share_of(share, g)
-        refs = (e, kap, weight, flux, e01)
-        rows = [[x[tile(base + r), :] for x in refs] + [temp4[tile(r), :]] for r in range(ROWS)]
-        ends = {at: (halo[j, tile(g), :], edge[j, tile(g), :]) for j, at in ((2, 0), (3, ROWS - 1))}
-        strips = [pl.ds(base * LAT + at, ROWS, stride=LAT) for at in (0, LAT - 1)]
-        strips = [(strip, e[strip, :]) for strip in strips]
-        out = []
-        for r in range(ROWS):
-            here, k, w, f, old, t4 = rows[r]
-            if r in ends:
-                w_out, f_out = face(here, *ends[r])
-                w, f = w + w_out, f + f_out
-            out.append((old + k * (row_share * t4) + (here * w + f), SCALE + k + w))
-        for r in range(ROWS):
-            numer[tile(base + r), :], denom[tile(base + r), :] = out[r]
-        for j, (strip, past) in enumerate(strips):
-            w, _ = face(past, halo[j, tile(g), :], edge[j, tile(g), :])
-            numer[strip, :] = numer[strip, :] + w * halo[j, tile(g), :]
-            denom[strip, :] = denom[strip, :] + w
-        return carry
-
-    lax.fori_loop(0, GROUPS, one, 0, unroll=8)
-
-    def two(g, sums):
         at = [tile(g * ROWS + r) for r in range(ROWS)]
-        fresh = [numer[i, :] / denom[i, :] for i in at]
-        sums = tuple(sums[r] + kap[at[r], :] * fresh[r] for r in range(ROWS))
+        ks = [kap[i, :] for i in at]
+        fresh = [(numer[at[r], :] + ks[r] * (row_share * temp4[tile(r), :])) / denom[at[r], :] for r in range(ROWS)]
+        sums = tuple(sums[r] + ks[r] * fresh[r] for r in range(ROWS))
         for r in range(ROWS):
             enew[at[r], :] = fresh[r]
         return sums
 
-    sums = lax.fori_loop(0, GROUPS, two, (jnp.zeros((LAT, LANES), F32),) * ROWS, unroll=8)
+    sums = lax.fori_loop(0, GROUPS, finish, (jnp.zeros((LAT, LANES), F32),) * ROWS, unroll=8)
     for r in range(ROWS):
         ksum[tile(r), :] = sums[r]
 
@@ -308,9 +304,9 @@
     return HEAT * told + 3.0 * stot * (cube * t), HEAT + 4.0 * stot * cube
 
 
-def outer_first(pos, e, e01, kap, share, told, ssum, flux, weight, h0, h1, h2, h3, *refs):
-    enew, sums, edge, t1, t2, r1, r2 = refs[:7]
-    temp4, halo, numer, denom = refs[7:]
+def outer_first(pos, e, kap, share, told, ssum, numer_in, denom_in, h0, h1, h2, h3, *refs):
+    enew, sums, edge, t1, t2, r1, r2, numer, denom = refs[:9]
+    temp4, halo = refs[9:]
     slabs = (h0, h1, h2, h3)
     unpack_halos(pos, slabs, TILES, halo)
     for j, at in ((0, 0), (1, LAT - 1)):
@@ -321,14 +317,14 @@
     unpack_halos(pos, slabs, 0, halo)
     t = own_rows(pos, told)
     temp4[...] = t * t * t * t
-    outer_body(e, e01, kap, share, temp4, halo, edge, flux, weight, enew, sums.at[pl.ds(0, N)], numer, denom)
+    outer_body(e, kap, share, temp4, halo, edge, numer, denom, enew, sums.at[pl.ds(0, N)])
     sums[pl.ds(N, N), :] = ssum[...]
     write_slabs(pos, enew, 0, t1, t2, r1, r2)
 
 
-def outer_middle(pos, e, e01, kap, share, told, sums, got, edge, flux, weight, h0, h1, h2, h3, *refs):
-    enew, ksum, tnow, stot, t1, t2, r1, r2 = refs[:8]
-    temp4, halo, numer, denom = refs[8:]
+def outer_middle(pos, e, kap, share, told, sums, got, edge, numer_in, denom_in, h0, h1, h2, h3, *refs):
+    enew, ksum, tnow, stot, t1, t2, r1, r2, numer, denom = refs[:10]
+    temp4, halo = refs[10:]
     unpack_halos(pos, (h0, h1, h2, h3), 0, halo)
     both = (sums[...] + got[...]) / SCALE
     s = both[N:]
@@ -338,20 +334,20 @@
     t = (up + both[:N]) / down
     tnow[...] = t
     temp4[...] = t * t * t * t
-    outer_body(e, e01, kap, share, temp4, halo, edge, flux, weight, enew, ksum, numer, denom)
+    outer_body(e, kap, share, temp4, halo, edge, numer, denom, enew, ksum)
     write_slabs(pos, enew, 0, t1, t2, r1, r2)
 
 
-def outer_last(pos, e, e01, kap, share, told, tprev, stot, part, got, edge, flux, weight, h0, h1, h2, h3, *refs):
-    eown, send, ksum = refs[:3]
-    temp4, halo, numer, denom, enew = refs[3:]
+def outer_last(pos, e, kap, share, told, tprev, stot, part, got, edge, numer_in, denom_in, h0, h1, h2, h3, *refs):
+    eown, send, ksum, numer, denom = refs[:5]
+    temp4, halo, enew = refs[5:]
     unpack_halos(pos, (h0, h1, h2, h3), 0, halo)
     s = stot[...]
     old = own_rows(pos, told)
     above, below = terms(old, tprev[...], s)
     t = (above + (part[...] + got[...]) / SCALE) / below
     temp4[...] = t * t * t * t
-    outer_body(e, e01, kap, share, temp4, halo, edge, flux, weight, enew, ksum, numer, denom)
+    outer_body(e, kap, share, temp4, halo, edge, numer, denom, enew, ksum)
     slot = pos[2] % 2
     eown[...] = enew[pl.ds(pl.multiple_of(slot * PART, PART), PART), :]
     send[pl.ds(0, PART), :] = enew[pl.ds(pl.multiple_of((1 - slot) * PART, PART), PART), :]
@@ -413,7 +409,7 @@
     told = temp_old.reshape(-1, LANES)
     tab = table.astype(F32).reshape(-1)
     slabs = [held((TILES, LANES), BF)] * 4
-    scratch = [VMEM((N, LANES), F32), VMEM((4, TILES, LANES), F32), VMEM((CELLS, LANES), F32), VMEM((CELLS, LANES), F32)]
+    scratch = [VMEM((N, LANES), F32), VMEM((4, TILES, LANES), F32)]
     full = held((CELLS, LANES))
     sheet = held((N, LANES))
     block = held((BINS, N, LANES), BF)
@@ -429,43 +425,45 @@
     far = xor(far, 3)
     early, e, share = call(
         early_kernel, [full, full, held((2, 2 * LAT, LANES))],
-        (pos, tab, planck, keep(mine), keep(pair), keep(far), keep(eown)), smem=3,
+        (pos, tab, planck, keep(mine), keep(pair), keep(near), keep(eown)), smem=3,
         scratch=[VMEM((3 * SIZE, LANES), F32)], flops=20_000_000,
     )
     e = keep(e)
     kap, *both = call(
         late_kernel,
         [full] + [held((2 * TILES, LANES), BF)] * 4,
-        (pos, tab, keep(early), keep(near), e), smem=2,
+        (pos, tab, keep(early), keep(far), e), smem=2,
         scratch=[VMEM((SIZE, LANES), F32)], flops=5_000_000,
     )
     kap, share = keep(kap), keep(share)
     halos, _ = swap_halos(both)
-    flux, weight, *coefs, e01, ssum = call(
+    numer, denom, *coefs, e01, ssum = call(
         inner_first, [full] * 6 + [sheet], (pos, e, kap, share), smem=1, flops=20_000_000,
     )
     coefs = [keep(x) for x in coefs]
     e01 = keep(e01)
     e, sums, edge, *rest = call(
-        outer_first, [full, held((2 * N, LANES)), held((4, TILES, LANES))] + slabs,
-        (pos, e, e01, kap, share, told, keep(ssum), keep(flux), keep(weight), *halos), smem=1,
-        scratch=scratch, flops=5_000_000,
-    )
+        outer_first, [full, held((2 * N, LANES)), held((4, TILES, LANES))] + slabs + [full, full],
+        (pos, e, kap, share, told, keep(ssum), keep(numer), keep(denom), *halos), smem=1,
+        scratch=scratch, flops=5_000_000, aliases=((6, 7), (7, 8)),
+    )
+    rest = rest[:4]
     e, edge, sums = keep(e), keep(edge), keep(sums)
     halos, got = swap_halos(rest, sums)
-    flux, weight = call(inner_next, [full] * 2, (pos, e, *coefs), smem=1, flops=20_000_000)
+    numer, denom = call(inner_next, [full] * 2, (pos, e, kap, e01, *coefs), smem=1, flops=20_000_000)
     e, part, temp, stot, *rest = call(
-        outer_middle, [full, sheet, sheet, sheet] + slabs,
-        (pos, e, e01, kap, share, told, sums, got, edge, keep(flux), keep(weight), *halos), smem=1,
-        scratch=scratch, flops=5_000_000,
-    )
+        outer_middle, [full, sheet, sheet, sheet] + slabs + [full, full],
+        (pos, e, kap, share, told, sums, got, edge, keep(numer), keep(denom), *halos), smem=1,
+        scratch=scratch, flops=5_000_000, aliases=((8, 8), (9, 9)),
+    )
+    rest = rest[:4]
     e, part = keep(e), keep(part)
     halos, got = swap_halos(rest, part)
-    flux, weight = call(inner_next, [full] * 2, (pos, e, *coefs), smem=1, flops=20_000_000)
-    eown, send, part = call(
-        outer_last, [held((PART, LANES)), held((PART + 3 * N, LANES)), sheet],
-        (pos, e, e01, kap, share, told, keep(temp), keep(stot), part, got, edge, keep(flux), keep(weight), *halos), smem=1,
-        scratch=scratch + [VMEM((CELLS, LANES), F32)], flops=5_000_000,
+    numer, denom = call(inner_next, [full] * 2, (pos, e, kap, e01, *coefs), smem=1, flops=20_000_000)
+    eown, send, part, _, _ = call(
+        outer_last, [held((PART, LANES)), held((PART + 3 * N, LANES)), sheet, full, full],
+        (pos, e, kap, share, told, keep(temp), keep(stot), part, got, edge, keep(numer), keep(denom), *halos), smem=1,
+        scratch=scratch + [VMEM((CELLS, LANES), F32)], flops=5_000_000, aliases=((10, 3), (11, 4)),
     )
     pair = xor(send, 1)
     far = xor(part, 3)

time: 114 us -> 113 us (level)
  waiting for transfers between devices: 16.2 us -> 14.3 us
    ppermute x8, waiting for transfers between devices: 16 us -> 14.3 us  [xor(): return lax.ppermute(x, 'group', [(i, i ^ k) for i in range(4)])]
  transfers between devices with their start and end apart: 20 -> 20, of which waited for: 5 -> 5; matrix products, arithmetic and copies ran while one was open for 0% -> 0% of each run, Pallas kernels for 7% -> 8%
where the time goes in v4:
time: 113 us; the launch traced here: 112 us
  starting transfers between devices  79.5 us (70%)
  Pallas kernels  17.4 us (15%)
  waiting for transfers between devices  14.3 us (13%)
    ppermute x8, starting transfers between devices, xor(): return lax.ppermute(x, 'group', [(i, i ^ k) for i in range(4)])  27.8 us
    ppermute x3, starting transfers between devices, swap_halos(): t2 = lax.ppermute(t2, 'theta', theta_pairs(nt, 1))  20 us
    ppermute x3, starting transfers between devices, swap_halos(): r2 = lax.ppermute(r2, ('row', 'group'), row_pairs(nr, 1))  17.9 us
    pallas_call x10, Pallas kernels, call(): pl.pallas_call(kernel, out_shape=outs, in_specs=specs, out_specs=[pl.Bloc...  17.4 us
    ppermute x8, waiting for transfers between devices, xor(): return lax.ppermute(x, 'group', [(i, i ^ k) for i in range(4)])  14.3 us
    ppermute x3, starting transfers between devices, swap_halos(): r1 = lax.ppermute(r1, ('row', 'group'), row_pairs(nr, 0))  7.41 us
    ppermute x3, starting transfers between devices, swap_halos(): t1 = lax.ppermute(t1, 'theta', theta_pairs(nt, 0))  6.29 us
  transfers between devices with their start and end apart: 20, of which 5 were waited for; matrix products, arithmetic and copies ran while one was open for 0% of the time, Pallas kernels for 8%

profile of v4, /device:TPU:31, one launch (start us, length us, event | category | flops | bytes accessed | tf_op | source)
XLA Modules:
  0.0 112.3 jit_solution(1414164220298713456)
XLA Ops:
  0.7 1.8 %shard_map.68 = (f32[12,64,128]{2,1,0:T(8,128)S(1)}, bf16[1328,128]{1,0:T(8,128)(2,1)S(1)}, bf16[8,64,128]{2,1,0:T(8,128)(2,1)S(1)}, bf16[8,64,128]{2,1,0:T(8,128)(2,1)S(1)}) custom-call(s32[4]{0:T(128)S(1)} %pad_add_fusion.pos, f32[12]{0:T(128)} %planck.3, bf16[8,128,128]{2,1,0:T(8,128)(2,1)} %bitcast.13, f32[12,128,128]{2,1,0:T(8,128)} %bitcast.12), custom_call_target="tpu_custom_call" | custom-call | flops 1000000 | bytes 1000000 | tf_op jit(solution)/shard_map/pallas_call | solution.py:32
  2.5 4.0 %collective-permute-start = (bf16[1328,128]{1,0:T(8,128)(2,1)S(1)}, bf16[1328,128]{1,0:T(8,128)(2,1)S(1)}, u32[]{:S(2)}, u32[]{:S(2)}) collective-permute-start(bf16[1328,128]{1,0:T(8,128)(2,1)S(1)} %get-tuple-element.46), channel_id=1, source_target_pairs={{0,1},{1,0},{2,3},{3,2},{4,5},{5,4},{6,7},{7,6},{8,9},{9,8},{10,11... | collective-permute-start | bytes 1019912 | tf_op jit(solution)/shard_map/ppermute | solution.py:389
  6.6 5.8 %collective-permute-start.1 = (bf16[8,64,128]{2,1,0:T(8,128)(2,1)S(1)}, bf16[8,64,128]{2,1,0:T(8,128)(2,1)S(1)}, u32[]{:S(2)}, u32[]{:S(2)}) collective-permute-start(bf16[8,64,128]{2,1,0:T(8,128)(2,1)S(1)} %get-tuple-element.45.mine), channel_id=1, source_target_pairs={{0,2},{1,3},{2,0},{3,1},{4,6},{5,7},{6,4},{7,5},{8,10},{9,11},{10,... | collective-permute-start | bytes 393224 | tf_op jit(solution)/shard_map/ppermute | solution.py:389
  12.4 1.9 %collective-permute-start.2 = (bf16[8,64,128]{2,1,0:T(8,128)(2,1)S(1)}, bf16[8,64,128]{2,1,0:T(8,128)(2,1)S(1)}, u32[]{:S(2)}, u32[]{:S(2)}) collective-permute-start(bf16[8,64,128]{2,1,0:T(8,128)(2,1)S(1)} %get-tuple-element.50), channel_id=1, source_target_pairs={{0,3},{1,2},{2,1},{3,0},{4,7},{5,6},{6,5},{7,4},{8,11},{9,10},{10,... | collective-permute-start | bytes 393224 | tf_op jit(solution)/shard_map/ppermute | solution.py:389
  14.4 1.6 %collective-permute-done.1.near = bf16[8,64,128]{2,1,0:T(8,128)(2,1)S(1)} collective-permute-done((bf16[8,64,128]{2,1,0:T(8,128)(2,1)S(1)}, bf16[8,64,128]{2,1,0:T(8,128)(2,1)S(1)}, u32[]{:S(2)}, u32[]{:S(2)}) %collective-permute-start.1) | collective-permute-done | bytes 131104 | tf_op jit(solution)/shard_map/ppermute | solution.py:389
  17.0 2.3 %shard_map.69 = (f32[1536,128]{1,0:T(8,128)S(1)}, f32[1536,128]{1,0:T(8,128)S(1)}, f32[2,16,128]{2,1,0:T(8,128)S(1)}) custom-call(s32[4]{0:T(128)S(1)} %pad_add_fusion.pos, f32[1536]{0:T(1024)S(1)} %reshape.32.tab, f32[12]{0:T(128)S(1)} %copy-done.1, bf16[8,64,128]{2,1,0:T(8,128)(2,1)S(1)} %get-tuple-element.45.mine, ...), custom_call_target="tpu_custom_call" | custom-call | flops 20000000 | bytes 1000000 | tf_op jit(solution)/shard_map/pallas_call | solution.py:32
  19.4 4.1 %collective-permute-done.2.far = bf16[8,64,128]{2,1,0:T(8,128)(2,1)S(1)} collective-permute-done((bf16[8,64,128]{2,1,0:T(8,128)(2,1)S(1)}, bf16[8,64,128]{2,1,0:T(8,128)(2,1)S(1)}, u32[]{:S(2)}, u32[]{:S(2)}) %collective-permute-start.2) | collective-permute-done | bytes 131104 | tf_op jit(solution)/shard_map/ppermute | solution.py:389
  23.5 1.4 %shard_map.70 = (f32[1536,128]{1,0:T(8,128)S(1)}, bf16[384,128]{1,0:T(8,128)(2,1)S(1)}, bf16[384,128]{1,0:T(8,128)(2,1)S(1)}, bf16[384,128]{1,0:T(8,128)(2,1)S(1)}, bf16[384,128]{1,0:T(8,128)(2,1)S(1)}) custom-call(s32[4]{0:T(128)S(1)} %pad_add_fusion.pos, f32[1536]{0:T(1024)S(1)} %reshape.32.tab, f32[1536,128]{1,0:T(8,128)S(1)} %get-tuple-element.49.part, ...), custom_call_target="tpu_custom_call" | custom-call | flops 5000000 | bytes 1000000 | tf_op jit(solution)/shard_map/pallas_call | solution.py:32
  24.9 2.5 %collective-permute-start.3 = (bf16[384,128]{1,0:T(8,128)(2,1)S(1)}, bf16[384,128]{1,0:T(8,128)(2,1)S(1)}, u32[]{:S(2)}, u32[]{:S(2)}) collective-permute-start(bf16[384,128]{1,0:T(8,128)(2,1)S(1)} %get-tuple-element.56), channel_id=1, source_target_pairs={{0,4},{4,0},{8,12},{12,8},{16,20},{20,16},{24,28},{28,24},{32,36},... | collective-permute-start | bytes 294920 | tf_op jit(solution)/shard_map/ppermute | solution.py:397
  27.3 10.9 %collective-permute-start.4 = (bf16[384,128]{1,0:T(8,128)(2,1)S(1)}, bf16[384,128]{1,0:T(8,128)(2,1)S(1)}, u32[]{:S(2)}, u32[]{:S(2)}) collective-permute-start(bf16[384,128]{1,0:T(8,128)(2,1)S(1)} %get-tuple-element.57), channel_id=1, source_target_pairs={{4,8},{8,4},{12,16},{16,12},{20,24},{24,20},{28,32},{32,28},{36,40... | collective-permute-start | bytes 294920 | tf_op jit(solution)/shard_map/ppermute | solution.py:395
  38.3 1.9 %collective-permute-start.5 = (bf16[384,128]{1,0:T(8,128)(2,1)S(1)}, bf16[384,128]{1,0:T(8,128)(2,1)S(1)}, u32[]{:S(2)}, u32[]{:S(2)}) collective-permute-start(bf16[384,128]{1,0:T(8,128)(2,1)S(1)} %get-tuple-element.58), channel_id=1, source_target_pairs={{0,1},{1,0},{49,48},{48,49},{96,97},{97,96},{145,144},{144,145},{1... | collective-permute-start | bytes 294920 | tf_op jit(solution)/shard_map/ppermute | solution.py:399
  40.2 7.4 %collective-permute-start.6 = (bf16[384,128]{1,0:T(8,128)(2,1)S(1)}, bf16[384,128]{1,0:T(8,128)(2,1)S(1)}, u32[]{:S(2)}, u32[]{:S(2)}) collective-permute-start(bf16[384,128]{1,0:T(8,128)(2,1)S(1)} %get-tuple-element.59), channel_id=1, source_target_pairs={{1,49},{49,1},{48,96},{96,48},{97,145},{145,97},{144,192},{192,144... | collective-permute-start | bytes 294920 | tf_op jit(solution)/shard_map/ppermute | solution.py:398
  47.6 2.3 %shard_map.71 = (f32[1536,128]{1,0:T(8,128)S(1)}, f32[1536,128]{1,0:T(8,128)S(1)}, f32[1536,128]{1,0:T(8,128)S(1)}, f32[1536,128]{1,0:T(8,128)S(1)}, f32[1536,12...) custom-call(s32[4]{0:T(128)S(1)} %pad_add_fusion.pos, f32[1536,128]{1,0:T(8,128)S(1)} %get-tuple-element.48.e, ...), custom_call_target="tpu_custom_call" | custom-call | flops 20000000 | bytes 1000000 | tf_op jit(solution)/shard_map/pallas_call | solution.py:32
  50.0 1.3 %shard_map.72 = (f32[1536,128]{1,0:T(8,128)S(1)}, f32[128,128]{1,0:T(8,128)S(1)}, f32[4,192,128]{2,1,0:T(8,128)S(1)}, bf16[192,128]{1,0:T(8,128)(2,1)S(1)}, bf16...) custom-call(s32[4]{0:T(128)S(1)} %pad_add_fusion.pos, ...), custom_call_target="tpu_custom_call", output_to_operand_aliasing={{7}: (6, {}), {8}: (7, {})} | custom-call | flops 5000000 | bytes 1000000 | tf_op jit(solution)/shard_map/pallas_call | solution.py:32
  51.3 4.9 %collective-permute-start.7 = (f32[128,128]{1,0:T(8,128)S(1)}, f32[128,128]{1,0:T(8,128)S(1)}, u32[]{:S(2)}, u32[]{:S(2)}) collective-permute-start(f32[128,128]{1,0:T(8,128)S(1)} %get-tuple-element.61.sums), channel_id=1, source_target_pairs={{0,2},{1,3},{2,0},{3,1},{4,6},{5,7},{6,4},{7,5},{8,10},{9,11},{10,... | collective-permute-start | bytes 196616 | tf_op jit(solution)/shard_map/ppermute | solution.py:389
  56.2 1.9 %collective-permute-start.8 = (bf16[192,128]{1,0:T(8,128)(2,1)S(1)}, bf16[192,128]{1,0:T(8,128)(2,1)S(1)}, u32[]{:S(2)}, u32[]{:S(2)}) collective-permute-start(bf16[192,128]{1,0:T(8,128)(2,1)S(1)} %get-tuple-element.69), channel_id=1, source_target_pairs={{0,4},{4,0},{8,12},{12,8},{16,20},{20,16},{24,28},{28,24},{32,36},... | collective-permute-start | bytes 147464 | tf_op jit(solution)/shard_map/ppermute | solution.py:397
  58.1 4.0 %collective-permute-start.9 = (bf16[192,128]{1,0:T(8,128)(2,1)S(1)}, bf16[192,128]{1,0:T(8,128)(2,1)S(1)}, u32[]{:S(2)}, u32[]{:S(2)}) collective-permute-start(bf16[192,128]{1,0:T(8,128)(2,1)S(1)} %get-tuple-element.70), channel_id=1, source_target_pairs={{4,8},{8,4},{12,16},{16,12},{20,24},{24,20},{28,32},{32,28},{36,40... | collective-permute-start | bytes 147464 | tf_op jit(solution)/shard_map/ppermute | solution.py:395
  62.2 3.6 %collective-permute-start.10 = (bf16[192,128]{1,0:T(8,128)(2,1)S(1)}, bf16[192,128]{1,0:T(8,128)(2,1)S(1)}, u32[]{:S(2)}, u32[]{:S(2)}) collective-permute-start(bf16[192,128]{1,0:T(8,128)(2,1)S(1)} %get-tuple-element.71), channel_id=1, source_target_pairs={{0,1},{1,0},{49,48},{48,49},{96,97},{97,96},{145,144},{144,145},{1... | collective-permute-start | bytes 147464 | tf_op jit(solution)/shard_map/ppermute | solution.py:399
  65.8 5.8 %collective-permute-start.11 = (bf16[192,128]{1,0:T(8,128)(2,1)S(1)}, bf16[192,128]{1,0:T(8,128)(2,1)S(1)}, u32[]{:S(2)}, u32[]{:S(2)}) collective-permute-start(bf16[192,128]{1,0:T(8,128)(2,1)S(1)} %get-tuple-element.72), channel_id=1, source_target_pairs={{1,49},{49,1},{48,96},{96,48},{97,145},{145,97},{144,192},{192,144... | collective-permute-start | bytes 147464 | tf_op jit(solution)/shard_map/ppermute | solution.py:398
  71.6 2.2 %shard_map.73 = (f32[1536,128]{1,0:T(8,128)S(1)}, f32[1536,128]{1,0:T(8,128)S(1)}) custom-call(s32[4]{0:T(128)S(1)} %pad_add_fusion.pos, f32[1536,128]{1,0:T(8,128)S(1)} %get-tuple-element.60.e, f32[1536,128]{1,0:T(8,128)S(1)} %get-tuple-element.51.kap, f32[1536,128]{1,0:T(8,128)S(1)} %get-tuple-element.63.e01, f32[1536,128]{1,0:T(8,128)S(1)} %get-tuple-element.64.up_c, ...), custom_call_target="tpu_custom_call" | custom-call | flops 20000000 | bytes 1000000 | tf_op jit(solution)/shard_map/pallas_call | solution.py:32
  75.0 1.9 %collective-permute-start.13 = (bf16[192,128]{1,0:T(8,128)(2,1)S(1)}, bf16[192,128]{1,0:T(8,128)(2,1)S(1)}, u32[]{:S(2)}, u32[]{:S(2)}) collective-permute-start(bf16[192,128]{1,0:T(8,128)(2,1)S(1)} %get-tuple-element.79), channel_id=1, source_target_pairs={{0,4},{4,0},{8,12},{12,8},{16,20},{20,16},{24,28},{28,24},{32,36},... | collective-permute-start | bytes 147464 | tf_op jit(solution)/shard_map/ppermute | solution.py:397
  77.0 5.1 %collective-permute-start.14 = (bf16[192,128]{1,0:T(8,128)(2,1)S(1)}, bf16[192,128]{1,0:T(8,128)(2,1)S(1)}, u32[]{:S(2)}, u32[]{:S(2)}) collective-permute-start(bf16[192,128]{1,0:T(8,128)(2,1)S(1)} %get-tuple-element.80), channel_id=1, source_target_pairs={{4,8},{8,4},{12,16},{16,12},{20,24},{24,20},{28,32},{32,28},{36,40... | collective-permute-start | bytes 147464 | tf_op jit(solution)/shard_map/ppermute | solution.py:395
  82.1 1.9 %collective-permute-start.15 = (bf16[192,128]{1,0:T(8,128)(2,1)S(1)}, bf16[192,128]{1,0:T(8,128)(2,1)S(1)}, u32[]{:S(2)}, u32[]{:S(2)}) collective-permute-start(bf16[192,128]{1,0:T(8,128)(2,1)S(1)} %get-tuple-element.81), channel_id=1, source_target_pairs={{0,1},{1,0},{49,48},{48,49},{96,97},{97,96},{145,144},{144,145},{1... | collective-permute-start | bytes 147464 | tf_op jit(solution)/shard_map/ppermute | solution.py:399
  84.0 4.6 %collective-permute-start.16 = (bf16[192,128]{1,0:T(8,128)(2,1)S(1)}, bf16[192,128]{1,0:T(8,128)(2,1)S(1)}, u32[]{:S(2)}, u32[]{:S(2)}) collective-permute-start(bf16[192,128]{1,0:T(8,128)(2,1)S(1)} %get-tuple-element.82), channel_id=1, source_target_pairs={{1,49},{49,1},{48,96},{96,48},{97,145},{145,97},{144,192},{192,144... | collective-permute-start | bytes 147464 | tf_op jit(solution)/shard_map/ppermute | solution.py:398
  88.6 2.8 %collective-permute-start.12 = (f32[64,128]{1,0:T(8,128)S(1)}, f32[64,128]{1,0:T(8,128)S(1)}, u32[]{:S(2)}, u32[]{:S(2)}) collective-permute-start(f32[64,128]{1,0:T(8,128)S(1)} %get-tuple-element.76.part), channel_id=1, source_target_pairs={{0,2},{1,3},{2,0},{3,1},{4,6},{5,7},{6,4},{7,5},{8,10},{9,11},{10,... | collective-permute-start | bytes 98312 | tf_op jit(solution)/shard_map/ppermute | solution.py:389
  91.4 2.2 %shard_map.75 = (f32[1536,128]{1,0:T(8,128)S(1)}, f32[1536,128]{1,0:T(8,128)S(1)}) custom-call(s32[4]{0:T(128)S(1)} %pad_add_fusion.pos, f32[1536,128]{1,0:T(8,128)S(1)} %get-tuple-element.73.e, f32[1536,128]{1,0:T(8,128)S(1)} %get-tuple-element.51.kap, f32[1536,128]{1,0:T(8,128)S(1)} %get-tuple-element.63.e01, f32[1536,128]{1,0:T(8,128)S(1)} %get-tuple-element.64.up_c, ...), custom_call_target="tpu_custom_call" | custom-call | flops 20000000 | bytes 1000000 | tf_op jit(solution)/shard_map/pallas_call | solution.py:32
  94.2 1.2 %shard_map.76 = (f32[768,128]{1,0:T(8,128)S(1)}, f32[960,128]{1,0:T(8,128)S(1)}, f32[64,128]{1,0:T(8,128)S(1)}, f32[1536,128]{1,0:T(8,128)S(1)}, f32[1536,128]{1,0:T(8,128)S(1)}) custom-call(s32[4]{0:T(128)S(1)} %pad_add_fusion.pos, f32[1536,128]{1,0:T(8,128)S(1)} %get-tuple-element.73.e, ...), custom_call_target="tpu_custom_call", output_to_operand_aliasing={{3}: (10, {}), {4}: (11, {})} | custom-call | flops 5000000 | bytes 1000000 | tf_op jit(solution)/shard_map/pallas_call | solution.py:32
  95.4 1.9 %collective-permute-start.17 = (f32[960,128]{1,0:T(8,128)S(1)}, f32[960,128]{1,0:T(8,128)S(1)}, u32[]{:S(2)}, u32[]{:S(2)}) collective-permute-start(f32[960,128]{1,0:T(8,128)S(1)} %get-tuple-element.84.send), channel_id=1, source_target_pairs={{0,1},{1,0},{2,3},{3,2},{4,5},{5,4},{6,7},{7,6},{8,9},{9,8},{10,11... | collective-permute-start | bytes 1474568 | tf_op jit(solution)/shard_map/ppermute | solution.py:389
  97.4 4.0 %collective-permute-start.19 = (f32[64,128]{1,0:T(8,128)S(1)}, f32[64,128]{1,0:T(8,128)S(1)}, u32[]{:S(2)}, u32[]{:S(2)}) collective-permute-start(f32[64,128]{1,0:T(8,128)S(1)} %get-tuple-element.85), channel_id=1, source_target_pairs={{0,3},{1,2},{2,1},{3,0},{4,7},{5,6},{6,5},{7,4},{8,11},{9,10},{10,... | collective-permute-start | bytes 98312 | tf_op jit(solution)/shard_map/ppermute | solution.py:389
  101.4 2.4 %collective-permute-start.18 = (f32[64,128]{1,0:T(8,128)S(1)}, f32[64,128]{1,0:T(8,128)S(1)}, u32[]{:S(2)}, u32[]{:S(2)}) collective-permute-start(f32[64,128]{1,0:T(8,128)S(1)} %get-tuple-element.85), channel_id=1, source_target_pairs={{0,2},{1,3},{2,0},{3,1},{4,6},{5,7},{6,4},{7,5},{8,10},{9,11},{10,... | collective-permute-start | bytes 98312 | tf_op jit(solution)/shard_map/ppermute | solution.py:389
  103.8 7.0 %collective-permute-done.19.far = f32[64,128]{1,0:T(8,128)S(1)} collective-permute-done((f32[64,128]{1,0:T(8,128)S(1)}, f32[64,128]{1,0:T(8,128)S(1)}, u32[]{:S(2)}, u32[]{:S(2)}) %collective-permute-start.19) | collective-permute-done | bytes 32800 | tf_op jit(solution)/shard_map/ppermute | solution.py:389
  110.8 1.5 %shard_map.77 = (f32[1536,128]{1,0:T(8,128)}, f32[128,128]{1,0:T(8,128)}) custom-call(s32[4]{0:T(128)S(1)} %pad_add_fusion.pos, f32[768,128]{1,0:T(8,128)S(1)} %get-tuple-element.83.eown, f32[960,128]{1,0:T(8,128)S(1)} %get-tuple-element.84.send, f32[960,128]{1,0:T(8,128)S(1)} %collective-permute-done.17.pair, f32[64,128]{1,0:T(8,128)S(1)} %collective-permute-done.18.near, ...), custom_call_target="tpu_custom_call" | custom-call | flops 1000000 | bytes 1000000 | tf_op jit(solution)/shard_map/pallas_call | solution.py:32
  (26 shorter events, 3.0 us)
Async XLA Ops:
  0.7 13.6 %copy-start.2 = (bf16[32,48]{1,0:T(8,128)(2,1)S(1)}, bf16[32,48]{1,0:T(8,128)(2,1)}, u32[]{:S(2)}) copy-start(bf16[32,48]{1,0:T(8,128)(2,1)} %param.6) | copy-start | bytes 9220
  2.5 14.5 %collective-permute-start = (bf16[1328,128]{1,0:T(8,128)(2,1)S(1)}, bf16[1328,128]{1,0:T(8,128)(2,1)S(1)}, u32[]{:S(2)}, u32[]{:S(2)}) collective-permute-start(bf16[1328,128]{1,0:T(8,128)(2,1)S(1)} %get-tuple-element.46), channel_id=1, source_target_pairs={{0,1},{1,0},{2,3},{3,2},{4,5},{5,4},{6,7},{7,6},{8,9},{9,8},{10,11... | collective-permute-start | bytes 1019912 | tf_op jit(solution)/shard_map/ppermute | solution.py:389
  6.6 9.4 %collective-permute-start.1 = (bf16[8,64,128]{2,1,0:T(8,128)(2,1)S(1)}, bf16[8,64,128]{2,1,0:T(8,128)(2,1)S(1)}, u32[]{:S(2)}, u32[]{:S(2)}) collective-permute-start(bf16[8,64,128]{2,1,0:T(8,128)(2,1)S(1)} %get-tuple-element.45.mine), channel_id=1, source_target_pairs={{0,2},{1,3},{2,0},{3,1},{4,6},{5,7},{6,4},{7,5},{8,10},{9,11},{10,... | collective-permute-start | bytes 393224 | tf_op jit(solution)/shard_map/ppermute | solution.py:389
  12.4 11.1 %collective-permute-start.2 = (bf16[8,64,128]{2,1,0:T(8,128)(2,1)S(1)}, bf16[8,64,128]{2,1,0:T(8,128)(2,1)S(1)}, u32[]{:S(2)}, u32[]{:S(2)}) collective-permute-start(bf16[8,64,128]{2,1,0:T(8,128)(2,1)S(1)} %get-tuple-element.50), channel_id=1, source_target_pairs={{0,3},{1,2},{2,1},{3,0},{4,7},{5,6},{6,5},{7,4},{8,11},{9,10},{10,... | collective-permute-start | bytes 393224 | tf_op jit(solution)/shard_map/ppermute | solution.py:389
  14.4 2.6 %copy-start.1 = (f32[12]{0:T(128)S(1)}, f32[12]{0:T(128)}, u32[]{:S(2)}) copy-start(f32[12]{0:T(128)} %planck.3) | copy-start | bytes 148
  24.9 25.1 %collective-permute-start.3 = (bf16[384,128]{1,0:T(8,128)(2,1)S(1)}, bf16[384,128]{1,0:T(8,128)(2,1)S(1)}, u32[]{:S(2)}, u32[]{:S(2)}) collective-permute-start(bf16[384,128]{1,0:T(8,128)(2,1)S(1)} %get-tuple-element.56), channel_id=1, source_target_pairs={{0,4},{4,0},{8,12},{12,8},{16,20},{20,16},{24,28},{28,24},{32,36},... | collective-permute-start | bytes 294920 | tf_op jit(solution)/shard_map/ppermute | solution.py:397
  27.3 22.7 %collective-permute-start.4 = (bf16[384,128]{1,0:T(8,128)(2,1)S(1)}, bf16[384,128]{1,0:T(8,128)(2,1)S(1)}, u32[]{:S(2)}, u32[]{:S(2)}) collective-permute-start(bf16[384,128]{1,0:T(8,128)(2,1)S(1)} %get-tuple-element.57), channel_id=1, source_target_pairs={{4,8},{8,4},{12,16},{16,12},{20,24},{24,20},{28,32},{32,28},{36,40... | collective-permute-start | bytes 294920 | tf_op jit(solution)/shard_map/ppermute | solution.py:395
  38.3 11.7 %collective-permute-start.5 = (bf16[384,128]{1,0:T(8,128)(2,1)S(1)}, bf16[384,128]{1,0:T(8,128)(2,1)S(1)}, u32[]{:S(2)}, u32[]{:S(2)}) collective-permute-start(bf16[384,128]{1,0:T(8,128)(2,1)S(1)} %get-tuple-element.58), channel_id=1, source_target_pairs={{0,1},{1,0},{49,48},{48,49},{96,97},{97,96},{145,144},{144,145},{1... | collective-permute-start | bytes 294920 | tf_op jit(solution)/shard_map/ppermute | solution.py:399
  40.2 9.8 %collective-permute-start.6 = (bf16[384,128]{1,0:T(8,128)(2,1)S(1)}, bf16[384,128]{1,0:T(8,128)(2,1)S(1)}, u32[]{:S(2)}, u32[]{:S(2)}) collective-permute-start(bf16[384,128]{1,0:T(8,128)(2,1)S(1)} %get-tuple-element.59), channel_id=1, source_target_pairs={{1,49},{49,1},{48,96},{96,48},{97,145},{145,97},{144,192},{192,144... | collective-permute-start | bytes 294920 | tf_op jit(solution)/shard_map/ppermute | solution.py:398
  47.6 2.4 %copy-start = (f32[16,8,128]{2,1,0:T(8,128)S(1)}, f32[16,8,128]{2,1,0:T(8,128)}, u32[]{:S(2)}) copy-start(f32[16,8,128]{2,1,0:T(8,128)} %param.9) | copy-start | bytes 196612
  51.3 22.5 %collective-permute-start.7 = (f32[128,128]{1,0:T(8,128)S(1)}, f32[128,128]{1,0:T(8,128)S(1)}, u32[]{:S(2)}, u32[]{:S(2)}) collective-permute-start(f32[128,128]{1,0:T(8,128)S(1)} %get-tuple-element.61.sums), channel_id=1, source_target_pairs={{0,2},{1,3},{2,0},{3,1},{4,6},{5,7},{6,4},{7,5},{8,10},{9,11},{10,... | collective-permute-start | bytes 196616 | tf_op jit(solution)/shard_map/ppermute | solution.py:389
  56.2 17.6 %collective-permute-start.8 = (bf16[192,128]{1,0:T(8,128)(2,1)S(1)}, bf16[192,128]{1,0:T(8,128)(2,1)S(1)}, u32[]{:S(2)}, u32[]{:S(2)}) collective-permute-start(bf16[192,128]{1,0:T(8,128)(2,1)S(1)} %get-tuple-element.69), channel_id=1, source_target_pairs={{0,4},{4,0},{8,12},{12,8},{16,20},{20,16},{24,28},{28,24},{32,36},... | collective-permute-start | bytes 147464 | tf_op jit(solution)/shard_map/ppermute | solution.py:397
  58.1 15.7 %collective-permute-start.9 = (bf16[192,128]{1,0:T(8,128)(2,1)S(1)}, bf16[192,128]{1,0:T(8,128)(2,1)S(1)}, u32[]{:S(2)}, u32[]{:S(2)}) collective-permute-start(bf16[192,128]{1,0:T(8,128)(2,1)S(1)} %get-tuple-element.70), channel_id=1, source_target_pairs={{4,8},{8,4},{12,16},{16,12},{20,24},{24,20},{28,32},{32,28},{36,40... | collective-permute-start | bytes 147464 | tf_op jit(solution)/shard_map/ppermute | solution.py:395
  62.2 11.6 %collective-permute-start.10 = (bf16[192,128]{1,0:T(8,128)(2,1)S(1)}, bf16[192,128]{1,0:T(8,128)(2,1)S(1)}, u32[]{:S(2)}, u32[]{:S(2)}) collective-permute-start(bf16[192,128]{1,0:T(8,128)(2,1)S(1)} %get-tuple-element.71), channel_id=1, source_target_pairs={{0,1},{1,0},{49,48},{48,49},{96,97},{97,96},{145,144},{144,145},{1... | collective-permute-start | bytes 147464 | tf_op jit(solution)/shard_map/ppermute | solution.py:399
  65.8 8.1 %collective-permute-start.11 = (bf16[192,128]{1,0:T(8,128)(2,1)S(1)}, bf16[192,128]{1,0:T(8,128)(2,1)S(1)}, u32[]{:S(2)}, u32[]{:S(2)}) collective-permute-start(bf16[192,128]{1,0:T(8,128)(2,1)S(1)} %get-tuple-element.72), channel_id=1, source_target_pairs={{1,49},{49,1},{48,96},{96,48},{97,145},{145,97},{144,192},{192,144... | collective-permute-start | bytes 147464 | tf_op jit(solution)/shard_map/ppermute | solution.py:398
  75.0 19.1 %collective-permute-start.13 = (bf16[192,128]{1,0:T(8,128)(2,1)S(1)}, bf16[192,128]{1,0:T(8,128)(2,1)S(1)}, u32[]{:S(2)}, u32[]{:S(2)}) collective-permute-start(bf16[192,128]{1,0:T(8,128)(2,1)S(1)} %get-tuple-element.79), channel_id=1, source_target_pairs={{0,4},{4,0},{8,12},{12,8},{16,20},{20,16},{24,28},{28,24},{32,36},... | collective-permute-start | bytes 147464 | tf_op jit(solution)/shard_map/ppermute | solution.py:397
  77.0 17.2 %collective-permute-start.14 = (bf16[192,128]{1,0:T(8,128)(2,1)S(1)}, bf16[192,128]{1,0:T(8,128)(2,1)S(1)}, u32[]{:S(2)}, u32[]{:S(2)}) collective-permute-start(bf16[192,128]{1,0:T(8,128)(2,1)S(1)} %get-tuple-element.80), channel_id=1, source_target_pairs={{4,8},{8,4},{12,16},{16,12},{20,24},{24,20},{28,32},{32,28},{36,40... | collective-permute-start | bytes 147464 | tf_op jit(solution)/shard_map/ppermute | solution.py:395
  82.1 12.1 %collective-permute-start.15 = (bf16[192,128]{1,0:T(8,128)(2,1)S(1)}, bf16[192,128]{1,0:T(8,128)(2,1)S(1)}, u32[]{:S(2)}, u32[]{:S(2)}) collective-permute-start(bf16[192,128]{1,0:T(8,128)(2,1)S(1)} %get-tuple-element.81), channel_id=1, source_target_pairs={{0,1},{1,0},{49,48},{48,49},{96,97},{97,96},{145,144},{144,145},{1... | collective-permute-start | bytes 147464 | tf_op jit(solution)/shard_map/ppermute | solution.py:399
  84.0 10.2 %collective-permute-start.16 = (bf16[192,128]{1,0:T(8,128)(2,1)S(1)}, bf16[192,128]{1,0:T(8,128)(2,1)S(1)}, u32[]{:S(2)}, u32[]{:S(2)}) collective-permute-start(bf16[192,128]{1,0:T(8,128)(2,1)S(1)} %get-tuple-element.82), channel_id=1, source_target_pairs={{1,49},{49,1},{48,96},{96,48},{97,145},{145,97},{144,192},{192,144... | collective-permute-start | bytes 147464 | tf_op jit(solution)/shard_map/ppermute | solution.py:398
  88.6 5.6 %collective-permute-start.12 = (f32[64,128]{1,0:T(8,128)S(1)}, f32[64,128]{1,0:T(8,128)S(1)}, u32[]{:S(2)}, u32[]{:S(2)}) collective-permute-start(f32[64,128]{1,0:T(8,128)S(1)} %get-tuple-element.76.part), channel_id=1, source_target_pairs={{0,2},{1,3},{2,0},{3,1},{4,6},{5,7},{6,4},{7,5},{8,10},{9,11},{10,... | collective-permute-start | bytes 98312 | tf_op jit(solution)/shard_map/ppermute | solution.py:389
  95.4 15.4 %collective-permute-start.17 = (f32[960,128]{1,0:T(8,128)S(1)}, f32[960,128]{1,0:T(8,128)S(1)}, u32[]{:S(2)}, u32[]{:S(2)}) collective-permute-start(f32[960,128]{1,0:T(8,128)S(1)} %get-tuple-element.84.send), channel_id=1, source_target_pairs={{0,1},{1,0},{2,3},{3,2},{4,5},{5,4},{6,7},{7,6},{8,9},{9,8},{10,11... | collective-permute-start | bytes 1474568 | tf_op jit(solution)/shard_map/ppermute | solution.py:389
  97.4 13.4 %collective-permute-start.19 = (f32[64,128]{1,0:T(8,128)S(1)}, f32[64,128]{1,0:T(8,128)S(1)}, u32[]{:S(2)}, u32[]{:S(2)}) collective-permute-start(f32[64,128]{1,0:T(8,128)S(1)} %get-tuple-element.85), channel_id=1, source_target_pairs={{0,3},{1,2},{2,1},{3,0},{4,7},{5,6},{6,5},{7,4},{8,11},{9,10},{10,... | collective-permute-start | bytes 98312 | tf_op jit(solution)/shard_map/ppermute | solution.py:389
  101.4 9.4 %collective-permute-start.18 = (f32[64,128]{1,0:T(8,128)S(1)}, f32[64,128]{1,0:T(8,128)S(1)}, u32[]{:S(2)}, u32[]{:S(2)}) collective-permute-start(f32[64,128]{1,0:T(8,128)S(1)} %get-tuple-element.85), channel_id=1, source_target_pairs={{0,2},{1,3},{2,0},{3,1},{4,6},{5,7},{6,4},{7,5},{8,10},{9,11},{10,... | collective-permute-start | bytes 98312 | tf_op jit(solution)/shard_map/ppermute | solution.py:389

commit v5 on v4

--- a/solution.py
+++ b/solution.py
@@ -54,6 +54,7 @@
 
 
 UNROLL = 4
+AHEAD = 4
 SIZE = BINS * ROWS * LAT
 PART = OWN * ROWS * LAT
 N = ROWS * LAT
@@ -339,8 +340,8 @@
 
 
 def outer_last(pos, e, kap, share, told, tprev, stot, part, got, edge, numer_in, denom_in, h0, h1, h2, h3, *refs):
-    eown, send, ksum, numer, denom = refs[:5]
-    temp4, halo, enew = refs[5:]
+    eown, ahead, behind, ksum, up, down, numer, denom = refs[:8]
+    temp4, halo, enew = refs[8:]
     unpack_halos(pos, (h0, h1, h2, h3), 0, halo)
     s = stot[...]
     old = own_rows(pos, told)
@@ -350,22 +351,24 @@
     outer_body(e, kap, share, temp4, halo, edge, numer, denom, enew, ksum)
     slot = pos[2] % 2
     eown[...] = enew[pl.ds(pl.multiple_of(slot * PART, PART), PART), :]
-    send[pl.ds(0, PART), :] = enew[pl.ds(pl.multiple_of((1 - slot) * PART, PART), PART), :]
-    up, down = terms(old, t, s)
-    send[pl.ds(PART, N), :] = ksum[...]
-    send[pl.ds(PART + N, N), :] = up
-    send[pl.ds(PART + 2 * N, N), :] = down
-
-
-def join_kernel(pos, eown, send, pair, near, far, energy, temp):
+    theirs = pl.multiple_of((1 - slot) * PART, PART)
+    ahead[...] = enew[pl.ds(theirs, AHEAD * N), :]
+    behind[...] = enew[pl.ds(pl.multiple_of(theirs + AHEAD * N, N), PART - AHEAD * N), :]
+    up[...], down[...] = terms(old, t, s)
+
+
+def finish_kernel(ksum, got, up, down, temp):
+    temp[...] = (up[...] + (ksum[...] + got[...]) / SCALE) / down[...]
+
+
+def join_kernel(pos, eown, ahead, behind, mine, other, energy, temp):
     half = pos[0]
     for g in range(OWN):
-        src = pl.ds(g * N, N)
-        energy[pl.ds(pl.multiple_of((2 * g + half) * N, N), N), :] = eown[src, :]
-        energy[pl.ds(pl.multiple_of((2 * g + 1 - half) * N, N), N), :] = pair[src, :]
-    k, up, down = pl.ds(PART, N), pl.ds(PART + N, N), pl.ds(PART + 2 * N, N)
-    temp[pl.ds(pl.multiple_of(half * N, N), N), :] = (send[up, :] + (send[k, :] + near[...]) / SCALE) / send[down, :]
-    temp[pl.ds(pl.multiple_of((1 - half) * N, N), N), :] = (pair[up, :] + (pair[k, :] + far[...]) / SCALE) / pair[down, :]
+        energy[half_rows(2 * g + half), :] = eown[pl.ds(g * N, N), :]
+        src, at = (ahead, g) if g < AHEAD else (behind, g - AHEAD)
+        energy[half_rows(2 * g + 1 - half), :] = src[pl.ds(at * N, N), :]
+    temp[half_rows(half), :] = mine[...]
+    temp[half_rows(1 - half), :] = other[...]
 
 
 def theta_pairs(count, odd):
@@ -460,18 +463,21 @@
     e, part = keep(e), keep(part)
     halos, got = swap_halos(rest, part)
     numer, denom = call(inner_next, [full] * 2, (pos, e, kap, e01, *coefs), smem=1, flops=20_000_000)
-    eown, send, part, _, _ = call(
-        outer_last, [held((PART, LANES)), held((PART + 3 * N, LANES)), sheet, full, full],
+    eown, ahead, behind, part, up, down, _, _ = call(
+        outer_last,
+        [held((PART, LANES)), held((AHEAD * N, LANES)), held((PART - AHEAD * N, LANES)), sheet, sheet, sheet, full, full],
         (pos, e, kap, share, told, keep(temp), keep(stot), part, got, edge, keep(numer), keep(denom), *halos), smem=1,
-        scratch=scratch + [VMEM((CELLS, LANES), F32)], flops=5_000_000, aliases=((10, 3), (11, 4)),
-    )
-    pair = xor(send, 1)
-    far = xor(part, 3)
-    near = xor(part, 2)
+        scratch=scratch + [VMEM((CELLS, LANES), F32)], flops=5_000_000, aliases=((10, 6), (11, 7)),
+    )
+    ahead = xor(ahead, 1)
+    got = xor(part, 2)
+    behind = xor(behind, 1)
+    mine, = call(finish_kernel, [sheet], [keep(x) for x in (part, got, up, down)])
+    other = xor(mine, 1)
     energy, temp = call(
         join_kernel,
         [jax.ShapeDtypeStruct((2 * PART, LANES), F32), jax.ShapeDtypeStruct((2 * N, LANES), F32)],
-        (pos, keep(eown), keep(send), keep(pair), keep(near), keep(far)), smem=1,
+        (pos, *(keep(x) for x in (eown, ahead, behind, mine, other))), smem=1,
     )
     return energy.reshape(OWN, 2 * ROWS, LAT, LANES), temp.reshape(2 * ROWS, LAT, LANES)
 

time: 113 us -> 115 us (1.018)
  the two profiles are of different devices: /device:TPU:31 before, /device:TPU:30 now
where the time goes in v5:
time: 115 us; the launch traced here: 114 us
  starting transfers between devices  77.5 us (67%)
  waiting for transfers between devices  18.1 us (16%)
  Pallas kernels  17.4 us (15%)
    ppermute x9, starting transfers between devices, xor(): return lax.ppermute(x, 'group', [(i, i ^ k) for i in range(4)])  33.9 us
    ppermute x3, starting transfers between devices, swap_halos(): t2 = lax.ppermute(t2, 'theta', theta_pairs(nt, 1))  21.8 us
    pallas_call x11, Pallas kernels, call(): pl.pallas_call(kernel, out_shape=outs, in_specs=specs, out_specs=[pl.Bloc...  17.4 us
    ppermute x9, waiting for transfers between devices, xor(): return lax.ppermute(x, 'group', [(i, i ^ k) for i in range(4)])  15.1 us
    ppermute x3, starting transfers between devices, swap_halos(): r1 = lax.ppermute(r1, ('row', 'group'), row_pairs(nr, 0))  9.46 us
    ppermute x3, starting transfers between devices, swap_halos(): t1 = lax.ppermute(t1, 'theta', theta_pairs(nt, 0))  6.57 us
    ppermute x3, starting transfers between devices, swap_halos(): r2 = lax.ppermute(r2, ('row', 'group'), row_pairs(nr, 1))  5.76 us
    ppermute x3, waiting for transfers between devices, swap_halos(): r2 = lax.ppermute(r2, ('row', 'group'), row_pairs(nr, 1))  2.9 us
  transfers between devices with their start and end apart: 21, of which 7 were waited for; matrix products, arithmetic and copies ran while one was open for 0% of the time, Pallas kernels for 8%

profile of v5, /device:TPU:30, one launch (start us, length us, event | category | flops | bytes accessed | tf_op | source)
XLA Modules:
  0.0 114.0 jit_solution(8396193859679536095)
XLA Ops:
  0.7 1.8 %shard_map.68 = (f32[12,64,128]{2,1,0:T(8,128)S(1)}, bf16[1328,128]{1,0:T(8,128)(2,1)S(1)}, bf16[8,64,128]{2,1,0:T(8,128)(2,1)S(1)}, bf16[8,64,128]{2,1,0:T(8,128)(2,1)S(1)}) custom-call(s32[4]{0:T(128)S(1)} %pad_add_fusion.pos, f32[12]{0:T(128)} %planck.3, bf16[8,128,128]{2,1,0:T(8,128)(2,1)} %bitcast.13, f32[12,128,128]{2,1,0:T(8,128)} %bitcast.12), custom_call_target="tpu_custom_call" | custom-call | flops 1000000 | bytes 1000000 | tf_op jit(solution)/shard_map/pallas_call | solution.py:32
  2.5 4.3 %collective-permute-start = (bf16[1328,128]{1,0:T(8,128)(2,1)S(1)}, bf16[1328,128]{1,0:T(8,128)(2,1)S(1)}, u32[]{:S(2)}, u32[]{:S(2)}) collective-permute-start(bf16[1328,128]{1,0:T(8,128)(2,1)S(1)} %get-tuple-element.49), channel_id=1, source_target_pairs={{0,1},{1,0},{2,3},{3,2},{4,5},{5,4},{6,7},{7,6},{8,9},{9,8},{10,11... | collective-permute-start | bytes 1019912 | tf_op jit(solution)/shard_map/ppermute | solution.py:392
  6.8 6.1 %collective-permute-start.1 = (bf16[8,64,128]{2,1,0:T(8,128)(2,1)S(1)}, bf16[8,64,128]{2,1,0:T(8,128)(2,1)S(1)}, u32[]{:S(2)}, u32[]{:S(2)}) collective-permute-start(bf16[8,64,128]{2,1,0:T(8,128)(2,1)S(1)} %get-tuple-element.48.mine), channel_id=1, source_target_pairs={{0,2},{1,3},{2,0},{3,1},{4,6},{5,7},{6,4},{7,5},{8,10},{9,11},{10,... | collective-permute-start | bytes 393224 | tf_op jit(solution)/shard_map/ppermute | solution.py:392
  12.9 1.9 %collective-permute-start.2 = (bf16[8,64,128]{2,1,0:T(8,128)(2,1)S(1)}, bf16[8,64,128]{2,1,0:T(8,128)(2,1)S(1)}, u32[]{:S(2)}, u32[]{:S(2)}) collective-permute-start(bf16[8,64,128]{2,1,0:T(8,128)(2,1)S(1)} %get-tuple-element.53), channel_id=1, source_target_pairs={{0,3},{1,2},{2,1},{3,0},{4,7},{5,6},{6,5},{7,4},{8,11},{9,10},{10,... | collective-permute-start | bytes 393224 | tf_op jit(solution)/shard_map/ppermute | solution.py:392
  14.9 3.1 %collective-permute-done.1.near = bf16[8,64,128]{2,1,0:T(8,128)(2,1)S(1)} collective-permute-done((bf16[8,64,128]{2,1,0:T(8,128)(2,1)S(1)}, bf16[8,64,128]{2,1,0:T(8,128)(2,1)S(1)}, u32[]{:S(2)}, u32[]{:S(2)}) %collective-permute-start.1) | collective-permute-done | bytes 131104 | tf_op jit(solution)/shard_map/ppermute | solution.py:392
  18.0 2.3 %shard_map.69 = (f32[1536,128]{1,0:T(8,128)S(1)}, f32[1536,128]{1,0:T(8,128)S(1)}, f32[2,16,128]{2,1,0:T(8,128)S(1)}) custom-call(s32[4]{0:T(128)S(1)} %pad_add_fusion.pos, f32[1536]{0:T(1024)S(1)} %reshape.32.tab, f32[12]{0:T(128)S(1)} %copy-done.1, bf16[8,64,128]{2,1,0:T(8,128)(2,1)S(1)} %get-tuple-element.48.mine, ...), custom_call_target="tpu_custom_call" | custom-call | flops 20000000 | bytes 1000000 | tf_op jit(solution)/shard_map/pallas_call | solution.py:32
  20.4 3.7 %collective-permute-done.2.far = bf16[8,64,128]{2,1,0:T(8,128)(2,1)S(1)} collective-permute-done((bf16[8,64,128]{2,1,0:T(8,128)(2,1)S(1)}, bf16[8,64,128]{2,1,0:T(8,128)(2,1)S(1)}, u32[]{:S(2)}, u32[]{:S(2)}) %collective-permute-start.2) | collective-permute-done | bytes 131104 | tf_op jit(solution)/shard_map/ppermute | solution.py:392
  25.5 2.7 %collective-permute-start.3 = (bf16[384,128]{1,0:T(8,128)(2,1)S(1)}, bf16[384,128]{1,0:T(8,128)(2,1)S(1)}, u32[]{:S(2)}, u32[]{:S(2)}) collective-permute-start(bf16[384,128]{1,0:T(8,128)(2,1)S(1)} %get-tuple-element.59), channel_id=1, source_target_pairs={{0,4},{4,0},{8,12},{12,8},{16,20},{20,16},{24,28},{28,24},{32,36},... | collective-permute-start | bytes 294920 | tf_op jit(solution)/shard_map/ppermute | solution.py:400
  28.2 11.2 %collective-permute-start.4 = (bf16[384,128]{1,0:T(8,128)(2,1)S(1)}, bf16[384,128]{1,0:T(8,128)(2,1)S(1)}, u32[]{:S(2)}, u32[]{:S(2)}) collective-permute-start(bf16[384,128]{1,0:T(8,128)(2,1)S(1)} %get-tuple-element.60), channel_id=1, source_target_pairs={{4,8},{8,4},{12,16},{16,12},{20,24},{24,20},{28,32},{32,28},{36,40... | collective-permute-start | bytes 294920 | tf_op jit(solution)/shard_map/ppermute | solution.py:398
  39.4 3.2 %collective-permute-start.5 = (bf16[384,128]{1,0:T(8,128)(2,1)S(1)}, bf16[384,128]{1,0:T(8,128)(2,1)S(1)}, u32[]{:S(2)}, u32[]{:S(2)}) collective-permute-start(bf16[384,128]{1,0:T(8,128)(2,1)S(1)} %get-tuple-element.61), channel_id=1, source_target_pairs={{0,1},{1,0},{49,48},{48,49},{96,97},{97,96},{145,144},{144,145},{1... | collective-permute-start | bytes 294920 | tf_op jit(solution)/shard_map/ppermute | solution.py:402
  42.6 1.9 %collective-permute-start.6 = (bf16[384,128]{1,0:T(8,128)(2,1)S(1)}, bf16[384,128]{1,0:T(8,128)(2,1)S(1)}, u32[]{:S(2)}, u32[]{:S(2)}) collective-permute-start(bf16[384,128]{1,0:T(8,128)(2,1)S(1)} %get-tuple-element.62), channel_id=1, source_target_pairs={{1,49},{49,1},{48,96},{96,48},{97,145},{145,97},{144,192},{192,144... | collective-permute-start | bytes 294920 | tf_op jit(solution)/shard_map/ppermute | solution.py:401
  44.6 2.3 %shard_map.71 = (f32[1536,128]{1,0:T(8,128)S(1)}, f32[1536,128]{1,0:T(8,128)S(1)}, f32[1536,128]{1,0:T(8,128)S(1)}, f32[1536,128]{1,0:T(8,128)S(1)}, f32[1536,12...) custom-call(s32[4]{0:T(128)S(1)} %pad_add_fusion.pos, f32[1536,128]{1,0:T(8,128)S(1)} %get-tuple-element.51.e, ...), custom_call_target="tpu_custom_call" | custom-call | flops 20000000 | bytes 1000000 | tf_op jit(solution)/shard_map/pallas_call | solution.py:32
  46.9 1.6 %collective-permute-done.6.h3 = bf16[384,128]{1,0:T(8,128)(2,1)S(1)} collective-permute-done((bf16[384,128]{1,0:T(8,128)(2,1)S(1)}, bf16[384,128]{1,0:T(8,128)(2,1)S(1)}, u32[]{:S(2)}, u32[]{:S(2)}) %collective-permute-start.6) | collective-permute-done | bytes 98336 | tf_op jit(solution)/shard_map/ppermute | solution.py:401
  49.9 5.2 %collective-permute-start.7 = (f32[128,128]{1,0:T(8,128)S(1)}, f32[128,128]{1,0:T(8,128)S(1)}, u32[]{:S(2)}, u32[]{:S(2)}) collective-permute-start(f32[128,128]{1,0:T(8,128)S(1)} %get-tuple-element.64.sums), channel_id=1, source_target_pairs={{0,2},{1,3},{2,0},{3,1},{4,6},{5,7},{6,4},{7,5},{8,10},{9,11},{10,... | collective-permute-start | bytes 196616 | tf_op jit(solution)/shard_map/ppermute | solution.py:392
  55.0 1.9 %collective-permute-start.8 = (bf16[192,128]{1,0:T(8,128)(2,1)S(1)}, bf16[192,128]{1,0:T(8,128)(2,1)S(1)}, u32[]{:S(2)}, u32[]{:S(2)}) collective-permute-start(bf16[192,128]{1,0:T(8,128)(2,1)S(1)} %get-tuple-element.72), channel_id=1, source_target_pairs={{0,4},{4,0},{8,12},{12,8},{16,20},{20,16},{24,28},{28,24},{32,36},... | collective-permute-start | bytes 147464 | tf_op jit(solution)/shard_map/ppermute | solution.py:400
  57.0 5.4 %collective-permute-start.9 = (bf16[192,128]{1,0:T(8,128)(2,1)S(1)}, bf16[192,128]{1,0:T(8,128)(2,1)S(1)}, u32[]{:S(2)}, u32[]{:S(2)}) collective-permute-start(bf16[192,128]{1,0:T(8,128)(2,1)S(1)} %get-tuple-element.73), channel_id=1, source_target_pairs={{4,8},{8,4},{12,16},{16,12},{20,24},{24,20},{28,32},{32,28},{36,40... | collective-permute-start | bytes 147464 | tf_op jit(solution)/shard_map/ppermute | solution.py:398
  62.3 4.3 %collective-permute-start.10 = (bf16[192,128]{1,0:T(8,128)(2,1)S(1)}, bf16[192,128]{1,0:T(8,128)(2,1)S(1)}, u32[]{:S(2)}, u32[]{:S(2)}) collective-permute-start(bf16[192,128]{1,0:T(8,128)(2,1)S(1)} %get-tuple-element.74), channel_id=1, source_target_pairs={{0,1},{1,0},{49,48},{48,49},{96,97},{97,96},{145,144},{144,145},{1... | collective-permute-start | bytes 147464 | tf_op jit(solution)/shard_map/ppermute | solution.py:402
  66.6 1.9 %collective-permute-start.11 = (bf16[192,128]{1,0:T(8,128)(2,1)S(1)}, bf16[192,128]{1,0:T(8,128)(2,1)S(1)}, u32[]{:S(2)}, u32[]{:S(2)}) collective-permute-start(bf16[192,128]{1,0:T(8,128)(2,1)S(1)} %get-tuple-element.75), channel_id=1, source_target_pairs={{1,49},{49,1},{48,96},{96,48},{97,145},{145,97},{144,192},{192,144... | collective-permute-start | bytes 147464 | tf_op jit(solution)/shard_map/ppermute | solution.py:401
  68.6 2.2 %shard_map.73 = (f32[1536,128]{1,0:T(8,128)S(1)}, f32[1536,128]{1,0:T(8,128)S(1)}) custom-call(s32[4]{0:T(128)S(1)} %pad_add_fusion.pos, f32[1536,128]{1,0:T(8,128)S(1)} %get-tuple-element.63.e, f32[1536,128]{1,0:T(8,128)S(1)} %get-tuple-element.54.kap, f32[1536,128]{1,0:T(8,128)S(1)} %get-tuple-element.66.e01, f32[1536,128]{1,0:T(8,128)S(1)} %get-tuple-element.67.up_c, ...), custom_call_target="tpu_custom_call" | custom-call | flops 20000000 | bytes 1000000 | tf_op jit(solution)/shard_map/pallas_call | solution.py:32
  73.2 1.9 %collective-permute-start.13 = (bf16[192,128]{1,0:T(8,128)(2,1)S(1)}, bf16[192,128]{1,0:T(8,128)(2,1)S(1)}, u32[]{:S(2)}, u32[]{:S(2)}) collective-permute-start(bf16[192,128]{1,0:T(8,128)(2,1)S(1)} %get-tuple-element.82), channel_id=1, source_target_pairs={{0,4},{4,0},{8,12},{12,8},{16,20},{20,16},{24,28},{28,24},{32,36},... | collective-permute-start | bytes 147464 | tf_op jit(solution)/shard_map/ppermute | solution.py:400
  75.2 5.3 %collective-permute-start.14 = (bf16[192,128]{1,0:T(8,128)(2,1)S(1)}, bf16[192,128]{1,0:T(8,128)(2,1)S(1)}, u32[]{:S(2)}, u32[]{:S(2)}) collective-permute-start(bf16[192,128]{1,0:T(8,128)(2,1)S(1)} %get-tuple-element.83), channel_id=1, source_target_pairs={{4,8},{8,4},{12,16},{16,12},{20,24},{24,20},{28,32},{32,28},{36,40... | collective-permute-start | bytes 147464 | tf_op jit(solution)/shard_map/ppermute | solution.py:398
  80.4 2.0 %collective-permute-start.15 = (bf16[192,128]{1,0:T(8,128)(2,1)S(1)}, bf16[192,128]{1,0:T(8,128)(2,1)S(1)}, u32[]{:S(2)}, u32[]{:S(2)}) collective-permute-start(bf16[192,128]{1,0:T(8,128)(2,1)S(1)} %get-tuple-element.84), channel_id=1, source_target_pairs={{0,1},{1,0},{49,48},{48,49},{96,97},{97,96},{145,144},{144,145},{1... | collective-permute-start | bytes 147464 | tf_op jit(solution)/shard_map/ppermute | solution.py:402
  82.4 1.9 %collective-permute-start.16 = (bf16[192,128]{1,0:T(8,128)(2,1)S(1)}, bf16[192,128]{1,0:T(8,128)(2,1)S(1)}, u32[]{:S(2)}, u32[]{:S(2)}) collective-permute-start(bf16[192,128]{1,0:T(8,128)(2,1)S(1)} %get-tuple-element.85), channel_id=1, source_target_pairs={{1,49},{49,1},{48,96},{96,48},{97,145},{145,97},{144,192},{192,144... | collective-permute-start | bytes 147464 | tf_op jit(solution)/shard_map/ppermute | solution.py:401
  84.4 3.1 %collective-permute-start.12 = (f32[64,128]{1,0:T(8,128)S(1)}, f32[64,128]{1,0:T(8,128)S(1)}, u32[]{:S(2)}, u32[]{:S(2)}) collective-permute-start(f32[64,128]{1,0:T(8,128)S(1)} %get-tuple-element.79.part), channel_id=1, source_target_pairs={{0,2},{1,3},{2,0},{3,1},{4,6},{5,7},{6,4},{7,5},{8,10},{9,11},{10,... | collective-permute-start | bytes 98312 | tf_op jit(solution)/shard_map/ppermute | solution.py:392
  87.5 2.2 %shard_map.75 = (f32[1536,128]{1,0:T(8,128)S(1)}, f32[1536,128]{1,0:T(8,128)S(1)}) custom-call(s32[4]{0:T(128)S(1)} %pad_add_fusion.pos, f32[1536,128]{1,0:T(8,128)S(1)} %get-tuple-element.76.e, f32[1536,128]{1,0:T(8,128)S(1)} %get-tuple-element.54.kap, f32[1536,128]{1,0:T(8,128)S(1)} %get-tuple-element.66.e01, f32[1536,128]{1,0:T(8,128)S(1)} %get-tuple-element.67.up_c, ...), custom_call_target="tpu_custom_call" | custom-call | flops 20000000 | bytes 1000000 | tf_op jit(solution)/shard_map/pallas_call | solution.py:32
  92.3 5.0 %collective-permute-start.18 = (f32[512,128]{1,0:T(8,128)S(1)}, f32[512,128]{1,0:T(8,128)S(1)}, u32[]{:S(2)}, u32[]{:S(2)}) collective-permute-start(f32[512,128]{1,0:T(8,128)S(1)} %get-tuple-element.88), channel_id=1, source_target_pairs={{0,1},{1,0},{2,3},{3,2},{4,5},{5,4},{6,7},{7,6},{8,9},{9,8},{10,11... | collective-permute-start | bytes 786440 | tf_op jit(solution)/shard_map/ppermute | solution.py:392
  97.3 1.9 %collective-permute-start.17 = (f32[256,128]{1,0:T(8,128)S(1)}, f32[256,128]{1,0:T(8,128)S(1)}, u32[]{:S(2)}, u32[]{:S(2)}) collective-permute-start(f32[256,128]{1,0:T(8,128)S(1)} %get-tuple-element.87), channel_id=1, source_target_pairs={{0,1},{1,0},{2,3},{3,2},{4,5},{5,4},{6,7},{7,6},{8,9},{9,8},{10,11... | collective-permute-start | bytes 393224 | tf_op jit(solution)/shard_map/ppermute | solution.py:392
  99.3 2.8 %collective-permute-start.19 = (f32[64,128]{1,0:T(8,128)S(1)}, f32[64,128]{1,0:T(8,128)S(1)}, u32[]{:S(2)}, u32[]{:S(2)}) collective-permute-start(f32[64,128]{1,0:T(8,128)S(1)} %get-tuple-element.89.ksum), channel_id=1, source_target_pairs={{0,2},{1,3},{2,0},{3,1},{4,6},{5,7},{6,4},{7,5},{8,10},{9,11},{10,... | collective-permute-start | bytes 98312 | tf_op jit(solution)/shard_map/ppermute | solution.py:392
  102.1 4.6 %collective-permute-done.19.got = f32[64,128]{1,0:T(8,128)S(1)} collective-permute-done((f32[64,128]{1,0:T(8,128)S(1)}, f32[64,128]{1,0:T(8,128)S(1)}, u32[]{:S(2)}, u32[]{:S(2)}) %collective-permute-start.19) | collective-permute-done | bytes 32800 | tf_op jit(solution)/shard_map/ppermute | solution.py:392
  106.7 3.5 %collective-permute-start.20 = (f32[64,128]{1,0:T(8,128)S(1)}, f32[64,128]{1,0:T(8,128)S(1)}, u32[]{:S(2)}, u32[]{:S(2)}) collective-permute-start(f32[64,128]{1,0:T(8,128)S(1)} %shard_map.77.mine), channel_id=1, source_target_pairs={{0,1},{1,0},{2,3},{3,2},{4,5},{5,4},{6,7},{7,6},{8,9},{9,8},{10,11... | collective-permute-start | bytes 98312 | tf_op jit(solution)/shard_map/ppermute | solution.py:392
  110.3 2.3 %collective-permute-done.20.other = f32[64,128]{1,0:T(8,128)S(1)} collective-permute-done((f32[64,128]{1,0:T(8,128)S(1)}, f32[64,128]{1,0:T(8,128)S(1)}, u32[]{:S(2)}, u32[]{:S(2)}) %collective-permute-start.20) | collective-permute-done | bytes 32800 | tf_op jit(solution)/shard_map/ppermute | solution.py:392
  112.5 1.5 %shard_map.78 = (f32[1536,128]{1,0:T(8,128)}, f32[128,128]{1,0:T(8,128)}) custom-call(s32[4]{0:T(128)S(1)} %pad_add_fusion.pos, f32[768,128]{1,0:T(8,128)S(1)} %get-tuple-element.86.eown, f32[256,128]{1,0:T(8,128)S(1)} %collective-permute-done.17.ahead, f32[512,128]{1,0:T(8,128)S(1)} %collective-permute-done.18.behind, f32[64,128]{1,0:T(8,128)S(1)} %shard_map.77.mine, ...), custom_call_target="tpu_custom_call" | custom-call | flops 1000000 | bytes 1000000 | tf_op jit(solution)/shard_map/pallas_call | solution.py:32
  (29 shorter events, 7.9 us)
Async XLA Ops:
  0.7 14.1 %copy-start.2 = (bf16[32,48]{1,0:T(8,128)(2,1)S(1)}, bf16[32,48]{1,0:T(8,128)(2,1)}, u32[]{:S(2)}) copy-start(bf16[32,48]{1,0:T(8,128)(2,1)} %param.6) | copy-start | bytes 9220
  2.5 15.5 %collective-permute-start = (bf16[1328,128]{1,0:T(8,128)(2,1)S(1)}, bf16[1328,128]{1,0:T(8,128)(2,1)S(1)}, u32[]{:S(2)}, u32[]{:S(2)}) collective-permute-start(bf16[1328,128]{1,0:T(8,128)(2,1)S(1)} %get-tuple-element.49), channel_id=1, source_target_pairs={{0,1},{1,0},{2,3},{3,2},{4,5},{5,4},{6,7},{7,6},{8,9},{9,8},{10,11... | collective-permute-start | bytes 1019912 | tf_op jit(solution)/shard_map/ppermute | solution.py:392
  6.8 11.2 %collective-permute-start.1 = (bf16[8,64,128]{2,1,0:T(8,128)(2,1)S(1)}, bf16[8,64,128]{2,1,0:T(8,128)(2,1)S(1)}, u32[]{:S(2)}, u32[]{:S(2)}) collective-permute-start(bf16[8,64,128]{2,1,0:T(8,128)(2,1)S(1)} %get-tuple-element.48.mine), channel_id=1, source_target_pairs={{0,2},{1,3},{2,0},{3,1},{4,6},{5,7},{6,4},{7,5},{8,10},{9,11},{10,... | collective-permute-start | bytes 393224 | tf_op jit(solution)/shard_map/ppermute | solution.py:392
  12.9 11.2 %collective-permute-start.2 = (bf16[8,64,128]{2,1,0:T(8,128)(2,1)S(1)}, bf16[8,64,128]{2,1,0:T(8,128)(2,1)S(1)}, u32[]{:S(2)}, u32[]{:S(2)}) collective-permute-start(bf16[8,64,128]{2,1,0:T(8,128)(2,1)S(1)} %get-tuple-element.53), channel_id=1, source_target_pairs={{0,3},{1,2},{2,1},{3,0},{4,7},{5,6},{6,5},{7,4},{8,11},{9,10},{10,... | collective-permute-start | bytes 393224 | tf_op jit(solution)/shard_map/ppermute | solution.py:392
  14.9 3.1 %copy-start.1 = (f32[12]{0:T(128)S(1)}, f32[12]{0:T(128)}, u32[]{:S(2)}) copy-start(f32[12]{0:T(128)} %planck.3) | copy-start | bytes 148
  25.5 21.4 %collective-permute-start.3 = (bf16[384,128]{1,0:T(8,128)(2,1)S(1)}, bf16[384,128]{1,0:T(8,128)(2,1)S(1)}, u32[]{:S(2)}, u32[]{:S(2)}) collective-permute-start(bf16[384,128]{1,0:T(8,128)(2,1)S(1)} %get-tuple-element.59), channel_id=1, source_target_pairs={{0,4},{4,0},{8,12},{12,8},{16,20},{20,16},{24,28},{28,24},{32,36},... | collective-permute-start | bytes 294920 | tf_op jit(solution)/shard_map/ppermute | solution.py:400
  28.2 18.7 %collective-permute-start.4 = (bf16[384,128]{1,0:T(8,128)(2,1)S(1)}, bf16[384,128]{1,0:T(8,128)(2,1)S(1)}, u32[]{:S(2)}, u32[]{:S(2)}) collective-permute-start(bf16[384,128]{1,0:T(8,128)(2,1)S(1)} %get-tuple-element.60), channel_id=1, source_target_pairs={{4,8},{8,4},{12,16},{16,12},{20,24},{24,20},{28,32},{32,28},{36,40... | collective-permute-start | bytes 294920 | tf_op jit(solution)/shard_map/ppermute | solution.py:398
  39.4 7.5 %collective-permute-start.5 = (bf16[384,128]{1,0:T(8,128)(2,1)S(1)}, bf16[384,128]{1,0:T(8,128)(2,1)S(1)}, u32[]{:S(2)}, u32[]{:S(2)}) collective-permute-start(bf16[384,128]{1,0:T(8,128)(2,1)S(1)} %get-tuple-element.61), channel_id=1, source_target_pairs={{0,1},{1,0},{49,48},{48,49},{96,97},{97,96},{145,144},{144,145},{1... | collective-permute-start | bytes 294920 | tf_op jit(solution)/shard_map/ppermute | solution.py:402
  42.6 5.9 %collective-permute-start.6 = (bf16[384,128]{1,0:T(8,128)(2,1)S(1)}, bf16[384,128]{1,0:T(8,128)(2,1)S(1)}, u32[]{:S(2)}, u32[]{:S(2)}) collective-permute-start(bf16[384,128]{1,0:T(8,128)(2,1)S(1)} %get-tuple-element.62), channel_id=1, source_target_pairs={{1,49},{49,1},{48,96},{96,48},{97,145},{145,97},{144,192},{192,144... | collective-permute-start | bytes 294920 | tf_op jit(solution)/shard_map/ppermute | solution.py:401
  44.6 4.0 %copy-start = (f32[16,8,128]{2,1,0:T(8,128)S(1)}, f32[16,8,128]{2,1,0:T(8,128)}, u32[]{:S(2)}) copy-start(f32[16,8,128]{2,1,0:T(8,128)} %param.9) | copy-start | bytes 196612
  49.9 22.2 %collective-permute-start.7 = (f32[128,128]{1,0:T(8,128)S(1)}, f32[128,128]{1,0:T(8,128)S(1)}, u32[]{:S(2)}, u32[]{:S(2)}) collective-permute-start(f32[128,128]{1,0:T(8,128)S(1)} %get-tuple-element.64.sums), channel_id=1, source_target_pairs={{0,2},{1,3},{2,0},{3,1},{4,6},{5,7},{6,4},{7,5},{8,10},{9,11},{10,... | collective-permute-start | bytes 196616 | tf_op jit(solution)/shard_map/ppermute | solution.py:392
  55.0 15.7 %collective-permute-start.8 = (bf16[192,128]{1,0:T(8,128)(2,1)S(1)}, bf16[192,128]{1,0:T(8,128)(2,1)S(1)}, u32[]{:S(2)}, u32[]{:S(2)}) collective-permute-start(bf16[192,128]{1,0:T(8,128)(2,1)S(1)} %get-tuple-element.72), channel_id=1, source_target_pairs={{0,4},{4,0},{8,12},{12,8},{16,20},{20,16},{24,28},{28,24},{32,36},... | collective-permute-start | bytes 147464 | tf_op jit(solution)/shard_map/ppermute | solution.py:400
  57.0 13.8 %collective-permute-start.9 = (bf16[192,128]{1,0:T(8,128)(2,1)S(1)}, bf16[192,128]{1,0:T(8,128)(2,1)S(1)}, u32[]{:S(2)}, u32[]{:S(2)}) collective-permute-start(bf16[192,128]{1,0:T(8,128)(2,1)S(1)} %get-tuple-element.73), channel_id=1, source_target_pairs={{4,8},{8,4},{12,16},{16,12},{20,24},{24,20},{28,32},{32,28},{36,40... | collective-permute-start | bytes 147464 | tf_op jit(solution)/shard_map/ppermute | solution.py:398
  62.3 8.4 %collective-permute-start.10 = (bf16[192,128]{1,0:T(8,128)(2,1)S(1)}, bf16[192,128]{1,0:T(8,128)(2,1)S(1)}, u32[]{:S(2)}, u32[]{:S(2)}) collective-permute-start(bf16[192,128]{1,0:T(8,128)(2,1)S(1)} %get-tuple-element.74), channel_id=1, source_target_pairs={{0,1},{1,0},{49,48},{48,49},{96,97},{97,96},{145,144},{144,145},{1... | collective-permute-start | bytes 147464 | tf_op jit(solution)/shard_map/ppermute | solution.py:402
  66.6 5.4 %collective-permute-start.11 = (bf16[192,128]{1,0:T(8,128)(2,1)S(1)}, bf16[192,128]{1,0:T(8,128)(2,1)S(1)}, u32[]{:S(2)}, u32[]{:S(2)}) collective-permute-start(bf16[192,128]{1,0:T(8,128)(2,1)S(1)} %get-tuple-element.75), channel_id=1, source_target_pairs={{1,49},{49,1},{48,96},{96,48},{97,145},{145,97},{144,192},{192,144... | collective-permute-start | bytes 147464 | tf_op jit(solution)/shard_map/ppermute | solution.py:401
  73.2 17.8 %collective-permute-start.13 = (bf16[192,128]{1,0:T(8,128)(2,1)S(1)}, bf16[192,128]{1,0:T(8,128)(2,1)S(1)}, u32[]{:S(2)}, u32[]{:S(2)}) collective-permute-start(bf16[192,128]{1,0:T(8,128)(2,1)S(1)} %get-tuple-element.82), channel_id=1, source_target_pairs={{0,4},{4,0},{8,12},{12,8},{16,20},{20,16},{24,28},{28,24},{32,36},... | collective-permute-start | bytes 147464 | tf_op jit(solution)/shard_map/ppermute | solution.py:400
  75.2 15.9 %collective-permute-start.14 = (bf16[192,128]{1,0:T(8,128)(2,1)S(1)}, bf16[192,128]{1,0:T(8,128)(2,1)S(1)}, u32[]{:S(2)}, u32[]{:S(2)}) collective-permute-start(bf16[192,128]{1,0:T(8,128)(2,1)S(1)} %get-tuple-element.83), channel_id=1, source_target_pairs={{4,8},{8,4},{12,16},{16,12},{20,24},{24,20},{28,32},{32,28},{36,40... | collective-permute-start | bytes 147464 | tf_op jit(solution)/shard_map/ppermute | solution.py:398
  80.4 10.7 %collective-permute-start.15 = (bf16[192,128]{1,0:T(8,128)(2,1)S(1)}, bf16[192,128]{1,0:T(8,128)(2,1)S(1)}, u32[]{:S(2)}, u32[]{:S(2)}) collective-permute-start(bf16[192,128]{1,0:T(8,128)(2,1)S(1)} %get-tuple-element.84), channel_id=1, source_target_pairs={{0,1},{1,0},{49,48},{48,49},{96,97},{97,96},{145,144},{144,145},{1... | collective-permute-start | bytes 147464 | tf_op jit(solution)/shard_map/ppermute | solution.py:402
  82.4 8.7 %collective-permute-start.16 = (bf16[192,128]{1,0:T(8,128)(2,1)S(1)}, bf16[192,128]{1,0:T(8,128)(2,1)S(1)}, u32[]{:S(2)}, u32[]{:S(2)}) collective-permute-start(bf16[192,128]{1,0:T(8,128)(2,1)S(1)} %get-tuple-element.85), channel_id=1, source_target_pairs={{1,49},{49,1},{48,96},{96,48},{97,145},{145,97},{144,192},{192,144... | collective-permute-start | bytes 147464 | tf_op jit(solution)/shard_map/ppermute | solution.py:401
  84.4 6.7 %collective-permute-start.12 = (f32[64,128]{1,0:T(8,128)S(1)}, f32[64,128]{1,0:T(8,128)S(1)}, u32[]{:S(2)}, u32[]{:S(2)}) collective-permute-start(f32[64,128]{1,0:T(8,128)S(1)} %get-tuple-element.79.part), channel_id=1, source_target_pairs={{0,2},{1,3},{2,0},{3,1},{4,6},{5,7},{6,4},{7,5},{8,10},{9,11},{10,... | collective-permute-start | bytes 98312 | tf_op jit(solution)/shard_map/ppermute | solution.py:392
  92.3 20.2 %collective-permute-start.18 = (f32[512,128]{1,0:T(8,128)S(1)}, f32[512,128]{1,0:T(8,128)S(1)}, u32[]{:S(2)}, u32[]{:S(2)}) collective-permute-start(f32[512,128]{1,0:T(8,128)S(1)} %get-tuple-element.88), channel_id=1, source_target_pairs={{0,1},{1,0},{2,3},{3,2},{4,5},{5,4},{6,7},{7,6},{8,9},{9,8},{10,11... | collective-permute-start | bytes 786440 | tf_op jit(solution)/shard_map/ppermute | solution.py:392
  97.3 15.2 %collective-permute-start.17 = (f32[256,128]{1,0:T(8,128)S(1)}, f32[256,128]{1,0:T(8,128)S(1)}, u32[]{:S(2)}, u32[]{:S(2)}) collective-permute-start(f32[256,128]{1,0:T(8,128)S(1)} %get-tuple-element.87), channel_id=1, source_target_pairs={{0,1},{1,0},{2,3},{3,2},{4,5},{5,4},{6,7},{7,6},{8,9},{9,8},{10,11... | collective-permute-start | bytes 393224 | tf_op jit(solution)/shard_map/ppermute | solution.py:392
  99.3 7.4 %collective-permute-start.19 = (f32[64,128]{1,0:T(8,128)S(1)}, f32[64,128]{1,0:T(8,128)S(1)}, u32[]{:S(2)}, u32[]{:S(2)}) collective-permute-start(f32[64,128]{1,0:T(8,128)S(1)} %get-tuple-element.89.ksum), channel_id=1, source_target_pairs={{0,2},{1,3},{2,0},{3,1},{4,6},{5,7},{6,4},{7,5},{8,10},{9,11},{10,... | collective-permute-start | bytes 98312 | tf_op jit(solution)/shard_map/ppermute | solution.py:392
  106.7 5.8 %collective-permute-start.20 = (f32[64,128]{1,0:T(8,128)S(1)}, f32[64,128]{1,0:T(8,128)S(1)}, u32[]{:S(2)}, u32[]{:S(2)}) collective-permute-start(f32[64,128]{1,0:T(8,128)S(1)} %shard_map.77.mine), channel_id=1, source_target_pairs={{0,1},{1,0},{2,3},{3,2},{4,5},{5,4},{6,7},{7,6},{8,9},{9,8},{10,11... | collective-permute-start | bytes 98312 | tf_op jit(solution)/shard_map/ppermute | solution.py:392

commit v6 on v5

--- a/solution.py
+++ b/solution.py
@@ -26,9 +26,10 @@
 CELLS = TILES * LAT
 
 
-def call(kernel, outs, args, smem=0, scratch=(), flops=1_000_000, space=VMEM, aliases=()):
+def call(kernel, outs, args, smem=0, scratch=(), flops=1_000_000, space=VMEM, aliases=(), hbm=0):
     specs = [pl.BlockSpec(memory_space=SMEM)] * smem
-    specs += [pl.BlockSpec(memory_space=space)] * (len(args) - smem)
+    specs += [pl.BlockSpec(memory_space=space)] * (len(args) - smem - hbm)
+    specs += [pl.BlockSpec(memory_space=pl.ANY)] * hbm
     return pl.pallas_call(
         kernel,
         out_shape=outs,
@@ -54,7 +55,7 @@
 
 
 UNROLL = 4
-AHEAD = 4
+AHEAD = 2
 SIZE = BINS * ROWS * LAT
 PART = OWN * ROWS * LAT
 N = ROWS * LAT
@@ -65,7 +66,7 @@
     return pl.ds(pl.multiple_of(N * half, N), N)
 
 
-def pack_kernel(pos, planck, dust, eold, eown, pair, near, far, stage, shares, sems):
+def pack_kernel(pos, planck, dust, eold, pair, near, far, stage, shares, sems):
     half = pos[0]
     mine = pl.ds(pl.multiple_of(N * half, N), N)
     other = pl.ds(pl.multiple_of(N * (1 - half), N), N)
@@ -73,8 +74,7 @@
         pltpu.make_async_copy(dust.at[:, other, :], far, sems.at[0]),
         pltpu.make_async_copy(eold.at[:, other, :], stage, sems.at[1]),
         pltpu.make_async_copy(dust.at[:, mine, :], near, sems.at[2]),
-        pltpu.make_async_copy(eold.at[:, mine, :], eown, sems.at[3]),
-        pltpu.make_async_copy(planck, shares, sems.at[4]),
+        pltpu.make_async_copy(planck, shares, sems.at[3]),
     ]
     for copy in copies:
         copy.start()
@@ -84,7 +84,7 @@
     copies[1].wait()
     for g in range(OWN):
         pair[pl.ds(SIZE + g * N, N), :] = stage[g].astype(BF)
-    copies[4].wait()
+    copies[3].wait()
     row = lax.broadcasted_iota(jnp.int32, (2 * LAT, LANES), 0)
     share = jnp.zeros((2 * LAT, LANES), F32)
     for g in range(OWN):
@@ -94,7 +94,6 @@
         pair[pl.ds(SIZE + PART + 2 * i * LAT, 2 * LAT), :] = piece
         share = share - piece.astype(F32)
     copies[2].wait()
-    copies[3].wait()
 
 
 def write_slabs(pos, src, at, t1, t2, r1, r2):
@@ -123,35 +122,25 @@
         r2[pl.ds(at + g * LAT, 2 * LAT), :] = edge((ROWS - 1) * part)
 
 
-def gather_bins(tab, wide, place, blocks, g, acc):
-    first = (place // 2) * GROUPS
-    for j, k in enumerate(blocks):
-        source = jnp.bitwise_xor(place, k)
-        for b in range(BINS):
-            t = SCALE * tab[(source * BINS + b) * 2 * GROUPS + first + g]
-            for r in range(ROWS):
-                term = t * wide[tile((j * BINS + b) * ROWS + r), :]
-                acc[r] = term if acc[r] is None else acc[r] + term
-    return acc
-
-
-def early_kernel(pos, tab, planck, mine, pair, near, eown, kap, e, share, wide):
+def widen(wide, tile_of, source):
+    for b in range(BINS):
+        for r in range(ROWS):
+            wide[tile(r * 4 * BINS + source * BINS + b), :] = tile_of(b, r).astype(F32)
+
+
+def early_kernel(pos, planck, mine, pair, near, eold, wide, e, share, sems):
     place = pos[2]
     slot = place % 2
-    for b in range(BINS):
-        wide[pl.ds(b * N, N), :] = mine[b].astype(F32)
-        wide[pl.ds(SIZE + b * N, N), :] = pair[pl.ds(b * N, N), :].astype(F32)
-        wide[pl.ds(2 * SIZE + b * N, N), :] = near[b].astype(F32)
-
-    def one(g, carry):
-        acc = gather_bins(tab, wide, place, (0, 1, 2), g, [None] * ROWS)
-        for r in range(ROWS):
-            kap[tile(g * ROWS + r), :] = acc[r]
-        return carry
-
-    lax.fori_loop(0, GROUPS, one, 0, unroll=2)
+    copies = [
+        pltpu.make_async_copy(eold.at[g, half_rows(pos[0]), :], e.at[half_rows(slot * OWN + g), :], sems.at[g])
+        for g in range(OWN)
+    ]
+    for copy in copies:
+        copy.start()
+    widen(wide, lambda b, r: mine[b, tile(r), :], place)
+    widen(wide, lambda b, r: near[b, tile(r), :], jnp.bitwise_xor(place, 2))
+    widen(wide, lambda b, r: pair[tile(b * ROWS + r), :], jnp.bitwise_xor(place, 1))
     for g in range(OWN):
-        e[half_rows(slot * OWN + g), :] = eown[g]
         e[half_rows((1 - slot) * OWN + g), :] = pair[pl.ds(SIZE + g * N, N), :].astype(F32)
     at = SIZE + PART
     pieces = [pair[pl.ds(at + 2 * LAT * i, 2 * LAT), :].astype(F32) for i in range(3)]
@@ -161,21 +150,27 @@
         ours = jnp.where(row == g, planck[g], ours)
     share[slot] = ours
     share[1 - slot] = pieces[0] + pieces[1] + pieces[2]
-
-
-def late_kernel(pos, tab, part, far, e, kap, t1, t2, r1, r2, wide):
+    for copy in copies:
+        copy.wait()
+
+
+def late_kernel(pos, columns, wide_in, far, e, kap, t1, t2, r1, r2, wide, turned):
     place = pos[2]
-    for b in range(BINS):
-        wide[pl.ds(b * N, N), :] = far[b].astype(F32)
-
-    def one(g, carry):
-        acc = [part[tile(g * ROWS + r), :] for r in range(ROWS)]
-        acc = gather_bins(tab, wide, place, (3,), g, acc)
-        for r in range(ROWS):
-            kap[tile(g * ROWS + r), :] = acc[r]
+    widen(wide, lambda b, r: far[b, tile(r), :], jnp.bitwise_xor(place, 3))
+    lhs = columns[pl.ds(pl.multiple_of((place // 2) * GROUPS, LAT), GROUPS), :].astype(BF)
+
+    def one(r, carry):
+        bins = 4 * BINS
+        rhs = [wide[pl.ds(r * bins * LAT + t, bins, stride=LAT), :] for t in range(LAT)]
+        rhs = jnp.concatenate(rhs, axis=1).astype(BF)
+        out = SCALE * jnp.dot(lhs, rhs, preferred_element_type=F32)
+        for t in range(LAT):
+            turned[pl.ds(r * GROUPS * LAT + t, GROUPS, stride=LAT), :] = out[:, t * LANES : (t + 1) * LANES]
+        for g in range(GROUPS):
+            kap[tile(g * ROWS + r), :] = turned[tile(r * GROUPS + g), :]
         return carry
 
-    lax.fori_loop(0, GROUPS, one, 0, unroll=4)
+    lax.fori_loop(0, ROWS, one, 0, unroll=2)
     write_slabs(pos, e, 0, t1, t2, r1, r2)
     write_slabs(pos, kap, TILES, t1, t2, r1, r2)
 
@@ -410,34 +405,35 @@
     dust = dust.reshape(BINS, 2 * N, LANES)
     energy_old = energy_old.reshape(OWN, 2 * N, LANES)
     told = temp_old.reshape(-1, LANES)
-    tab = table.astype(F32).reshape(-1)
+    columns = table.astype(F32).T
     slabs = [held((TILES, LANES), BF)] * 4
     scratch = [VMEM((N, LANES), F32), VMEM((4, TILES, LANES), F32)]
     full = held((CELLS, LANES))
     sheet = held((N, LANES))
     block = held((BINS, N, LANES), BF)
 
-    eown, pair, mine, far = call(
+    pair, mine, far = call(
         pack_kernel,
-        [held((OWN, N, LANES)), held((SIZE + PART + 6 * LAT, LANES), BF), block, block],
+        [held((SIZE + PART + 6 * LAT, LANES), BF), block, block],
         (pos, *(pltpu.with_memory_space_constraint(x, pltpu.HBM) for x in (planck, dust, energy_old))), smem=1, space=pl.ANY,
-        scratch=[VMEM((OWN, N, LANES), F32), SMEM(planck.shape, F32), pltpu.SemaphoreType.DMA((5,))],
+        scratch=[VMEM((OWN, N, LANES), F32), SMEM(planck.shape, F32), pltpu.SemaphoreType.DMA((4,))],
     )
     pair = xor(pair, 1)
     near = xor(mine, 2)
     far = xor(far, 3)
-    early, e, share = call(
-        early_kernel, [full, full, held((2, 2 * LAT, LANES))],
-        (pos, tab, planck, keep(mine), keep(pair), keep(near), keep(eown)), smem=3,
-        scratch=[VMEM((3 * SIZE, LANES), F32)], flops=20_000_000,
+    wide, e, share = call(
+        early_kernel, [held((4 * SIZE, LANES)), full, held((2, 2 * LAT, LANES))],
+        (pos, planck, keep(mine), keep(pair), keep(near), pltpu.with_memory_space_constraint(energy_old, pltpu.HBM)),
+        smem=2, hbm=1, flops=20_000_000, scratch=[pltpu.SemaphoreType.DMA((OWN,))],
     )
     e = keep(e)
     kap, *both = call(
         late_kernel,
-        [full] + [held((2 * TILES, LANES), BF)] * 4,
-        (pos, tab, keep(early), keep(far), e), smem=2,
-        scratch=[VMEM((SIZE, LANES), F32)], flops=5_000_000,
-    )
+        [full] + [held((2 * TILES, LANES), BF)] * 4 + [held((4 * SIZE, LANES))],
+        (pos, keep(columns), keep(wide), keep(far), e), smem=1,
+        scratch=[VMEM((CELLS, LANES), F32)], flops=5_000_000, aliases=((2, 5),),
+    )
+    both = both[:4]
     kap, share = keep(kap), keep(share)
     halos, _ = swap_halos(both)
     numer, denom, *coefs, e01, ssum = call(

time: 115 us -> 114 us (level)
  starting transfers between devices: 77.5 us -> 75.1 us
  waiting for transfers between devices: 18.1 us -> 20.2 us
    ppermute x9, starting transfers between devices: 33.9 us -> 30.8 us  [xor(): return lax.ppermute(x, 'group', [(i, i ^ k) for i in range(4)])]
    ppermute x9, waiting for transfers between devices: 15.1 us -> 17.2 us  [xor(): return lax.ppermute(x, 'group', [(i, i ^ k) for i in range(4)])]
    ppermute x3, starting transfers between devices: 21.8 us -> 23.1 us  [swap_halos(): t2 = lax.ppermute(t2, 'theta', theta_pairs(nt, 1))]
  transfers between devices with their start and end apart: 21 -> 21, of which waited for: 7 -> 8; matrix products, arithmetic and copies ran while one was open for 0% -> 0% of each run, Pallas kernels for 8% -> 7%
where the time goes in v6:
time: 114 us; the launch traced here: 113 us
  starting transfers between devices  75.1 us (66%)
  waiting for transfers between devices  20.2 us (18%)
  Pallas kernels  16.6 us (15%)
    ppermute x9, starting transfers between devices, xor(): return lax.ppermute(x, 'group', [(i, i ^ k) for i in range(4)])  30.8 us
    ppermute x3, starting transfers between devices, swap_halos(): t2 = lax.ppermute(t2, 'theta', theta_pairs(nt, 1))  23.1 us
    ppermute x9, waiting for transfers between devices, xor(): return lax.ppermute(x, 'group', [(i, i ^ k) for i in range(4)])  17.2 us
    pallas_call x11, Pallas kernels, call(): pl.pallas_call(kernel, out_shape=outs, in_specs=specs, out_specs=[pl.Bloc...  16.6 us
    ppermute x3, starting transfers between devices, swap_halos(): r1 = lax.ppermute(r1, ('row', 'group'), row_pairs(nr, 0))  8.8 us
    ppermute x3, starting transfers between devices, swap_halos(): t1 = lax.ppermute(t1, 'theta', theta_pairs(nt, 0))  6.58 us
    ppermute x3, starting transfers between devices, swap_halos(): r2 = lax.ppermute(r2, ('row', 'group'), row_pairs(nr, 1))  5.76 us
    ppermute x3, waiting for transfers between devices, swap_halos(): r2 = lax.ppermute(r2, ('row', 'group'), row_pairs(nr, 1))  2.61 us
  transfers between devices with their start and end apart: 21, of which 8 were waited for; matrix products, arithmetic and copies ran while one was open for 0% of the time, Pallas kernels for 7%

profile of v6, /device:TPU:30, one launch (start us, length us, event | category | flops | bytes accessed | tf_op | source)
XLA Modules:
  0.0 113.0 jit_solution(12023611386171334659)
XLA Ops:
  0.7 1.7 %shard_map.68 = (bf16[1328,128]{1,0:T(8,128)(2,1)S(1)}, bf16[8,64,128]{2,1,0:T(8,128)(2,1)S(1)}, bf16[8,64,128]{2,1,0:T(8,128)(2,1)S(1)}) custom-call(s32[4]{0:T(128)S(1)} %pad_add_fusion.pos, f32[12]{0:T(128)} %planck.3, bf16[8,128,128]{2,1,0:T(8,128)(2,1)} %bitcast.16, f32[12,128,128]{2,1,0:T(8,128)} %bitcast.14), custom_call_target="tpu_custom_call" | custom-call | flops 1000000 | bytes 1000000 | tf_op jit(solution)/shard_map/pallas_call | solution.py:33
  2.4 4.3 %collective-permute-start = (bf16[1328,128]{1,0:T(8,128)(2,1)S(1)}, bf16[1328,128]{1,0:T(8,128)(2,1)S(1)}, u32[]{:S(2)}, u32[]{:S(2)}) collective-permute-start(bf16[1328,128]{1,0:T(8,128)(2,1)S(1)} %get-tuple-element.48), channel_id=1, source_target_pairs={{0,1},{1,0},{2,3},{3,2},{4,5},{5,4},{6,7},{7,6},{8,9},{9,8},{10,11... | collective-permute-start | bytes 1019912 | tf_op jit(solution)/shard_map/ppermute | solution.py:387
  6.7 6.1 %collective-permute-start.1 = (bf16[8,64,128]{2,1,0:T(8,128)(2,1)S(1)}, bf16[8,64,128]{2,1,0:T(8,128)(2,1)S(1)}, u32[]{:S(2)}, u32[]{:S(2)}) collective-permute-start(bf16[8,64,128]{2,1,0:T(8,128)(2,1)S(1)} %get-tuple-element.47.mine), channel_id=1, source_target_pairs={{0,2},{1,3},{2,0},{3,1},{4,6},{5,7},{6,4},{7,5},{8,10},{9,11},{10,... | collective-permute-start | bytes 393224 | tf_op jit(solution)/shard_map/ppermute | solution.py:387
  12.8 1.9 %collective-permute-start.2 = (bf16[8,64,128]{2,1,0:T(8,128)(2,1)S(1)}, bf16[8,64,128]{2,1,0:T(8,128)(2,1)S(1)}, u32[]{:S(2)}, u32[]{:S(2)}) collective-permute-start(bf16[8,64,128]{2,1,0:T(8,128)(2,1)S(1)} %get-tuple-element.51), channel_id=1, source_target_pairs={{0,3},{1,2},{2,1},{3,0},{4,7},{5,6},{6,5},{7,4},{8,11},{9,10},{10,... | collective-permute-start | bytes 393224 | tf_op jit(solution)/shard_map/ppermute | solution.py:387
  14.8 3.1 %collective-permute-done.1.near = bf16[8,64,128]{2,1,0:T(8,128)(2,1)S(1)} collective-permute-done((bf16[8,64,128]{2,1,0:T(8,128)(2,1)S(1)}, bf16[8,64,128]{2,1,0:T(8,128)(2,1)S(1)}, u32[]{:S(2)}, u32[]{:S(2)}) %collective-permute-start.1) | collective-permute-done | bytes 131104 | tf_op jit(solution)/shard_map/ppermute | solution.py:387
  17.9 1.6 %shard_map.69 = (f32[2048,128]{1,0:T(8,128)S(1)}, f32[1536,128]{1,0:T(8,128)S(1)}, f32[2,16,128]{2,1,0:T(8,128)S(1)}) custom-call(s32[4]{0:T(128)S(1)} %pad_add_fusion.pos, f32[12]{0:T(128)S(1)} %copy-done.1, bf16[8,64,128]{2,1,0:T(8,128)(2,1)S(1)} %get-tuple-element.47.mine, bf16[1328,128]{1,0:T(8,128)(2,1)S(1)} %collective-permute-done.pair, ...), custom_call_target="tpu_custom_call" | custom-call | flops 20000000 | bytes 1000000 | tf_op jit(solution)/shard_map/pallas_call | solution.py:33
  19.5 4.5 %collective-permute-done.2.far = bf16[8,64,128]{2,1,0:T(8,128)(2,1)S(1)} collective-permute-done((bf16[8,64,128]{2,1,0:T(8,128)(2,1)S(1)}, bf16[8,64,128]{2,1,0:T(8,128)(2,1)S(1)}, u32[]{:S(2)}, u32[]{:S(2)}) %collective-permute-start.2) | collective-permute-done | bytes 131104 | tf_op jit(solution)/shard_map/ppermute | solution.py:387
  24.0 1.5 %shard_map.70 = (f32[1536,128]{1,0:T(8,128)S(1)}, bf16[384,128]{1,0:T(8,128)(2,1)S(1)}, bf16[384,128]{1,0:T(8,128)(2,1)S(1)}, bf16[384,128]{1,0:T(8,128)(2,1)S(1...) custom-call(s32[4]{0:T(128)S(1)} %pad_add_fusion.pos, ...), custom_call_target="tpu_custom_call", output_to_operand_aliasing={{5}: (2, {})} | custom-call | flops 5000000 | bytes 1000000 | tf_op jit(solution)/shard_map/pallas_call | solution.py:33
  25.5 2.7 %collective-permute-start.3 = (bf16[384,128]{1,0:T(8,128)(2,1)S(1)}, bf16[384,128]{1,0:T(8,128)(2,1)S(1)}, u32[]{:S(2)}, u32[]{:S(2)}) collective-permute-start(bf16[384,128]{1,0:T(8,128)(2,1)S(1)} %get-tuple-element.57), channel_id=1, source_target_pairs={{0,4},{4,0},{8,12},{12,8},{16,20},{20,16},{24,28},{28,24},{32,36},... | collective-permute-start | bytes 294920 | tf_op jit(solution)/shard_map/ppermute | solution.py:395
  28.2 11.2 %collective-permute-start.4 = (bf16[384,128]{1,0:T(8,128)(2,1)S(1)}, bf16[384,128]{1,0:T(8,128)(2,1)S(1)}, u32[]{:S(2)}, u32[]{:S(2)}) collective-permute-start(bf16[384,128]{1,0:T(8,128)(2,1)S(1)} %get-tuple-element.58), channel_id=1, source_target_pairs={{4,8},{8,4},{12,16},{16,12},{20,24},{24,20},{28,32},{32,28},{36,40... | collective-permute-start | bytes 294920 | tf_op jit(solution)/shard_map/ppermute | solution.py:393
  39.4 3.2 %collective-permute-start.5 = (bf16[384,128]{1,0:T(8,128)(2,1)S(1)}, bf16[384,128]{1,0:T(8,128)(2,1)S(1)}, u32[]{:S(2)}, u32[]{:S(2)}) collective-permute-start(bf16[384,128]{1,0:T(8,128)(2,1)S(1)} %get-tuple-element.59), channel_id=1, source_target_pairs={{0,1},{1,0},{49,48},{48,49},{96,97},{97,96},{145,144},{144,145},{1... | collective-permute-start | bytes 294920 | tf_op jit(solution)/shard_map/ppermute | solution.py:397
  42.7 1.9 %collective-permute-start.6 = (bf16[384,128]{1,0:T(8,128)(2,1)S(1)}, bf16[384,128]{1,0:T(8,128)(2,1)S(1)}, u32[]{:S(2)}, u32[]{:S(2)}) collective-permute-start(bf16[384,128]{1,0:T(8,128)(2,1)S(1)} %get-tuple-element.60), channel_id=1, source_target_pairs={{1,49},{49,1},{48,96},{96,48},{97,145},{145,97},{144,192},{192,144... | collective-permute-start | bytes 294920 | tf_op jit(solution)/shard_map/ppermute | solution.py:396
  44.6 2.3 %shard_map.71 = (f32[1536,128]{1,0:T(8,128)S(1)}, f32[1536,128]{1,0:T(8,128)S(1)}, f32[1536,128]{1,0:T(8,128)S(1)}, f32[1536,128]{1,0:T(8,128)S(1)}, f32[1536,12...) custom-call(s32[4]{0:T(128)S(1)} %pad_add_fusion.pos, f32[1536,128]{1,0:T(8,128)S(1)} %get-tuple-element.49.e, ...), custom_call_target="tpu_custom_call" | custom-call | flops 20000000 | bytes 1000000 | tf_op jit(solution)/shard_map/pallas_call | solution.py:33
  49.9 4.4 %collective-permute-start.7 = (f32[128,128]{1,0:T(8,128)S(1)}, f32[128,128]{1,0:T(8,128)S(1)}, u32[]{:S(2)}, u32[]{:S(2)}) collective-permute-start(f32[128,128]{1,0:T(8,128)S(1)} %get-tuple-element.62.sums), channel_id=1, source_target_pairs={{0,2},{1,3},{2,0},{3,1},{4,6},{5,7},{6,4},{7,5},{8,10},{9,11},{10,... | collective-permute-start | bytes 196616 | tf_op jit(solution)/shard_map/ppermute | solution.py:387
  54.3 1.9 %collective-permute-start.8 = (bf16[192,128]{1,0:T(8,128)(2,1)S(1)}, bf16[192,128]{1,0:T(8,128)(2,1)S(1)}, u32[]{:S(2)}, u32[]{:S(2)}) collective-permute-start(bf16[192,128]{1,0:T(8,128)(2,1)S(1)} %get-tuple-element.70), channel_id=1, source_target_pairs={{0,4},{4,0},{8,12},{12,8},{16,20},{20,16},{24,28},{28,24},{32,36},... | collective-permute-start | bytes 147464 | tf_op jit(solution)/shard_map/ppermute | solution.py:395
  56.2 6.0 %collective-permute-start.9 = (bf16[192,128]{1,0:T(8,128)(2,1)S(1)}, bf16[192,128]{1,0:T(8,128)(2,1)S(1)}, u32[]{:S(2)}, u32[]{:S(2)}) collective-permute-start(bf16[192,128]{1,0:T(8,128)(2,1)S(1)} %get-tuple-element.71), channel_id=1, source_target_pairs={{4,8},{8,4},{12,16},{16,12},{20,24},{24,20},{28,32},{32,28},{36,40... | collective-permute-start | bytes 147464 | tf_op jit(solution)/shard_map/ppermute | solution.py:393
  62.2 3.7 %collective-permute-start.10 = (bf16[192,128]{1,0:T(8,128)(2,1)S(1)}, bf16[192,128]{1,0:T(8,128)(2,1)S(1)}, u32[]{:S(2)}, u32[]{:S(2)}) collective-permute-start(bf16[192,128]{1,0:T(8,128)(2,1)S(1)} %get-tuple-element.72), channel_id=1, source_target_pairs={{0,1},{1,0},{49,48},{48,49},{96,97},{97,96},{145,144},{144,145},{1... | collective-permute-start | bytes 147464 | tf_op jit(solution)/shard_map/ppermute | solution.py:397
  65.9 1.9 %collective-permute-start.11 = (bf16[192,128]{1,0:T(8,128)(2,1)S(1)}, bf16[192,128]{1,0:T(8,128)(2,1)S(1)}, u32[]{:S(2)}, u32[]{:S(2)}) collective-permute-start(bf16[192,128]{1,0:T(8,128)(2,1)S(1)} %get-tuple-element.73), channel_id=1, source_target_pairs={{1,49},{49,1},{48,96},{96,48},{97,145},{145,97},{144,192},{192,144... | collective-permute-start | bytes 147464 | tf_op jit(solution)/shard_map/ppermute | solution.py:396
  67.8 2.2 %shard_map.73 = (f32[1536,128]{1,0:T(8,128)S(1)}, f32[1536,128]{1,0:T(8,128)S(1)}) custom-call(s32[4]{0:T(128)S(1)} %pad_add_fusion.pos, f32[1536,128]{1,0:T(8,128)S(1)} %get-tuple-element.61.e, f32[1536,128]{1,0:T(8,128)S(1)} %get-tuple-element.52.kap, f32[1536,128]{1,0:T(8,128)S(1)} %get-tuple-element.64.e01, f32[1536,128]{1,0:T(8,128)S(1)} %get-tuple-element.65.up_c, ...), custom_call_target="tpu_custom_call" | custom-call | flops 20000000 | bytes 1000000 | tf_op jit(solution)/shard_map/pallas_call | solution.py:33
  72.5 1.9 %collective-permute-start.13 = (bf16[192,128]{1,0:T(8,128)(2,1)S(1)}, bf16[192,128]{1,0:T(8,128)(2,1)S(1)}, u32[]{:S(2)}, u32[]{:S(2)}) collective-permute-start(bf16[192,128]{1,0:T(8,128)(2,1)S(1)} %get-tuple-element.80), channel_id=1, source_target_pairs={{0,4},{4,0},{8,12},{12,8},{16,20},{20,16},{24,28},{28,24},{32,36},... | collective-permute-start | bytes 147464 | tf_op jit(solution)/shard_map/ppermute | solution.py:395
  74.4 6.0 %collective-permute-start.14 = (bf16[192,128]{1,0:T(8,128)(2,1)S(1)}, bf16[192,128]{1,0:T(8,128)(2,1)S(1)}, u32[]{:S(2)}, u32[]{:S(2)}) collective-permute-start(bf16[192,128]{1,0:T(8,128)(2,1)S(1)} %get-tuple-element.81), channel_id=1, source_target_pairs={{4,8},{8,4},{12,16},{16,12},{20,24},{24,20},{28,32},{32,28},{36,40... | collective-permute-start | bytes 147464 | tf_op jit(solution)/shard_map/ppermute | solution.py:393
  80.4 1.9 %collective-permute-start.15 = (bf16[192,128]{1,0:T(8,128)(2,1)S(1)}, bf16[192,128]{1,0:T(8,128)(2,1)S(1)}, u32[]{:S(2)}, u32[]{:S(2)}) collective-permute-start(bf16[192,128]{1,0:T(8,128)(2,1)S(1)} %get-tuple-element.82), channel_id=1, source_target_pairs={{0,1},{1,0},{49,48},{48,49},{96,97},{97,96},{145,144},{144,145},{1... | collective-permute-start | bytes 147464 | tf_op jit(solution)/shard_map/ppermute | solution.py:397
  82.3 1.9 %collective-permute-start.16 = (bf16[192,128]{1,0:T(8,128)(2,1)S(1)}, bf16[192,128]{1,0:T(8,128)(2,1)S(1)}, u32[]{:S(2)}, u32[]{:S(2)}) collective-permute-start(bf16[192,128]{1,0:T(8,128)(2,1)S(1)} %get-tuple-element.83), channel_id=1, source_target_pairs={{1,49},{49,1},{48,96},{96,48},{97,145},{145,97},{144,192},{192,144... | collective-permute-start | bytes 147464 | tf_op jit(solution)/shard_map/ppermute | solution.py:396
  84.2 3.1 %collective-permute-start.12 = (f32[64,128]{1,0:T(8,128)S(1)}, f32[64,128]{1,0:T(8,128)S(1)}, u32[]{:S(2)}, u32[]{:S(2)}) collective-permute-start(f32[64,128]{1,0:T(8,128)S(1)} %get-tuple-element.77.part), channel_id=1, source_target_pairs={{0,2},{1,3},{2,0},{3,1},{4,6},{5,7},{6,4},{7,5},{8,10},{9,11},{10,... | collective-permute-start | bytes 98312 | tf_op jit(solution)/shard_map/ppermute | solution.py:387
  87.3 2.2 %shard_map.75 = (f32[1536,128]{1,0:T(8,128)S(1)}, f32[1536,128]{1,0:T(8,128)S(1)}) custom-call(s32[4]{0:T(128)S(1)} %pad_add_fusion.pos, f32[1536,128]{1,0:T(8,128)S(1)} %get-tuple-element.74.e, f32[1536,128]{1,0:T(8,128)S(1)} %get-tuple-element.52.kap, f32[1536,128]{1,0:T(8,128)S(1)} %get-tuple-element.64.e01, f32[1536,128]{1,0:T(8,128)S(1)} %get-tuple-element.65.up_c, ...), custom_call_target="tpu_custom_call" | custom-call | flops 20000000 | bytes 1000000 | tf_op jit(solution)/shard_map/pallas_call | solution.py:33
  92.2 4.7 %collective-permute-start.18 = (f32[640,128]{1,0:T(8,128)S(1)}, f32[640,128]{1,0:T(8,128)S(1)}, u32[]{:S(2)}, u32[]{:S(2)}) collective-permute-start(f32[640,128]{1,0:T(8,128)S(1)} %get-tuple-element.86), channel_id=1, source_target_pairs={{0,1},{1,0},{2,3},{3,2},{4,5},{5,4},{6,7},{7,6},{8,9},{9,8},{10,11... | collective-permute-start | bytes 983048 | tf_op jit(solution)/shard_map/ppermute | solution.py:387
  96.9 2.5 %collective-permute-start.19 = (f32[64,128]{1,0:T(8,128)S(1)}, f32[64,128]{1,0:T(8,128)S(1)}, u32[]{:S(2)}, u32[]{:S(2)}) collective-permute-start(f32[64,128]{1,0:T(8,128)S(1)} %get-tuple-element.87.ksum), channel_id=1, source_target_pairs={{0,2},{1,3},{2,0},{3,1},{4,6},{5,7},{6,4},{7,5},{8,10},{9,11},{10,... | collective-permute-start | bytes 98312 | tf_op jit(solution)/shard_map/ppermute | solution.py:387
  99.4 1.9 %collective-permute-start.17 = (f32[128,128]{1,0:T(8,128)S(1)}, f32[128,128]{1,0:T(8,128)S(1)}, u32[]{:S(2)}, u32[]{:S(2)}) collective-permute-start(f32[128,128]{1,0:T(8,128)S(1)} %get-tuple-element.85), channel_id=1, source_target_pairs={{0,1},{1,0},{2,3},{3,2},{4,5},{5,4},{6,7},{7,6},{8,9},{9,8},{10,11... | collective-permute-start | bytes 196616 | tf_op jit(solution)/shard_map/ppermute | solution.py:387
  101.3 4.4 %collective-permute-done.19.got = f32[64,128]{1,0:T(8,128)S(1)} collective-permute-done((f32[64,128]{1,0:T(8,128)S(1)}, f32[64,128]{1,0:T(8,128)S(1)}, u32[]{:S(2)}, u32[]{:S(2)}) %collective-permute-start.19) | collective-permute-done | bytes 32800 | tf_op jit(solution)/shard_map/ppermute | solution.py:387
  105.7 1.9 %collective-permute-start.20 = (f32[64,128]{1,0:T(8,128)S(1)}, f32[64,128]{1,0:T(8,128)S(1)}, u32[]{:S(2)}, u32[]{:S(2)}) collective-permute-start(f32[64,128]{1,0:T(8,128)S(1)} %shard_map.77.mine), channel_id=1, source_target_pairs={{0,1},{1,0},{2,3},{3,2},{4,5},{5,4},{6,7},{7,6},{8,9},{9,8},{10,11... | collective-permute-start | bytes 98312 | tf_op jit(solution)/shard_map/ppermute | solution.py:387
  107.7 3.9 %collective-permute-done.20.other = f32[64,128]{1,0:T(8,128)S(1)} collective-permute-done((f32[64,128]{1,0:T(8,128)S(1)}, f32[64,128]{1,0:T(8,128)S(1)}, u32[]{:S(2)}, u32[]{:S(2)}) %collective-permute-start.20) | collective-permute-done | bytes 32800 | tf_op jit(solution)/shard_map/ppermute | solution.py:387
  111.5 1.5 %shard_map.78 = (f32[1536,128]{1,0:T(8,128)}, f32[128,128]{1,0:T(8,128)}) custom-call(s32[4]{0:T(128)S(1)} %pad_add_fusion.pos, f32[768,128]{1,0:T(8,128)S(1)} %get-tuple-element.84.eown, f32[128,128]{1,0:T(8,128)S(1)} %collective-permute-done.17.ahead, f32[640,128]{1,0:T(8,128)S(1)} %collective-permute-done.18.behind, f32[64,128]{1,0:T(8,128)S(1)} %shard_map.77.mine, ...), custom_call_target="tpu_custom_call" | custom-call | flops 1000000 | bytes 1000000 | tf_op jit(solution)/shard_map/pallas_call | solution.py:33
  (29 shorter events, 8.2 us)
Async XLA Ops:
  0.7 14.0 %copy-start.2 = (bf16[32,48]{1,0:T(8,128)(2,1)S(1)}, bf16[32,48]{1,0:T(8,128)(2,1)}, u32[]{:S(2)}) copy-start(bf16[32,48]{1,0:T(8,128)(2,1)} %param.6) | copy-start | bytes 9220
  2.4 15.5 %collective-permute-start = (bf16[1328,128]{1,0:T(8,128)(2,1)S(1)}, bf16[1328,128]{1,0:T(8,128)(2,1)S(1)}, u32[]{:S(2)}, u32[]{:S(2)}) collective-permute-start(bf16[1328,128]{1,0:T(8,128)(2,1)S(1)} %get-tuple-element.48), channel_id=1, source_target_pairs={{0,1},{1,0},{2,3},{3,2},{4,5},{5,4},{6,7},{7,6},{8,9},{9,8},{10,11... | collective-permute-start | bytes 1019912 | tf_op jit(solution)/shard_map/ppermute | solution.py:387
  6.7 11.2 %collective-permute-start.1 = (bf16[8,64,128]{2,1,0:T(8,128)(2,1)S(1)}, bf16[8,64,128]{2,1,0:T(8,128)(2,1)S(1)}, u32[]{:S(2)}, u32[]{:S(2)}) collective-permute-start(bf16[8,64,128]{2,1,0:T(8,128)(2,1)S(1)} %get-tuple-element.47.mine), channel_id=1, source_target_pairs={{0,2},{1,3},{2,0},{3,1},{4,6},{5,7},{6,4},{7,5},{8,10},{9,11},{10,... | collective-permute-start | bytes 393224 | tf_op jit(solution)/shard_map/ppermute | solution.py:387
  12.8 5.1 %copy-start.1 = (f32[12]{0:T(128)S(1)}, f32[12]{0:T(128)}, u32[]{:S(2)}) copy-start(f32[12]{0:T(128)} %planck.3) | copy-start | bytes 148
  12.8 11.2 %collective-permute-start.2 = (bf16[8,64,128]{2,1,0:T(8,128)(2,1)S(1)}, bf16[8,64,128]{2,1,0:T(8,128)(2,1)S(1)}, u32[]{:S(2)}, u32[]{:S(2)}) collective-permute-start(bf16[8,64,128]{2,1,0:T(8,128)(2,1)S(1)} %get-tuple-element.51), channel_id=1, source_target_pairs={{0,3},{1,2},{2,1},{3,0},{4,7},{5,6},{6,5},{7,4},{8,11},{9,10},{10,... | collective-permute-start | bytes 393224 | tf_op jit(solution)/shard_map/ppermute | solution.py:387
  25.5 21.4 %collective-permute-start.3 = (bf16[384,128]{1,0:T(8,128)(2,1)S(1)}, bf16[384,128]{1,0:T(8,128)(2,1)S(1)}, u32[]{:S(2)}, u32[]{:S(2)}) collective-permute-start(bf16[384,128]{1,0:T(8,128)(2,1)S(1)} %get-tuple-element.57), channel_id=1, source_target_pairs={{0,4},{4,0},{8,12},{12,8},{16,20},{20,16},{24,28},{28,24},{32,36},... | collective-permute-start | bytes 294920 | tf_op jit(solution)/shard_map/ppermute | solution.py:395
  28.2 19.0 %collective-permute-start.4 = (bf16[384,128]{1,0:T(8,128)(2,1)S(1)}, bf16[384,128]{1,0:T(8,128)(2,1)S(1)}, u32[]{:S(2)}, u32[]{:S(2)}) collective-permute-start(bf16[384,128]{1,0:T(8,128)(2,1)S(1)} %get-tuple-element.58), channel_id=1, source_target_pairs={{4,8},{8,4},{12,16},{16,12},{20,24},{24,20},{28,32},{32,28},{36,40... | collective-permute-start | bytes 294920 | tf_op jit(solution)/shard_map/ppermute | solution.py:393
  39.4 7.8 %collective-permute-start.5 = (bf16[384,128]{1,0:T(8,128)(2,1)S(1)}, bf16[384,128]{1,0:T(8,128)(2,1)S(1)}, u32[]{:S(2)}, u32[]{:S(2)}) collective-permute-start(bf16[384,128]{1,0:T(8,128)(2,1)S(1)} %get-tuple-element.59), channel_id=1, source_target_pairs={{0,1},{1,0},{49,48},{48,49},{96,97},{97,96},{145,144},{144,145},{1... | collective-permute-start | bytes 294920 | tf_op jit(solution)/shard_map/ppermute | solution.py:397
  42.7 5.9 %collective-permute-start.6 = (bf16[384,128]{1,0:T(8,128)(2,1)S(1)}, bf16[384,128]{1,0:T(8,128)(2,1)S(1)}, u32[]{:S(2)}, u32[]{:S(2)}) collective-permute-start(bf16[384,128]{1,0:T(8,128)(2,1)S(1)} %get-tuple-element.60), channel_id=1, source_target_pairs={{1,49},{49,1},{48,96},{96,48},{97,145},{145,97},{144,192},{192,144... | collective-permute-start | bytes 294920 | tf_op jit(solution)/shard_map/ppermute | solution.py:396
  44.6 4.0 %copy-start = (f32[16,8,128]{2,1,0:T(8,128)S(1)}, f32[16,8,128]{2,1,0:T(8,128)}, u32[]{:S(2)}) copy-start(f32[16,8,128]{2,1,0:T(8,128)} %param.9) | copy-start | bytes 196612
  49.9 21.4 %collective-permute-start.7 = (f32[128,128]{1,0:T(8,128)S(1)}, f32[128,128]{1,0:T(8,128)S(1)}, u32[]{:S(2)}, u32[]{:S(2)}) collective-permute-start(f32[128,128]{1,0:T(8,128)S(1)} %get-tuple-element.62.sums), channel_id=1, source_target_pairs={{0,2},{1,3},{2,0},{3,1},{4,6},{5,7},{6,4},{7,5},{8,10},{9,11},{10,... | collective-permute-start | bytes 196616 | tf_op jit(solution)/shard_map/ppermute | solution.py:387
  54.3 15.7 %collective-permute-start.8 = (bf16[192,128]{1,0:T(8,128)(2,1)S(1)}, bf16[192,128]{1,0:T(8,128)(2,1)S(1)}, u32[]{:S(2)}, u32[]{:S(2)}) collective-permute-start(bf16[192,128]{1,0:T(8,128)(2,1)S(1)} %get-tuple-element.70), channel_id=1, source_target_pairs={{0,4},{4,0},{8,12},{12,8},{16,20},{20,16},{24,28},{28,24},{32,36},... | collective-permute-start | bytes 147464 | tf_op jit(solution)/shard_map/ppermute | solution.py:395
  56.2 13.8 %collective-permute-start.9 = (bf16[192,128]{1,0:T(8,128)(2,1)S(1)}, bf16[192,128]{1,0:T(8,128)(2,1)S(1)}, u32[]{:S(2)}, u32[]{:S(2)}) collective-permute-start(bf16[192,128]{1,0:T(8,128)(2,1)S(1)} %get-tuple-element.71), channel_id=1, source_target_pairs={{4,8},{8,4},{12,16},{16,12},{20,24},{24,20},{28,32},{32,28},{36,40... | collective-permute-start | bytes 147464 | tf_op jit(solution)/shard_map/ppermute | solution.py:393
  62.2 7.8 %collective-permute-start.10 = (bf16[192,128]{1,0:T(8,128)(2,1)S(1)}, bf16[192,128]{1,0:T(8,128)(2,1)S(1)}, u32[]{:S(2)}, u32[]{:S(2)}) collective-permute-start(bf16[192,128]{1,0:T(8,128)(2,1)S(1)} %get-tuple-element.72), channel_id=1, source_target_pairs={{0,1},{1,0},{49,48},{48,49},{96,97},{97,96},{145,144},{144,145},{1... | collective-permute-start | bytes 147464 | tf_op jit(solution)/shard_map/ppermute | solution.py:397
  65.9 5.4 %collective-permute-start.11 = (bf16[192,128]{1,0:T(8,128)(2,1)S(1)}, bf16[192,128]{1,0:T(8,128)(2,1)S(1)}, u32[]{:S(2)}, u32[]{:S(2)}) collective-permute-start(bf16[192,128]{1,0:T(8,128)(2,1)S(1)} %get-tuple-element.73), channel_id=1, source_target_pairs={{1,49},{49,1},{48,96},{96,48},{97,145},{145,97},{144,192},{192,144... | collective-permute-start | bytes 147464 | tf_op jit(solution)/shard_map/ppermute | solution.py:396
  72.5 18.5 %collective-permute-start.13 = (bf16[192,128]{1,0:T(8,128)(2,1)S(1)}, bf16[192,128]{1,0:T(8,128)(2,1)S(1)}, u32[]{:S(2)}, u32[]{:S(2)}) collective-permute-start(bf16[192,128]{1,0:T(8,128)(2,1)S(1)} %get-tuple-element.80), channel_id=1, source_target_pairs={{0,4},{4,0},{8,12},{12,8},{16,20},{20,16},{24,28},{28,24},{32,36},... | collective-permute-start | bytes 147464 | tf_op jit(solution)/shard_map/ppermute | solution.py:395
  74.4 16.5 %collective-permute-start.14 = (bf16[192,128]{1,0:T(8,128)(2,1)S(1)}, bf16[192,128]{1,0:T(8,128)(2,1)S(1)}, u32[]{:S(2)}, u32[]{:S(2)}) collective-permute-start(bf16[192,128]{1,0:T(8,128)(2,1)S(1)} %get-tuple-element.81), channel_id=1, source_target_pairs={{4,8},{8,4},{12,16},{16,12},{20,24},{24,20},{28,32},{32,28},{36,40... | collective-permute-start | bytes 147464 | tf_op jit(solution)/shard_map/ppermute | solution.py:393
  80.4 10.6 %collective-permute-start.15 = (bf16[192,128]{1,0:T(8,128)(2,1)S(1)}, bf16[192,128]{1,0:T(8,128)(2,1)S(1)}, u32[]{:S(2)}, u32[]{:S(2)}) collective-permute-start(bf16[192,128]{1,0:T(8,128)(2,1)S(1)} %get-tuple-element.82), channel_id=1, source_target_pairs={{0,1},{1,0},{49,48},{48,49},{96,97},{97,96},{145,144},{144,145},{1... | collective-permute-start | bytes 147464 | tf_op jit(solution)/shard_map/ppermute | solution.py:397
  82.3 8.7 %collective-permute-start.16 = (bf16[192,128]{1,0:T(8,128)(2,1)S(1)}, bf16[192,128]{1,0:T(8,128)(2,1)S(1)}, u32[]{:S(2)}, u32[]{:S(2)}) collective-permute-start(bf16[192,128]{1,0:T(8,128)(2,1)S(1)} %get-tuple-element.83), channel_id=1, source_target_pairs={{1,49},{49,1},{48,96},{96,48},{97,145},{145,97},{144,192},{192,144... | collective-permute-start | bytes 147464 | tf_op jit(solution)/shard_map/ppermute | solution.py:396
  84.2 6.7 %collective-permute-start.12 = (f32[64,128]{1,0:T(8,128)S(1)}, f32[64,128]{1,0:T(8,128)S(1)}, u32[]{:S(2)}, u32[]{:S(2)}) collective-permute-start(f32[64,128]{1,0:T(8,128)S(1)} %get-tuple-element.77.part), channel_id=1, source_target_pairs={{0,2},{1,3},{2,0},{3,1},{4,6},{5,7},{6,4},{7,5},{8,10},{9,11},{10,... | collective-permute-start | bytes 98312 | tf_op jit(solution)/shard_map/ppermute | solution.py:387
  92.2 19.3 %collective-permute-start.18 = (f32[640,128]{1,0:T(8,128)S(1)}, f32[640,128]{1,0:T(8,128)S(1)}, u32[]{:S(2)}, u32[]{:S(2)}) collective-permute-start(f32[640,128]{1,0:T(8,128)S(1)} %get-tuple-element.86), channel_id=1, source_target_pairs={{0,1},{1,0},{2,3},{3,2},{4,5},{5,4},{6,7},{7,6},{8,9},{9,8},{10,11... | collective-permute-start | bytes 983048 | tf_op jit(solution)/shard_map/ppermute | solution.py:387
  96.9 8.8 %collective-permute-start.19 = (f32[64,128]{1,0:T(8,128)S(1)}, f32[64,128]{1,0:T(8,128)S(1)}, u32[]{:S(2)}, u32[]{:S(2)}) collective-permute-start(f32[64,128]{1,0:T(8,128)S(1)} %get-tuple-element.87.ksum), channel_id=1, source_target_pairs={{0,2},{1,3},{2,0},{3,1},{4,6},{5,7},{6,4},{7,5},{8,10},{9,11},{10,... | collective-permute-start | bytes 98312 | tf_op jit(solution)/shard_map/ppermute | solution.py:387
  99.4 8.3 %collective-permute-start.17 = (f32[128,128]{1,0:T(8,128)S(1)}, f32[128,128]{1,0:T(8,128)S(1)}, u32[]{:S(2)}, u32[]{:S(2)}) collective-permute-start(f32[128,128]{1,0:T(8,128)S(1)} %get-tuple-element.85), channel_id=1, source_target_pairs={{0,1},{1,0},{2,3},{3,2},{4,5},{5,4},{6,7},{7,6},{8,9},{9,8},{10,11... | collective-permute-start | bytes 196616 | tf_op jit(solution)/shard_map/ppermute | solution.py:387
  105.7 5.8 %collective-permute-start.20 = (f32[64,128]{1,0:T(8,128)S(1)}, f32[64,128]{1,0:T(8,128)S(1)}, u32[]{:S(2)}, u32[]{:S(2)}) collective-permute-start(f32[64,128]{1,0:T(8,128)S(1)} %shard_map.77.mine), channel_id=1, source_target_pairs={{0,1},{1,0},{2,3},{3,2},{4,5},{5,4},{6,7},{7,6},{8,9},{9,8},{10,11... | collective-permute-start | bytes 98312 | tf_op jit(solution)/shard_map/ppermute | solution.py:387

commit v7 on v6

--- a/solution.py
+++ b/solution.py
@@ -26,10 +26,9 @@
 CELLS = TILES * LAT
 
 
-def call(kernel, outs, args, smem=0, scratch=(), flops=1_000_000, space=VMEM, aliases=(), hbm=0):
+def call(kernel, outs, args, smem=0, scratch=(), flops=1_000_000, space=VMEM, aliases=()):
     specs = [pl.BlockSpec(memory_space=SMEM)] * smem
-    specs += [pl.BlockSpec(memory_space=space)] * (len(args) - smem - hbm)
-    specs += [pl.BlockSpec(memory_space=pl.ANY)] * hbm
+    specs += [pl.BlockSpec(memory_space=space)] * (len(args) - smem)
     return pl.pallas_call(
         kernel,
         out_shape=outs,
@@ -55,7 +54,7 @@
 
 
 UNROLL = 4
-AHEAD = 2
+AHEAD = 6
 SIZE = BINS * ROWS * LAT
 PART = OWN * ROWS * LAT
 N = ROWS * LAT
@@ -66,7 +65,7 @@
     return pl.ds(pl.multiple_of(N * half, N), N)
 
 
-def pack_kernel(pos, planck, dust, eold, pair, near, far, stage, shares, sems):
+def pack_kernel(pos, planck, dust, eold, eown, pair, near, far, stage, shares, sems):
     half = pos[0]
     mine = pl.ds(pl.multiple_of(N * half, N), N)
     other = pl.ds(pl.multiple_of(N * (1 - half), N), N)
@@ -74,7 +73,8 @@
         pltpu.make_async_copy(dust.at[:, other, :], far, sems.at[0]),
         pltpu.make_async_copy(eold.at[:, other, :], stage, sems.at[1]),
         pltpu.make_async_copy(dust.at[:, mine, :], near, sems.at[2]),
-        pltpu.make_async_copy(planck, shares, sems.at[3]),
+        pltpu.make_async_copy(eold.at[:, mine, :], eown, sems.at[3]),
+        pltpu.make_async_copy(planck, shares, sems.at[4]),
     ]
     for copy in copies:
         copy.start()
@@ -84,7 +84,7 @@
     copies[1].wait()
     for g in range(OWN):
         pair[pl.ds(SIZE + g * N, N), :] = stage[g].astype(BF)
-    copies[3].wait()
+    copies[4].wait()
     row = lax.broadcasted_iota(jnp.int32, (2 * LAT, LANES), 0)
     share = jnp.zeros((2 * LAT, LANES), F32)
     for g in range(OWN):
@@ -94,6 +94,7 @@
         pair[pl.ds(SIZE + PART + 2 * i * LAT, 2 * LAT), :] = piece
         share = share - piece.astype(F32)
     copies[2].wait()
+    copies[3].wait()
 
 
 def write_slabs(pos, src, at, t1, t2, r1, r2):
@@ -128,19 +129,14 @@
             wide[tile(r * 4 * BINS + source * BINS + b), :] = tile_of(b, r).astype(F32)
 
 
-def early_kernel(pos, planck, mine, pair, near, eold, wide, e, share, sems):
+def early_kernel(pos, planck, mine, pair, near, eown, wide, e, share):
     place = pos[2]
     slot = place % 2
-    copies = [
-        pltpu.make_async_copy(eold.at[g, half_rows(pos[0]), :], e.at[half_rows(slot * OWN + g), :], sems.at[g])
-        for g in range(OWN)
-    ]
-    for copy in copies:
-        copy.start()
     widen(wide, lambda b, r: mine[b, tile(r), :], place)
     widen(wide, lambda b, r: near[b, tile(r), :], jnp.bitwise_xor(place, 2))
     widen(wide, lambda b, r: pair[tile(b * ROWS + r), :], jnp.bitwise_xor(place, 1))
     for g in range(OWN):
+        e[half_rows(slot * OWN + g), :] = eown[g]
         e[half_rows((1 - slot) * OWN + g), :] = pair[pl.ds(SIZE + g * N, N), :].astype(F32)
     at = SIZE + PART
     pieces = [pair[pl.ds(at + 2 * LAT * i, 2 * LAT), :].astype(F32) for i in range(3)]
@@ -150,8 +146,6 @@
         ours = jnp.where(row == g, planck[g], ours)
     share[slot] = ours
     share[1 - slot] = pieces[0] + pieces[1] + pieces[2]
-    for copy in copies:
-        copy.wait()
 
 
 def late_kernel(pos, columns, wide_in, far, e, kap, t1, t2, r1, r2, wide, turned):
@@ -412,19 +406,18 @@
     sheet = held((N, LANES))
     block = held((BINS, N, LANES), BF)
 
-    pair, mine, far = call(
+    eown, pair, mine, far = call(
         pack_kernel,
-        [held((SIZE + PART + 6 * LAT, LANES), BF), block, block],
+        [held((OWN, N, LANES)), held((SIZE + PART + 6 * LAT, LANES), BF), block, block],
         (pos, *(pltpu.with_memory_space_constraint(x, pltpu.HBM) for x in (planck, dust, energy_old))), smem=1, space=pl.ANY,
-        scratch=[VMEM((OWN, N, LANES), F32), SMEM(planck.shape, F32), pltpu.SemaphoreType.DMA((4,))],
+        scratch=[VMEM((OWN, N, LANES), F32), SMEM(planck.shape, F32), pltpu.SemaphoreType.DMA((5,))],
     )
     pair = xor(pair, 1)
     near = xor(mine, 2)
     far = xor(far, 3)
     wide, e, share = call(
         early_kernel, [held((4 * SIZE, LANES)), full, held((2, 2 * LAT, LANES))],
-        (pos, planck, keep(mine), keep(pair), keep(near), pltpu.with_memory_space_constraint(energy_old, pltpu.HBM)),
-        smem=2, hbm=1, flops=20_000_000, scratch=[pltpu.SemaphoreType.DMA((OWN,))],
+        (pos, planck, keep(mine), keep(pair), keep(near), keep(eown)), smem=2, flops=20_000_000,
     )
     e = keep(e)
     kap, *both = call(

time: 114 us -> 114 us (level)
  the two profiles are of different devices: /device:TPU:30 before, /device:TPU:38 now
where the time goes in v7:
time: 114 us; the launch traced here: 113 us
  starting transfers between devices  75.8 us (66%)
  waiting for transfers between devices  20.5 us (18%)
  Pallas kernels  15.8 us (14%)
    ppermute x9, starting transfers between devices, xor(): return lax.ppermute(x, 'group', [(i, i ^ k) for i in range(4)])  32.6 us
    ppermute x3, starting transfers between devices, swap_halos(): t2 = lax.ppermute(t2, 'theta', theta_pairs(nt, 1))  22.2 us
    pallas_call x11, Pallas kernels, call(): pl.pallas_call(kernel, out_shape=outs, in_specs=specs, out_specs=[pl.Bloc...  15.8 us
    ppermute x9, waiting for transfers between devices, xor(): return lax.ppermute(x, 'group', [(i, i ^ k) for i in range(4)])  15.2 us
    ppermute x3, starting transfers between devices, swap_halos(): r1 = lax.ppermute(r1, ('row', 'group'), row_pairs(nr, 0))  8.61 us
    ppermute x3, starting transfers between devices, swap_halos(): t1 = lax.ppermute(t1, 'theta', theta_pairs(nt, 0))  6.57 us
    ppermute x3, starting transfers between devices, swap_halos(): r2 = lax.ppermute(r2, ('row', 'group'), row_pairs(nr, 1))  5.76 us
    ppermute x3, waiting for transfers between devices, swap_halos(): r2 = lax.ppermute(r2, ('row', 'group'), row_pairs(nr, 1))  4.97 us
  transfers between devices with their start and end apart: 21, of which 8 were waited for; matrix products, arithmetic and copies ran while one was open for 0% of the time, Pallas kernels for 6%

profile of v7, /device:TPU:38, one launch (start us, length us, event | category | flops | bytes accessed | tf_op | source)
XLA Modules:
  0.0 113.2 jit_solution(18427969609939442713)
XLA Ops:
  0.7 1.8 %shard_map.68 = (f32[12,64,128]{2,1,0:T(8,128)S(1)}, bf16[1328,128]{1,0:T(8,128)(2,1)S(1)}, bf16[8,64,128]{2,1,0:T(8,128)(2,1)S(1)}, bf16[8,64,128]{2,1,0:T(8,128)(2,1)S(1)}) custom-call(s32[4]{0:T(128)S(1)} %pad_add_fusion.pos, f32[12]{0:T(128)} %planck.3, bf16[8,128,128]{2,1,0:T(8,128)(2,1)} %bitcast.15, f32[12,128,128]{2,1,0:T(8,128)} %bitcast.14), custom_call_target="tpu_custom_call" | custom-call | flops 1000000 | bytes 1000000 | tf_op jit(solution)/shard_map/pallas_call | solution.py:32
  2.5 4.3 %collective-permute-start = (bf16[1328,128]{1,0:T(8,128)(2,1)S(1)}, bf16[1328,128]{1,0:T(8,128)(2,1)S(1)}, u32[]{:S(2)}, u32[]{:S(2)}) collective-permute-start(bf16[1328,128]{1,0:T(8,128)(2,1)S(1)} %get-tuple-element.49), channel_id=1, source_target_pairs={{0,1},{1,0},{2,3},{3,2},{4,5},{5,4},{6,7},{7,6},{8,9},{9,8},{10,11... | collective-permute-start | bytes 1019912 | tf_op jit(solution)/shard_map/ppermute | solution.py:381
  6.8 6.1 %collective-permute-start.1 = (bf16[8,64,128]{2,1,0:T(8,128)(2,1)S(1)}, bf16[8,64,128]{2,1,0:T(8,128)(2,1)S(1)}, u32[]{:S(2)}, u32[]{:S(2)}) collective-permute-start(bf16[8,64,128]{2,1,0:T(8,128)(2,1)S(1)} %get-tuple-element.48.mine), channel_id=1, source_target_pairs={{0,2},{1,3},{2,0},{3,1},{4,6},{5,7},{6,4},{7,5},{8,10},{9,11},{10,... | collective-permute-start | bytes 393224 | tf_op jit(solution)/shard_map/ppermute | solution.py:381
  12.9 1.9 %collective-permute-start.2 = (bf16[8,64,128]{2,1,0:T(8,128)(2,1)S(1)}, bf16[8,64,128]{2,1,0:T(8,128)(2,1)S(1)}, u32[]{:S(2)}, u32[]{:S(2)}) collective-permute-start(bf16[8,64,128]{2,1,0:T(8,128)(2,1)S(1)} %get-tuple-element.53), channel_id=1, source_target_pairs={{0,3},{1,2},{2,1},{3,0},{4,7},{5,6},{6,5},{7,4},{8,11},{9,10},{10,... | collective-permute-start | bytes 393224 | tf_op jit(solution)/shard_map/ppermute | solution.py:381
  15.0 3.1 %collective-permute-done.1.near = bf16[8,64,128]{2,1,0:T(8,128)(2,1)S(1)} collective-permute-done((bf16[8,64,128]{2,1,0:T(8,128)(2,1)S(1)}, bf16[8,64,128]{2,1,0:T(8,128)(2,1)S(1)}, u32[]{:S(2)}, u32[]{:S(2)}) %collective-permute-start.1) | collective-permute-done | bytes 131104 | tf_op jit(solution)/shard_map/ppermute | solution.py:381
  18.7 5.4 %collective-permute-done.2.far = bf16[8,64,128]{2,1,0:T(8,128)(2,1)S(1)} collective-permute-done((bf16[8,64,128]{2,1,0:T(8,128)(2,1)S(1)}, bf16[8,64,128]{2,1,0:T(8,128)(2,1)S(1)}, u32[]{:S(2)}, u32[]{:S(2)}) %collective-permute-start.2) | collective-permute-done | bytes 131104 | tf_op jit(solution)/shard_map/ppermute | solution.py:381
  25.6 2.7 %collective-permute-start.3 = (bf16[384,128]{1,0:T(8,128)(2,1)S(1)}, bf16[384,128]{1,0:T(8,128)(2,1)S(1)}, u32[]{:S(2)}, u32[]{:S(2)}) collective-permute-start(bf16[384,128]{1,0:T(8,128)(2,1)S(1)} %get-tuple-element.59), channel_id=1, source_target_pairs={{0,4},{4,0},{8,12},{12,8},{16,20},{20,16},{24,28},{28,24},{32,36},... | collective-permute-start | bytes 294920 | tf_op jit(solution)/shard_map/ppermute | solution.py:389
  28.4 11.2 %collective-permute-start.4 = (bf16[384,128]{1,0:T(8,128)(2,1)S(1)}, bf16[384,128]{1,0:T(8,128)(2,1)S(1)}, u32[]{:S(2)}, u32[]{:S(2)}) collective-permute-start(bf16[384,128]{1,0:T(8,128)(2,1)S(1)} %get-tuple-element.60), channel_id=1, source_target_pairs={{4,8},{8,4},{12,16},{16,12},{20,24},{24,20},{28,32},{32,28},{36,40... | collective-permute-start | bytes 294920 | tf_op jit(solution)/shard_map/ppermute | solution.py:387
  39.6 3.2 %collective-permute-start.5 = (bf16[384,128]{1,0:T(8,128)(2,1)S(1)}, bf16[384,128]{1,0:T(8,128)(2,1)S(1)}, u32[]{:S(2)}, u32[]{:S(2)}) collective-permute-start(bf16[384,128]{1,0:T(8,128)(2,1)S(1)} %get-tuple-element.61), channel_id=1, source_target_pairs={{0,1},{1,0},{49,48},{48,49},{96,97},{97,96},{145,144},{144,145},{1... | collective-permute-start | bytes 294920 | tf_op jit(solution)/shard_map/ppermute | solution.py:391
  42.8 1.9 %collective-permute-start.6 = (bf16[384,128]{1,0:T(8,128)(2,1)S(1)}, bf16[384,128]{1,0:T(8,128)(2,1)S(1)}, u32[]{:S(2)}, u32[]{:S(2)}) collective-permute-start(bf16[384,128]{1,0:T(8,128)(2,1)S(1)} %get-tuple-element.62), channel_id=1, source_target_pairs={{1,49},{49,1},{48,96},{96,48},{97,145},{145,97},{144,192},{192,144... | collective-permute-start | bytes 294920 | tf_op jit(solution)/shard_map/ppermute | solution.py:390
  44.7 2.3 %shard_map.71 = (f32[1536,128]{1,0:T(8,128)S(1)}, f32[1536,128]{1,0:T(8,128)S(1)}, f32[1536,128]{1,0:T(8,128)S(1)}, f32[1536,128]{1,0:T(8,128)S(1)}, f32[1536,12...) custom-call(s32[4]{0:T(128)S(1)} %pad_add_fusion.pos, f32[1536,128]{1,0:T(8,128)S(1)} %get-tuple-element.51.e, ...), custom_call_target="tpu_custom_call" | custom-call | flops 20000000 | bytes 1000000 | tf_op jit(solution)/shard_map/pallas_call | solution.py:32
  47.4 2.5 %collective-permute-done.6.h3 = bf16[384,128]{1,0:T(8,128)(2,1)S(1)} collective-permute-done((bf16[384,128]{1,0:T(8,128)(2,1)S(1)}, bf16[384,128]{1,0:T(8,128)(2,1)S(1)}, u32[]{:S(2)}, u32[]{:S(2)}) %collective-permute-start.6) | collective-permute-done | bytes 98336 | tf_op jit(solution)/shard_map/ppermute | solution.py:390
  51.2 3.5 %collective-permute-start.7 = (f32[128,128]{1,0:T(8,128)S(1)}, f32[128,128]{1,0:T(8,128)S(1)}, u32[]{:S(2)}, u32[]{:S(2)}) collective-permute-start(f32[128,128]{1,0:T(8,128)S(1)} %get-tuple-element.64.sums), channel_id=1, source_target_pairs={{0,2},{1,3},{2,0},{3,1},{4,6},{5,7},{6,4},{7,5},{8,10},{9,11},{10,... | collective-permute-start | bytes 196616 | tf_op jit(solution)/shard_map/ppermute | solution.py:381
  54.7 1.9 %collective-permute-start.8 = (bf16[192,128]{1,0:T(8,128)(2,1)S(1)}, bf16[192,128]{1,0:T(8,128)(2,1)S(1)}, u32[]{:S(2)}, u32[]{:S(2)}) collective-permute-start(bf16[192,128]{1,0:T(8,128)(2,1)S(1)} %get-tuple-element.72), channel_id=1, source_target_pairs={{0,4},{4,0},{8,12},{12,8},{16,20},{20,16},{24,28},{28,24},{32,36},... | collective-permute-start | bytes 147464 | tf_op jit(solution)/shard_map/ppermute | solution.py:389
  56.6 5.7 %collective-permute-start.9 = (bf16[192,128]{1,0:T(8,128)(2,1)S(1)}, bf16[192,128]{1,0:T(8,128)(2,1)S(1)}, u32[]{:S(2)}, u32[]{:S(2)}) collective-permute-start(bf16[192,128]{1,0:T(8,128)(2,1)S(1)} %get-tuple-element.73), channel_id=1, source_target_pairs={{4,8},{8,4},{12,16},{16,12},{20,24},{24,20},{28,32},{32,28},{36,40... | collective-permute-start | bytes 147464 | tf_op jit(solution)/shard_map/ppermute | solution.py:387
  62.3 3.5 %collective-permute-start.10 = (bf16[192,128]{1,0:T(8,128)(2,1)S(1)}, bf16[192,128]{1,0:T(8,128)(2,1)S(1)}, u32[]{:S(2)}, u32[]{:S(2)}) collective-permute-start(bf16[192,128]{1,0:T(8,128)(2,1)S(1)} %get-tuple-element.74), channel_id=1, source_target_pairs={{0,1},{1,0},{49,48},{48,49},{96,97},{97,96},{145,144},{144,145},{1... | collective-permute-start | bytes 147464 | tf_op jit(solution)/shard_map/ppermute | solution.py:391
  65.9 1.9 %collective-permute-start.11 = (bf16[192,128]{1,0:T(8,128)(2,1)S(1)}, bf16[192,128]{1,0:T(8,128)(2,1)S(1)}, u32[]{:S(2)}, u32[]{:S(2)}) collective-permute-start(bf16[192,128]{1,0:T(8,128)(2,1)S(1)} %get-tuple-element.75), channel_id=1, source_target_pairs={{1,49},{49,1},{48,96},{96,48},{97,145},{145,97},{144,192},{192,144... | collective-permute-start | bytes 147464 | tf_op jit(solution)/shard_map/ppermute | solution.py:390
  67.8 2.2 %shard_map.73 = (f32[1536,128]{1,0:T(8,128)S(1)}, f32[1536,128]{1,0:T(8,128)S(1)}) custom-call(s32[4]{0:T(128)S(1)} %pad_add_fusion.pos, f32[1536,128]{1,0:T(8,128)S(1)} %get-tuple-element.63.e, f32[1536,128]{1,0:T(8,128)S(1)} %get-tuple-element.54.kap, f32[1536,128]{1,0:T(8,128)S(1)} %get-tuple-element.66.e01, f32[1536,128]{1,0:T(8,128)S(1)} %get-tuple-element.67.up_c, ...), custom_call_target="tpu_custom_call" | custom-call | flops 20000000 | bytes 1000000 | tf_op jit(solution)/shard_map/pallas_call | solution.py:32
  70.0 2.5 %collective-permute-done.11.h3 = bf16[192,128]{1,0:T(8,128)(2,1)S(1)} collective-permute-done((bf16[192,128]{1,0:T(8,128)(2,1)S(1)}, bf16[192,128]{1,0:T(8,128)(2,1)S(1)}, u32[]{:S(2)}, u32[]{:S(2)}) %collective-permute-start.11) | collective-permute-done | bytes 49184 | tf_op jit(solution)/shard_map/ppermute | solution.py:390
  73.7 1.9 %collective-permute-start.13 = (bf16[192,128]{1,0:T(8,128)(2,1)S(1)}, bf16[192,128]{1,0:T(8,128)(2,1)S(1)}, u32[]{:S(2)}, u32[]{:S(2)}) collective-permute-start(bf16[192,128]{1,0:T(8,128)(2,1)S(1)} %get-tuple-element.82), channel_id=1, source_target_pairs={{0,4},{4,0},{8,12},{12,8},{16,20},{20,16},{24,28},{28,24},{32,36},... | collective-permute-start | bytes 147464 | tf_op jit(solution)/shard_map/ppermute | solution.py:389
  75.6 5.2 %collective-permute-start.14 = (bf16[192,128]{1,0:T(8,128)(2,1)S(1)}, bf16[192,128]{1,0:T(8,128)(2,1)S(1)}, u32[]{:S(2)}, u32[]{:S(2)}) collective-permute-start(bf16[192,128]{1,0:T(8,128)(2,1)S(1)} %get-tuple-element.83), channel_id=1, source_target_pairs={{4,8},{8,4},{12,16},{16,12},{20,24},{24,20},{28,32},{32,28},{36,40... | collective-permute-start | bytes 147464 | tf_op jit(solution)/shard_map/ppermute | solution.py:387
  80.8 1.9 %collective-permute-start.15 = (bf16[192,128]{1,0:T(8,128)(2,1)S(1)}, bf16[192,128]{1,0:T(8,128)(2,1)S(1)}, u32[]{:S(2)}, u32[]{:S(2)}) collective-permute-start(bf16[192,128]{1,0:T(8,128)(2,1)S(1)} %get-tuple-element.84), channel_id=1, source_target_pairs={{0,1},{1,0},{49,48},{48,49},{96,97},{97,96},{145,144},{144,145},{1... | collective-permute-start | bytes 147464 | tf_op jit(solution)/shard_map/ppermute | solution.py:391
  82.8 1.9 %collective-permute-start.16 = (bf16[192,128]{1,0:T(8,128)(2,1)S(1)}, bf16[192,128]{1,0:T(8,128)(2,1)S(1)}, u32[]{:S(2)}, u32[]{:S(2)}) collective-permute-start(bf16[192,128]{1,0:T(8,128)(2,1)S(1)} %get-tuple-element.85), channel_id=1, source_target_pairs={{1,49},{49,1},{48,96},{96,48},{97,145},{145,97},{144,192},{192,144... | collective-permute-start | bytes 147464 | tf_op jit(solution)/shard_map/ppermute | solution.py:390
  84.7 3.2 %collective-permute-start.12 = (f32[64,128]{1,0:T(8,128)S(1)}, f32[64,128]{1,0:T(8,128)S(1)}, u32[]{:S(2)}, u32[]{:S(2)}) collective-permute-start(f32[64,128]{1,0:T(8,128)S(1)} %get-tuple-element.79.part), channel_id=1, source_target_pairs={{0,2},{1,3},{2,0},{3,1},{4,6},{5,7},{6,4},{7,5},{8,10},{9,11},{10,... | collective-permute-start | bytes 98312 | tf_op jit(solution)/shard_map/ppermute | solution.py:381
  87.9 2.2 %shard_map.75 = (f32[1536,128]{1,0:T(8,128)S(1)}, f32[1536,128]{1,0:T(8,128)S(1)}) custom-call(s32[4]{0:T(128)S(1)} %pad_add_fusion.pos, f32[1536,128]{1,0:T(8,128)S(1)} %get-tuple-element.76.e, f32[1536,128]{1,0:T(8,128)S(1)} %get-tuple-element.54.kap, f32[1536,128]{1,0:T(8,128)S(1)} %get-tuple-element.66.e01, f32[1536,128]{1,0:T(8,128)S(1)} %get-tuple-element.67.up_c, ...), custom_call_target="tpu_custom_call" | custom-call | flops 20000000 | bytes 1000000 | tf_op jit(solution)/shard_map/pallas_call | solution.py:32
  92.6 3.9 %collective-permute-start.17 = (f32[384,128]{1,0:T(8,128)S(1)}, f32[384,128]{1,0:T(8,128)S(1)}, u32[]{:S(2)}, u32[]{:S(2)}) collective-permute-start(f32[384,128]{1,0:T(8,128)S(1)} %get-tuple-element.87), channel_id=1, source_target_pairs={{0,1},{1,0},{2,3},{3,2},{4,5},{5,4},{6,7},{7,6},{8,9},{9,8},{10,11... | collective-permute-start | bytes 589832 | tf_op jit(solution)/shard_map/ppermute | solution.py:381
  96.6 1.9 %collective-permute-start.18 = (f32[384,128]{1,0:T(8,128)S(1)}, f32[384,128]{1,0:T(8,128)S(1)}, u32[]{:S(2)}, u32[]{:S(2)}) collective-permute-start(f32[384,128]{1,0:T(8,128)S(1)} %get-tuple-element.88), channel_id=1, source_target_pairs={{0,1},{1,0},{2,3},{3,2},{4,5},{5,4},{6,7},{7,6},{8,9},{9,8},{10,11... | collective-permute-start | bytes 589832 | tf_op jit(solution)/shard_map/ppermute | solution.py:381
  98.5 3.3 %collective-permute-start.19 = (f32[64,128]{1,0:T(8,128)S(1)}, f32[64,128]{1,0:T(8,128)S(1)}, u32[]{:S(2)}, u32[]{:S(2)}) collective-permute-start(f32[64,128]{1,0:T(8,128)S(1)} %get-tuple-element.89.ksum), channel_id=1, source_target_pairs={{0,2},{1,3},{2,0},{3,1},{4,6},{5,7},{6,4},{7,5},{8,10},{9,11},{10,... | collective-permute-start | bytes 98312 | tf_op jit(solution)/shard_map/ppermute | solution.py:381
  101.9 3.5 %collective-permute-done.19.got = f32[64,128]{1,0:T(8,128)S(1)} collective-permute-done((f32[64,128]{1,0:T(8,128)S(1)}, f32[64,128]{1,0:T(8,128)S(1)}, u32[]{:S(2)}, u32[]{:S(2)}) %collective-permute-start.19) | collective-permute-done | bytes 32800 | tf_op jit(solution)/shard_map/ppermute | solution.py:381
  105.3 4.5 %collective-permute-start.20 = (f32[64,128]{1,0:T(8,128)S(1)}, f32[64,128]{1,0:T(8,128)S(1)}, u32[]{:S(2)}, u32[]{:S(2)}) collective-permute-start(f32[64,128]{1,0:T(8,128)S(1)} %shard_map.77.mine), channel_id=1, source_target_pairs={{0,1},{1,0},{2,3},{3,2},{4,5},{5,4},{6,7},{7,6},{8,9},{9,8},{10,11... | collective-permute-start | bytes 98312 | tf_op jit(solution)/shard_map/ppermute | solution.py:381
  109.8 1.9 %collective-permute-done.20.other = f32[64,128]{1,0:T(8,128)S(1)} collective-permute-done((f32[64,128]{1,0:T(8,128)S(1)}, f32[64,128]{1,0:T(8,128)S(1)}, u32[]{:S(2)}, u32[]{:S(2)}) %collective-permute-start.20) | collective-permute-done | bytes 32800 | tf_op jit(solution)/shard_map/ppermute | solution.py:381
  111.7 1.5 %shard_map.78 = (f32[1536,128]{1,0:T(8,128)}, f32[128,128]{1,0:T(8,128)}) custom-call(s32[4]{0:T(128)S(1)} %pad_add_fusion.pos, f32[768,128]{1,0:T(8,128)S(1)} %get-tuple-element.86.eown, f32[384,128]{1,0:T(8,128)S(1)} %collective-permute-done.17.ahead, f32[384,128]{1,0:T(8,128)S(1)} %collective-permute-done.18.behind, f32[64,128]{1,0:T(8,128)S(1)} %shard_map.77.mine, ...), custom_call_target="tpu_custom_call" | custom-call | flops 1000000 | bytes 1000000 | tf_op jit(solution)/shard_map/pallas_call | solution.py:32
  (29 shorter events, 7.7 us)
Async XLA Ops:
  0.7 14.1 %copy-start.2 = (bf16[32,48]{1,0:T(8,128)(2,1)S(1)}, bf16[32,48]{1,0:T(8,128)(2,1)}, u32[]{:S(2)}) copy-start(bf16[32,48]{1,0:T(8,128)(2,1)} %param.6) | copy-start | bytes 9220
  2.5 15.5 %collective-permute-start = (bf16[1328,128]{1,0:T(8,128)(2,1)S(1)}, bf16[1328,128]{1,0:T(8,128)(2,1)S(1)}, u32[]{:S(2)}, u32[]{:S(2)}) collective-permute-start(bf16[1328,128]{1,0:T(8,128)(2,1)S(1)} %get-tuple-element.49), channel_id=1, source_target_pairs={{0,1},{1,0},{2,3},{3,2},{4,5},{5,4},{6,7},{7,6},{8,9},{9,8},{10,11... | collective-permute-start | bytes 1019912 | tf_op jit(solution)/shard_map/ppermute | solution.py:381
  6.8 11.2 %collective-permute-start.1 = (bf16[8,64,128]{2,1,0:T(8,128)(2,1)S(1)}, bf16[8,64,128]{2,1,0:T(8,128)(2,1)S(1)}, u32[]{:S(2)}, u32[]{:S(2)}) collective-permute-start(bf16[8,64,128]{2,1,0:T(8,128)(2,1)S(1)} %get-tuple-element.48.mine), channel_id=1, source_target_pairs={{0,2},{1,3},{2,0},{3,1},{4,6},{5,7},{6,4},{7,5},{8,10},{9,11},{10,... | collective-permute-start | bytes 393224 | tf_op jit(solution)/shard_map/ppermute | solution.py:381
  12.9 11.2 %collective-permute-start.2 = (bf16[8,64,128]{2,1,0:T(8,128)(2,1)S(1)}, bf16[8,64,128]{2,1,0:T(8,128)(2,1)S(1)}, u32[]{:S(2)}, u32[]{:S(2)}) collective-permute-start(bf16[8,64,128]{2,1,0:T(8,128)(2,1)S(1)} %get-tuple-element.53), channel_id=1, source_target_pairs={{0,3},{1,2},{2,1},{3,0},{4,7},{5,6},{6,5},{7,4},{8,11},{9,10},{10,... | collective-permute-start | bytes 393224 | tf_op jit(solution)/shard_map/ppermute | solution.py:381
  15.0 3.1 %copy-start.1 = (f32[12]{0:T(128)S(1)}, f32[12]{0:T(128)}, u32[]{:S(2)}) copy-start(f32[12]{0:T(128)} %planck.3) | copy-start | bytes 148
  25.6 21.4 %collective-permute-start.3 = (bf16[384,128]{1,0:T(8,128)(2,1)S(1)}, bf16[384,128]{1,0:T(8,128)(2,1)S(1)}, u32[]{:S(2)}, u32[]{:S(2)}) collective-permute-start(bf16[384,128]{1,0:T(8,128)(2,1)S(1)} %get-tuple-element.59), channel_id=1, source_target_pairs={{0,4},{4,0},{8,12},{12,8},{16,20},{20,16},{24,28},{28,24},{32,36},... | collective-permute-start | bytes 294920 | tf_op jit(solution)/shard_map/ppermute | solution.py:389
  28.4 19.1 %collective-permute-start.4 = (bf16[384,128]{1,0:T(8,128)(2,1)S(1)}, bf16[384,128]{1,0:T(8,128)(2,1)S(1)}, u32[]{:S(2)}, u32[]{:S(2)}) collective-permute-start(bf16[384,128]{1,0:T(8,128)(2,1)S(1)} %get-tuple-element.60), channel_id=1, source_target_pairs={{4,8},{8,4},{12,16},{16,12},{20,24},{24,20},{28,32},{32,28},{36,40... | collective-permute-start | bytes 294920 | tf_op jit(solution)/shard_map/ppermute | solution.py:387
  39.6 7.8 %collective-permute-start.5 = (bf16[384,128]{1,0:T(8,128)(2,1)S(1)}, bf16[384,128]{1,0:T(8,128)(2,1)S(1)}, u32[]{:S(2)}, u32[]{:S(2)}) collective-permute-start(bf16[384,128]{1,0:T(8,128)(2,1)S(1)} %get-tuple-element.61), channel_id=1, source_target_pairs={{0,1},{1,0},{49,48},{48,49},{96,97},{97,96},{145,144},{144,145},{1... | collective-permute-start | bytes 294920 | tf_op jit(solution)/shard_map/ppermute | solution.py:391
  42.8 7.1 %collective-permute-start.6 = (bf16[384,128]{1,0:T(8,128)(2,1)S(1)}, bf16[384,128]{1,0:T(8,128)(2,1)S(1)}, u32[]{:S(2)}, u32[]{:S(2)}) collective-permute-start(bf16[384,128]{1,0:T(8,128)(2,1)S(1)} %get-tuple-element.62), channel_id=1, source_target_pairs={{1,49},{49,1},{48,96},{96,48},{97,145},{145,97},{144,192},{192,144... | collective-permute-start | bytes 294920 | tf_op jit(solution)/shard_map/ppermute | solution.py:390
  44.7 5.2 %copy-start = (f32[16,8,128]{2,1,0:T(8,128)S(1)}, f32[16,8,128]{2,1,0:T(8,128)}, u32[]{:S(2)}) copy-start(f32[16,8,128]{2,1,0:T(8,128)} %param.9) | copy-start | bytes 196612
  51.2 21.3 %collective-permute-start.7 = (f32[128,128]{1,0:T(8,128)S(1)}, f32[128,128]{1,0:T(8,128)S(1)}, u32[]{:S(2)}, u32[]{:S(2)}) collective-permute-start(f32[128,128]{1,0:T(8,128)S(1)} %get-tuple-element.64.sums), channel_id=1, source_target_pairs={{0,2},{1,3},{2,0},{3,1},{4,6},{5,7},{6,4},{7,5},{8,10},{9,11},{10,... | collective-permute-start | bytes 196616 | tf_op jit(solution)/shard_map/ppermute | solution.py:381
  54.7 15.3 %collective-permute-start.8 = (bf16[192,128]{1,0:T(8,128)(2,1)S(1)}, bf16[192,128]{1,0:T(8,128)(2,1)S(1)}, u32[]{:S(2)}, u32[]{:S(2)}) collective-permute-start(bf16[192,128]{1,0:T(8,128)(2,1)S(1)} %get-tuple-element.72), channel_id=1, source_target_pairs={{0,4},{4,0},{8,12},{12,8},{16,20},{20,16},{24,28},{28,24},{32,36},... | collective-permute-start | bytes 147464 | tf_op jit(solution)/shard_map/ppermute | solution.py:389
  56.6 13.4 %collective-permute-start.9 = (bf16[192,128]{1,0:T(8,128)(2,1)S(1)}, bf16[192,128]{1,0:T(8,128)(2,1)S(1)}, u32[]{:S(2)}, u32[]{:S(2)}) collective-permute-start(bf16[192,128]{1,0:T(8,128)(2,1)S(1)} %get-tuple-element.73), channel_id=1, source_target_pairs={{4,8},{8,4},{12,16},{16,12},{20,24},{24,20},{28,32},{32,28},{36,40... | collective-permute-start | bytes 147464 | tf_op jit(solution)/shard_map/ppermute | solution.py:387
  62.3 7.6 %collective-permute-start.10 = (bf16[192,128]{1,0:T(8,128)(2,1)S(1)}, bf16[192,128]{1,0:T(8,128)(2,1)S(1)}, u32[]{:S(2)}, u32[]{:S(2)}) collective-permute-start(bf16[192,128]{1,0:T(8,128)(2,1)S(1)} %get-tuple-element.74), channel_id=1, source_target_pairs={{0,1},{1,0},{49,48},{48,49},{96,97},{97,96},{145,144},{144,145},{1... | collective-permute-start | bytes 147464 | tf_op jit(solution)/shard_map/ppermute | solution.py:391
  65.9 6.6 %collective-permute-start.11 = (bf16[192,128]{1,0:T(8,128)(2,1)S(1)}, bf16[192,128]{1,0:T(8,128)(2,1)S(1)}, u32[]{:S(2)}, u32[]{:S(2)}) collective-permute-start(bf16[192,128]{1,0:T(8,128)(2,1)S(1)} %get-tuple-element.75), channel_id=1, source_target_pairs={{1,49},{49,1},{48,96},{96,48},{97,145},{145,97},{144,192},{192,144... | collective-permute-start | bytes 147464 | tf_op jit(solution)/shard_map/ppermute | solution.py:390
  73.7 17.7 %collective-permute-start.13 = (bf16[192,128]{1,0:T(8,128)(2,1)S(1)}, bf16[192,128]{1,0:T(8,128)(2,1)S(1)}, u32[]{:S(2)}, u32[]{:S(2)}) collective-permute-start(bf16[192,128]{1,0:T(8,128)(2,1)S(1)} %get-tuple-element.82), channel_id=1, source_target_pairs={{0,4},{4,0},{8,12},{12,8},{16,20},{20,16},{24,28},{28,24},{32,36},... | collective-permute-start | bytes 147464 | tf_op jit(solution)/shard_map/ppermute | solution.py:389
  75.6 15.8 %collective-permute-start.14 = (bf16[192,128]{1,0:T(8,128)(2,1)S(1)}, bf16[192,128]{1,0:T(8,128)(2,1)S(1)}, u32[]{:S(2)}, u32[]{:S(2)}) collective-permute-start(bf16[192,128]{1,0:T(8,128)(2,1)S(1)} %get-tuple-element.83), channel_id=1, source_target_pairs={{4,8},{8,4},{12,16},{16,12},{20,24},{24,20},{28,32},{32,28},{36,40... | collective-permute-start | bytes 147464 | tf_op jit(solution)/shard_map/ppermute | solution.py:387
  80.8 10.6 %collective-permute-start.15 = (bf16[192,128]{1,0:T(8,128)(2,1)S(1)}, bf16[192,128]{1,0:T(8,128)(2,1)S(1)}, u32[]{:S(2)}, u32[]{:S(2)}) collective-permute-start(bf16[192,128]{1,0:T(8,128)(2,1)S(1)} %get-tuple-element.84), channel_id=1, source_target_pairs={{0,1},{1,0},{49,48},{48,49},{96,97},{97,96},{145,144},{144,145},{1... | collective-permute-start | bytes 147464 | tf_op jit(solution)/shard_map/ppermute | solution.py:391
  82.8 8.7 %collective-permute-start.16 = (bf16[192,128]{1,0:T(8,128)(2,1)S(1)}, bf16[192,128]{1,0:T(8,128)(2,1)S(1)}, u32[]{:S(2)}, u32[]{:S(2)}) collective-permute-start(bf16[192,128]{1,0:T(8,128)(2,1)S(1)} %get-tuple-element.85), channel_id=1, source_target_pairs={{1,49},{49,1},{48,96},{96,48},{97,145},{145,97},{144,192},{192,144... | collective-permute-start | bytes 147464 | tf_op jit(solution)/shard_map/ppermute | solution.py:390
  84.7 6.7 %collective-permute-start.12 = (f32[64,128]{1,0:T(8,128)S(1)}, f32[64,128]{1,0:T(8,128)S(1)}, u32[]{:S(2)}, u32[]{:S(2)}) collective-permute-start(f32[64,128]{1,0:T(8,128)S(1)} %get-tuple-element.79.part), channel_id=1, source_target_pairs={{0,2},{1,3},{2,0},{3,1},{4,6},{5,7},{6,4},{7,5},{8,10},{9,11},{10,... | collective-permute-start | bytes 98312 | tf_op jit(solution)/shard_map/ppermute | solution.py:381
  92.6 19.1 %collective-permute-start.17 = (f32[384,128]{1,0:T(8,128)S(1)}, f32[384,128]{1,0:T(8,128)S(1)}, u32[]{:S(2)}, u32[]{:S(2)}) collective-permute-start(f32[384,128]{1,0:T(8,128)S(1)} %get-tuple-element.87), channel_id=1, source_target_pairs={{0,1},{1,0},{2,3},{3,2},{4,5},{5,4},{6,7},{7,6},{8,9},{9,8},{10,11... | collective-permute-start | bytes 589832 | tf_op jit(solution)/shard_map/ppermute | solution.py:381
  96.6 15.1 %collective-permute-start.18 = (f32[384,128]{1,0:T(8,128)S(1)}, f32[384,128]{1,0:T(8,128)S(1)}, u32[]{:S(2)}, u32[]{:S(2)}) collective-permute-start(f32[384,128]{1,0:T(8,128)S(1)} %get-tuple-element.88), channel_id=1, source_target_pairs={{0,1},{1,0},{2,3},{3,2},{4,5},{5,4},{6,7},{7,6},{8,9},{9,8},{10,11... | collective-permute-start | bytes 589832 | tf_op jit(solution)/shard_map/ppermute | solution.py:381
  98.5 6.8 %collective-permute-start.19 = (f32[64,128]{1,0:T(8,128)S(1)}, f32[64,128]{1,0:T(8,128)S(1)}, u32[]{:S(2)}, u32[]{:S(2)}) collective-permute-start(f32[64,128]{1,0:T(8,128)S(1)} %get-tuple-element.89.ksum), channel_id=1, source_target_pairs={{0,2},{1,3},{2,0},{3,1},{4,6},{5,7},{6,4},{7,5},{8,10},{9,11},{10,... | collective-permute-start | bytes 98312 | tf_op jit(solution)/shard_map/ppermute | solution.py:381
  105.3 6.4 %collective-permute-start.20 = (f32[64,128]{1,0:T(8,128)S(1)}, f32[64,128]{1,0:T(8,128)S(1)}, u32[]{:S(2)}, u32[]{:S(2)}) collective-permute-start(f32[64,128]{1,0:T(8,128)S(1)} %shard_map.77.mine), channel_id=1, source_target_pairs={{0,1},{1,0},{2,3},{3,2},{4,5},{5,4},{6,7},{7,6},{8,9},{9,8},{10,11... | collective-permute-start | bytes 98312 | tf_op jit(solution)/shard_map/ppermute | solution.py:381
